TPU v7x, 512 devices: a whole 4x8x8 slice. The times are simulated.
512 devices in a mesh: rad: 64 (over z, y), col: 8 (over x, core).
Axes of the slice: x: 4, y: 8, z: 8, core: 2. Of those that a mesh axis runs over, the one named last changes fastest.
Arguments:
- right_sides: bfloat16 [256, 384, 1024], P('rad', None, 'col'), may hold values from -6 to 6
- coarse_solution: bfloat16 [64, 384, 1024], P('rad', None, 'col'), may hold values from -6 to 6
- lift_one: bfloat16 [128, 2, 1024, 1024], P('rad', None, 'col'), may hold values from -0.125 to 0.125
- solve_one: bfloat16 [128, 3, 1024, 1024], P('rad', None, 'col'), may hold values from -0.109375 to 0.109375
- lift_two: bfloat16 [64, 2, 1024, 1024], P('rad', None, 'col'), may hold values from -0.125 to 0.125
- solve_two: bfloat16 [64, 3, 1024, 1024], P('rad', None, 'col'), may hold values from -0.109375 to 0.109375
Outputs:
- solution: bfloat16 [256, 384, 1024], P('rad', None, 'col')
- reduced_sides: bfloat16 [64, 384, 1024], P('rad', None, 'col')
All inputs are finite; a program needn't handle non-finite values.
Results may differ from a plain program's by a relative error of at most 0.007.
Values may be sent and summed in bfloat16 or wider, within the bound.
No kernel may reach another device: no remote copies, remote signals or barrier semaphores. Data moves between devices by JAX's collectives and lax.ppermute only.
A program may use at most 64 MiB of HBM per device.

v0:
```python
import jax
import jax.numpy as jnp
from jax import lax
from jax.sharding import PartitionSpec as P


def padded(array, sides, width):
    for axis, dim in sides:
        peers, length = (lax.axis_size(axis), array.shape[dim])
        up = [(i, (i + 1) % peers) for i in range(peers - 1)]
        down = [(j, i) for i, j in up]
        last = lax.slice_in_dim(array, length - width, length, axis=dim)
        initial = lax.slice_in_dim(array, 0, width, axis=dim)
        before = lax.ppermute(last, axis, up)
        after = lax.ppermute(initial, axis, down)
        array = jnp.concatenate([before, array, after], axis=dim)
    return array


def passed_along(array, axis, by):
    peers = lax.axis_size(axis)
    pairs = [(i, i + by) for i in range(peers) if 0 <= i + by < peers]
    return lax.ppermute(array, axis, pairs)


def apply(vector, matrix):
    return lax.dot_general(
        vector, matrix, (((1,), (1,)), ((), ())), preferred_element_type=jnp.float32
    )


def local(right_sides, coarse_solution, lift_one, solve_one, lift_two, solve_two):
    coarse_here = coarse_solution[0]
    edge_blocks = jnp.stack([coarse_here, right_sides[1], right_sides[3]])
    gathered = lax.all_gather(edge_blocks, "col", axis=2, tiled=True)
    haloed = padded(gathered, (("rad", 0),), 1)
    before_odd = haloed[0]
    coarse_full = haloed[1]
    second_full = haloed[2]
    fourth_full = haloed[3]
    coarse_next = haloed[4]
    kept = (
        right_sides[0].astype(jnp.float32)
        - apply(before_odd, lift_one[0, 0])
        - apply(second_full, lift_one[0, 1])
    )
    kept = kept.astype(jnp.bfloat16)
    middle = (
        right_sides[2].astype(jnp.float32)
        - apply(second_full, lift_one[1, 0])
        - apply(fourth_full, lift_one[1, 1])
    )
    middle = middle.astype(jnp.bfloat16)
    middle_full = lax.all_gather(middle, "col", axis=1, tiled=True)
    middle_before = passed_along(middle_full, "rad", 1)
    reduced = (
        kept.astype(jnp.float32)
        - apply(middle_before, lift_two[0, 0])
        - apply(middle_full, lift_two[0, 1])
    )
    centre = (
        apply(middle_full, solve_two[0, 0])
        - apply(coarse_full, solve_two[0, 1])
        - apply(coarse_next, solve_two[0, 2])
    )
    centre = centre.astype(jnp.bfloat16)
    centre_full = lax.all_gather(centre, "col", axis=1, tiled=True)
    second = (
        apply(second_full, solve_one[0, 0])
        - apply(coarse_full, solve_one[0, 1])
        - apply(centre_full, solve_one[0, 2])
    )
    fourth = (
        apply(fourth_full, solve_one[1, 0])
        - apply(centre_full, solve_one[1, 1])
        - apply(coarse_next, solve_one[1, 2])
    )
    solved = jnp.stack(
        [coarse_here, second.astype(jnp.bfloat16), centre, fourth.astype(jnp.bfloat16)]
    )
    return (solved, reduced.astype(jnp.bfloat16)[None])


def solution(mesh):
    return jax.shard_map(
        local,
        mesh=mesh,
        in_specs=(
            P("rad", None, "col"),
            P("rad", None, "col"),
            P("rad", None, "col", None),
            P("rad", None, "col", None),
            P("rad", None, "col", None),
            P("rad", None, "col", None),
        ),
        out_specs=(P("rad", None, "col"), P("rad", None, "col")),
        check_vma=False,
    )
```

profile of v0, /device:TPU:249, one launch (start us, length us, event | category | flops | bytes accessed | tf_op | source)
XLA Modules:
  0.0 121.4 jit_solution(3570309489867178483)
XLA Ops:
  7.2 0.0 copy-start.5
  7.2 0.0 all-gather.2.cloned.1.call-start
  7.2 1.0 fusion.59
  8.3 0.0 copy-start.1
  8.3 1.7 %pad_maximum_fusion.1 = bf16[3,384,128]{2,1,0:T(8,128)(2,1)} fusion(bf16[1,384,128]{2,1,0:T(8,128)(2,1)S(1)} %get-tuple-element.5, bf16[1,384,128]{2,1,0:T(8,128)(2,1)S(1)} %get-tuple-element.4, bf16[1,384,128]{2,1,0:T(8,128)(2,1)} %param.7), kind=kLoop, calls=%fused_computation.34 | loop fusion | flops 294912 | bytes 589824 | tf_op jit(solution)/shard_map/stack | solution.py:34
  10.0 0.0 all-gather.2.cloned.1.call-update
  10.0 0.0 copy-start.4
  10.0 36.1 %all-gather.2.cloned.1.call-done = bf16[3,384,1024]{2,1,0:T(8,128)(2,1)} async-done(((bf16[3,384,128]{2,1,0:T(8,128)(2,1)}), bf16[3,384,1024]{2,1,0:T(8,128)(2,1)}) %all-gather.2.cloned.1.call-update) | async-done | bytes 2359312 | tf_op jit(solution)/shard_map/all_gather | solution.py:35
  46.1 1.6 %convolution_subtract_fusion.8 = f32[384,128]{1,0:T(8,128)S(1)} fusion(bf16[3,384,1024]{2,1,0:T(8,128)(2,1)} %all-gather.2.cloned.1.call-done, bf16[2,2,128,1024]{3,2,1,0:T(8,128)(2,1)} %param.8, bf16[4,384,128]{2,1,0:T(8,128)(2,1)} %param.6), kind=kOutput, calls=%fused_computation.8 | convolution fusion | flops 100761600 | bytes 1343488 | tf_op jit(solution)/shard_map/dot_general | solution.py:27
  47.7 0.0 copy-done.5
  47.7 0.0 copy-start
  47.7 1.7 %fusion.2 = bf16[384,128]{1,0:T(8,128)(2,1)S(1)} fusion(f32[384,128]{1,0:T(8,128)S(1)} %convolution_subtract_fusion.8, bf16[2,2,128,1024]{3,2,1,0:T(8,128)(2,1)S(1)} %copy-done.5, bf16[3,384,1024]{2,1,0:T(8,128)(2,1)} %all-gather.2.cloned.1.call-done), kind=kOutput, calls=%fused_computation.12 | convolution fusion | flops 100761600 | bytes 1343488 | tf_op jit(solution)/shard_map/dot_general | solution.py:27
  49.4 14.0 %all_gather.10 = bf16[384,1024]{1,0:T(8,128)(2,1)S(1)} all-gather(bf16[384,128]{1,0:T(8,128)(2,1)S(1)} %fusion.2), channel_id=1, replica_groups=mesh['rad'=64,'col'=8] {'col'}, dimensions={1}, use_global_device_ids=true | all-gather | bytes 884736 | tf_op jit(solution)/shard_map/all_gather | solution.py:54
  63.3 4.3 %collective-permute-start.2 = (bf16[384,1024]{1,0:T(8,128)(2,1)S(1)}, bf16[384,1024]{1,0:T(8,128)(2,1)S(1)}, u32[]{:S(2)}, u32[]{:S(2)}) collective-permute-start(bf16[384,1024]{1,0:T(8,128)(2,1)S(1)} %all_gather.10), channel_id=1, source_target_pairs={{0,8},{8,16},{16,24},{24,32},{32,40},{40,48},{48,56},{56,64},{64,7... | collective-permute-start | bytes 2359304 | tf_op jit(solution)/shard_map/ppermute | solution.py:23
  67.7 0.0 copy-done.1
  67.7 0.4 fusion.22
  68.0 0.0 copy-done.4
  68.0 0.4 fusion.33
  68.4 0.0 copy-done
  68.4 0.0 copy-start.3
  68.4 0.1 fusion.58
  68.6 3.2 %collective-permute-start.1 = (bf16[1,384,1024]{2,1,0:T(8,128)(2,1)S(1)}, bf16[1,384,1024]{2,1,0:T(8,128)(2,1)S(1)}, u32[]{:S(2)}, u32[]{:S(2)}) collective-permute-start(bf16[1,384,1024]{2,1,0:T(8,128)(2,1)S(1)} %get-tuple-element.2), channel_id=1, source_target_pairs={{0,8},{8,16},{16,24},{24,32},{32,40},{40,48},{48,56},{56,64},{64,7... | collective-permute-start | bytes 2359304 | tf_op jit(solution)/shard_map/ppermute | solution.py:14
  71.8 2.2 %collective-permute-start = (bf16[1,384,1024]{2,1,0:T(8,128)(2,1)S(1)}, bf16[1,384,1024]{2,1,0:T(8,128)(2,1)S(1)}, u32[]{:S(2)}, u32[]{:S(2)}) collective-permute-start(bf16[1,384,1024]{2,1,0:T(8,128)(2,1)S(1)} %get-tuple-element.3), channel_id=1, source_target_pairs={{8,0},{16,8},{24,16},{32,24},{40,32},{48,40},{56,48},{64,56},{72,6... | collective-permute-start | bytes 2359304 | tf_op jit(solution)/shard_map/ppermute | solution.py:15
  74.0 0.4 fusion.20
  74.4 0.0 copy-done.3
  74.4 0.4 fusion.15
  74.8 0.4 fusion.21
  75.1 0.4 convolution_subtract_fusion.9
  75.5 0.4 convolution_subtract_fusion.6
  75.9 19.5 %collective-permute-done = bf16[1,384,1024]{2,1,0:T(8,128)(2,1)S(1)} collective-permute-done((bf16[1,384,1024]{2,1,0:T(8,128)(2,1)S(1)}, bf16[1,384,1024]{2,1,0:T(8,128)(2,1)S(1)}, u32[]{:S(2)}, u32[]{:S(2)}) %collective-permute-start) | collective-permute-done | bytes 786464 | tf_op jit(solution)/shard_map/ppermute | solution.py:15
  95.4 0.4 fusion.3
  95.8 0.0 copy-start.2
  95.8 14.5 %all_gather.11 = bf16[384,1024]{1,0:T(8,128)(2,1)S(1)} all-gather(bf16[384,128]{1,0:T(8,128)(2,1)S(1)} %fusion.3), channel_id=1, replica_groups=mesh['rad'=64,'col'=8] {'col'}, dimensions={1}, use_global_device_ids=true | all-gather | bytes 884736 | tf_op jit(solution)/shard_map/all_gather | solution.py:67
  110.3 0.4 fusion.11
  110.7 0.4 convolution_subtract_fusion.3
  111.1 0.4 fusion.10
  111.5 0.0 copy-done.2
  111.5 0.8 pad_maximum_fusion
  112.3 0.0 collective-permute-done.1
  112.3 1.3 %fusion.8 = f32[384,128]{1,0:T(8,128)S(1)} fusion(f32[384,128]{1,0:T(8,128)S(1)} %fusion.20, bf16[1,384,1024]{2,1,0:T(8,128)(2,1)S(1)} %collective-permute-done.1, bf16[2,2,128,1024]{3,2,1,0:T(8,128)(2,1)S(1)} %copy-done.5, bf16[4,384,128]{2,1,0:T(8,128)(2,1)} %param.6), kind=kOutput, calls=%fused_computation.18 | convolution fusion | flops 100909056 | bytes 1540096 | tf_op jit(solution)/shard_map/dot_general | solution.py:27
  113.5 0.0 collective-permute-done.2
  113.6 1.0 fusion.9
Async XLA Ops:
  7.2 40.5 %copy-start.5 = (bf16[2,2,128,1024]{3,2,1,0:T(8,128)(2,1)S(1)}, bf16[2,2,128,1024]{3,2,1,0:T(8,128)(2,1)}, u32[]{:S(2)}) copy-start(bf16[2,2,128,1024]{3,2,1,0:T(8,128)(2,1)} %param.8) | copy-start | bytes 3145732
  7.2 38.9 %all-gather.2.cloned.1.call-start = ((), (), s32[]{:S(2)}) async-start(), calls=%async_computation | async-start | bytes 2654208 | tf_op jit(solution)/shard_map/all_gather | solution.py:35
  8.3 59.4 %copy-start.1 = (bf16[1,2,128,1024]{3,2,1,0:T(8,128)(2,1)S(1)}, bf16[1,2,128,1024]{3,2,1,0:T(8,128)(2,1)}, u32[]{:S(2)}) copy-start(bf16[1,2,128,1024]{3,2,1,0:T(8,128)(2,1)} %param.10) | copy-start | bytes 1572868
  10.0 58.0 %copy-start.4 = (bf16[1,3,128,1024]{3,2,1,0:T(8,128)(2,1)S(1)}, bf16[1,3,128,1024]{3,2,1,0:T(8,128)(2,1)}, u32[]{:S(2)}) copy-start(bf16[1,3,128,1024]{3,2,1,0:T(8,128)(2,1)} %param.11) | copy-start | bytes 2359300
  47.7 20.7 %copy-start = (bf16[3,384,1024]{2,1,0:T(8,128)(2,1)S(1)}, bf16[3,384,1024]{2,1,0:T(8,128)(2,1)}, u32[]{:S(2)}) copy-start(bf16[3,384,1024]{2,1,0:T(8,128)(2,1)} %all-gather.2.cloned.1.call-done) | copy-start | bytes 7077892
  63.3 50.2 %collective-permute-start.2 = (bf16[384,1024]{1,0:T(8,128)(2,1)S(1)}, bf16[384,1024]{1,0:T(8,128)(2,1)S(1)}, u32[]{:S(2)}, u32[]{:S(2)}) collective-permute-start(bf16[384,1024]{1,0:T(8,128)(2,1)S(1)} %all_gather.10), channel_id=1, source_target_pairs={{0,8},{8,16},{16,24},{24,32},{32,40},{40,48},{48,56},{56,64},{64,7... | collective-permute-start | bytes 2359304 | tf_op jit(solution)/shard_map/ppermute | solution.py:23
  68.4 6.0 %copy-start.3 = (bf16[2,3,128,1024]{3,2,1,0:T(8,128)(2,1)S(1)}, bf16[2,3,128,1024]{3,2,1,0:T(8,128)(2,1)}, u32[]{:S(2)}) copy-start(bf16[2,3,128,1024]{3,2,1,0:T(8,128)(2,1)} %param.9) | copy-start | bytes 4718596
  68.6 43.7 %collective-permute-start.1 = (bf16[1,384,1024]{2,1,0:T(8,128)(2,1)S(1)}, bf16[1,384,1024]{2,1,0:T(8,128)(2,1)S(1)}, u32[]{:S(2)}, u32[]{:S(2)}) collective-permute-start(bf16[1,384,1024]{2,1,0:T(8,128)(2,1)S(1)} %get-tuple-element.2), channel_id=1, source_target_pairs={{0,8},{8,16},{16,24},{24,32},{32,40},{40,48},{48,56},{56,64},{64,7... | collective-permute-start | bytes 2359304 | tf_op jit(solution)/shard_map/ppermute | solution.py:14
  71.8 23.6 %collective-permute-start = (bf16[1,384,1024]{2,1,0:T(8,128)(2,1)S(1)}, bf16[1,384,1024]{2,1,0:T(8,128)(2,1)S(1)}, u32[]{:S(2)}, u32[]{:S(2)}) collective-permute-start(bf16[1,384,1024]{2,1,0:T(8,128)(2,1)S(1)} %get-tuple-element.3), channel_id=1, source_target_pairs={{8,0},{16,8},{24,16},{32,24},{40,32},{48,40},{56,48},{64,56},{72,6... | collective-permute-start | bytes 2359304 | tf_op jit(solution)/shard_map/ppermute | solution.py:15
  95.8 15.7 %copy-start.2 = (bf16[1,384,128]{2,1,0:T(8,128)(2,1)S(1)}, bf16[1,384,128]{2,1,0:T(8,128)(2,1)}, u32[]{:S(2)}) copy-start(bf16[1,384,128]{2,1,0:T(8,128)(2,1)} %param.7) | copy-start | bytes 294916
Sparse Core Ops, SparseCore 0:
  10.7 35.3 all-gather.1
where the time goes:
time: 122 us; the launch traced here: 121 us
  waiting for transfers between devices  55.6 us (46%)
  blocking collectives  28.5 us (23%)
  between operations  14.3 us (12%)
  starting transfers between devices  9.76 us (8%)
  matrix products  9.63 us (8%)
  other arithmetic  2.5 us (2%)
    all_gather x1, waiting for transfers between devices, local(): gathered = lax.all_gather(edge_blocks, 'col', axis=2, tiled=True)  36.1 us
    ppermute x1, waiting for transfers between devices, padded(): after = lax.ppermute(initial, axis, down)  19.5 us
    all_gather x1, blocking collectives, local(): centre_full = lax.all_gather(centre, 'col', axis=1, tiled=True)  14.5 us
    all_gather x1, blocking collectives, local(): middle_full = lax.all_gather(middle, 'col', axis=1, tiled=True)  14 us
    dot_general x15, matrix products, apply(): lax.dot_general(vector, matrix, (((1,), (1,)), ((), ())), preferred_eleme...  9.63 us
    ppermute x1, starting transfers between devices, passed_along(): return lax.ppermute(array, axis, pairs)  4.31 us
    ppermute x1, starting transfers between devices, padded(): before = lax.ppermute(last, axis, up)  3.25 us
  transfers between devices with their start and end apart: 4, of which 2 were waited for; matrix products, arithmetic and copies ran while one was open for 5% of the time, Pallas kernels for 0%

commit v1 on v0

v1 whole, which is shorter than its diff:
```python
import functools

import jax
import jax.numpy as jnp
from jax import lax
from jax.experimental import pallas as pl
from jax.experimental.pallas import tpu as pltpu
from jax.sharding import PartitionSpec as P

ROWS = 384
WIDTH = 128
BF16 = jnp.bfloat16
F32 = jnp.float32


def chips_of(peers):
    return [[i for i in range(peers) if i % 2 == core] for core in range(2)]


def cores_of(peers):
    return [[i, i + 1] for i in range(0, peers, 2)]


def over_chips(array):
    peers = lax.axis_size("col")
    chips = peers // 2
    copies = jnp.broadcast_to(array[None], (chips, *array.shape))
    return lax.all_to_all(copies, "col", 0, 0, axis_index_groups=chips_of(peers))


def over_cores(array):
    peers = lax.axis_size("col")
    return lax.all_gather(array, "col", axis=0, axis_index_groups=cores_of(peers))


def passed_along(array, by):
    peers = lax.axis_size("rad")
    pairs = [(i, i + by) for i in range(peers) if 0 <= i + by < peers]
    return lax.ppermute(array, "rad", pairs)


def wide(blocks):
    return jnp.concatenate(
        [blocks[core, chip] for chip in range(4) for core in range(2)], axis=1
    )


def apply(vector, matrix):
    return lax.dot_general(
        vector, matrix, (((1,), (1,)), ((), ())), preferred_element_type=F32
    )


def call(body, outs, *args, products=1):
    spec = pl.BlockSpec(memory_space=pltpu.VMEM)
    return pl.pallas_call(
        body,
        out_shape=[jax.ShapeDtypeStruct(shape, dtype) for shape, dtype in outs],
        in_specs=[spec] * len(args),
        out_specs=[spec] * len(outs),
        cost_estimate=pl.CostEstimate(
            flops=products * 2 * ROWS * 1024 * WIDTH,
            bytes_accessed=products * 1000000,
            transcendentals=0,
        ),
    )(*args)


BLOCK = ((ROWS, WIDTH), BF16)
TOTAL = ((ROWS, WIDTH), F32)


def middle_body(second, fourth, side, lift, middle):
    total = side[...].astype(F32) - apply(wide(second), lift[1, 0])
    middle[...] = (total - apply(wide(fourth), lift[1, 1])).astype(BF16)


def coarse_body(here, following, solve, total):
    total[...] = apply(wide(here), solve[0, 1]) + apply(wide(following), solve[0, 2])


def centre_body(middle, solve, coarse, centre):
    centre[...] = (apply(wide(middle), solve[0, 0]) - coarse[...]).astype(BF16)


def onward_body(fourth, middle, lifts, total):
    both = apply(wide(fourth), lifts[0]) + apply(wide(middle), lifts[1])
    total[...] = both.astype(BF16)


def reduced_body(second, middle, side, lift_one, lift_two, total):
    both = apply(wide(second), lift_one[0, 1]) + apply(wide(middle), lift_two[0, 1])
    total[...] = side[...].astype(F32) - both


def odd_body(second, fourth, here, following, solve, two, four):
    two[...] = apply(wide(second), solve[0, 0]) - apply(wide(here), solve[0, 1])
    four[...] = apply(wide(fourth), solve[1, 0]) - apply(wide(following), solve[1, 2])


def final_body(whole, solve, two, four, coarse, centre, total, before, solved, reduced):
    full = wide(whole)
    solved[0] = coarse[...]
    solved[1] = (two[...] - apply(full, solve[0, 2])).astype(BF16)
    solved[2] = centre[...]
    solved[3] = (four[...] - apply(full, solve[1, 1])).astype(BF16)
    reduced[0] = (total[...] - before[...].astype(F32)).astype(BF16)


def local(right_sides, coarse_solution, lift_one, solve_one, lift_two, solve_two):
    coarse_here = coarse_solution[0]
    coarse_next = passed_along(coarse_here, -1)
    lifts_next = passed_along(jnp.stack([lift_one[0, 0], lift_two[0, 0]]), -1)

    odd = over_chips(jnp.stack([right_sides[1], right_sides[3]]))
    second = over_cores(odd[:, 0])
    fourth = over_cores(odd[:, 1])
    coarse = over_chips(jnp.stack([coarse_here, coarse_next]))

    (middle,) = call(
        middle_body, [BLOCK], second, fourth, right_sides[2], lift_one, products=2
    )
    middle_part = over_chips(middle)
    here = over_cores(coarse[:, 0])
    following = over_cores(coarse[:, 1])
    (coarse_total,) = call(
        coarse_body, [TOTAL], here, following, solve_two, products=2
    )
    two, four = call(
        odd_body, [TOTAL, TOTAL], second, fourth, here, following, solve_one, products=4
    )
    middle_full = over_cores(middle_part)

    (centre,) = call(centre_body, [BLOCK], middle_full, solve_two, coarse_total)
    centre_part = over_chips(centre)
    (onward,) = call(
        onward_body, [BLOCK], fourth, middle_full, lifts_next, products=2
    )
    before = passed_along(onward, 1)
    (total,) = call(
        reduced_body,
        [TOTAL],
        second,
        middle_full,
        right_sides[0],
        lift_one,
        lift_two,
        products=2,
    )
    centre_full = over_cores(centre_part)
    solved, reduced = call(
        final_body,
        [((4, ROWS, WIDTH), BF16), ((1, ROWS, WIDTH), BF16)],
        centre_full,
        solve_one,
        two,
        four,
        coarse_here,
        centre,
        total,
        before,
        products=2,
    )
    return solved, reduced


def solution(mesh):
    return jax.shard_map(
        local,
        mesh=mesh,
        in_specs=(
            P("rad", None, "col"),
            P("rad", None, "col"),
            P("rad", None, "col", None),
            P("rad", None, "col", None),
            P("rad", None, "col", None),
            P("rad", None, "col", None),
        ),
        out_specs=(P("rad", None, "col"), P("rad", None, "col")),
        check_vma=False,
    )
```

time: 122 us -> 87.5 us (0.72)
  the two profiles are of different devices: /device:TPU:249 before, /device:TPU:251 now
where the time goes in v1:
time: 87.5 us; the launch traced here: 86.8 us
  starting transfers between devices  29.1 us (33%)
  Pallas kernels  21.2 us (24%)
  blocking collectives  20.1 us (23%)
  local copies, waits for them, and re-layouts  9.63 us (11%)
  waiting for transfers between devices  5.89 us (7%)
    pallas_call x7, Pallas kernels, call(): pl.pallas_call(body, out_shape=[jax.ShapeDtypeStruct(shape, dtype) for sh...  21.2 us
    all_gather x6, blocking collectives, over_cores(): lax.all_gather(array, 'col', axis=0, axis_index_groups=cores_of(peers))  20.1 us
    all_to_all x4, starting transfers between devices, over_chips(): lax.all_to_all(copies, 'col', 0, 0, axis_index_groups=chips_of(peers))  17.5 us
    ppermute x3, starting transfers between devices, passed_along(): return lax.ppermute(array, 'rad', pairs)  11.6 us
    all_to_all x4, waiting for transfers between devices, over_chips(): lax.all_to_all(copies, 'col', 0, 0, axis_index_groups=chips_of(peers))  5.88 us
    broadcast_in_dim x4, local copies, waits for them, and re-layouts, over_chips(): copies = jnp.broadcast_to(array[None], (chips, *array.shape))  5.36 us
  transfers between devices with their start and end apart: 7, of which 1 were waited for; matrix products, arithmetic and copies ran while one was open for 10% of the time, Pallas kernels for 21%

profile of v1, /device:TPU:251, one launch (start us, length us, event | category | flops | bytes accessed | tf_op | source)
XLA Modules:
  0.0 86.8 jit_solution(12094020741639259838)
XLA Ops:
  0.6 3.0 %collective-permute-start = (bf16[384,128]{1,0:T(8,128)(2,1)}, bf16[384,128]{1,0:T(8,128)(2,1)S(1)}, u32[]{:S(2)}, u32[]{:S(2)}) collective-permute-start(bf16[384,128]{1,0:T(8,128)(2,1)} %bitcast.30), channel_id=1, source_target_pairs={{8,0},{16,8},{24,16},{32,24},{40,32},{48,40},{56,48},{64,56},{72,6... | collective-permute-start | bytes 294920 | tf_op jit(solution)/shard_map/ppermute | solution.py:39
  3.6 1.7 %slice_bitcast_fusion.2 = (bf16[384,128]{1,0:T(8,128)(2,1)}, bf16[1,384,128]{2,1,0:T(8,128)(2,1)S(1)}, bf16[1,384,128]{2,1,0:T(8,128)(2,1)S(1)}, bf16[384,128]{1,0:T(8,128)(2,1)}) fusion(bf16[4,384,128]{2,1,0:T(8,128)(2,1)} %param.6), kind=kLoop, calls=%fused_computation.5 | loop fusion | bytes 786432 | tf_op jit(solution)/shard_map/squeeze | solution.py:145
  5.4 0.0 copy-start
  5.4 1.0 %broadcast_in_dim.8 = bf16[4,2,384,128]{3,2,1,0:T(8,128)(2,1)} broadcast(bf16[2,384,128]{2,1,0:T(8,128)(2,1)S(1)} %pad_maximum_fusion.1), dimensions={1,2,3} | broadcast | bytes 983040 | tf_op jit(solution)/shard_map/broadcast_in_dim | solution.py:27
  6.4 0.0 copy-start.2
  6.4 4.4 %all-to-all-start = ((bf16[4,2,384,128]{3,2,1,0:T(8,128)(2,1)}), bf16[4,2,384,128]{3,2,1,0:T(8,128)(2,1)S(1)}, u32[]{:S(2)}, u32[]{:S(2)}) async-start(bf16[4,2,384,128]{3,2,1,0:T(8,128)(2,1)} %broadcast_in_dim.8), calls=%async_computation | async-start | bytes 1572864 | tf_op jit(solution)/shard_map/all_to_all | solution.py:28
  10.8 0.0 copy-done
  10.8 1.0 %slice_bitcast_fusion.1 = bf16[1,128,1024]{2,1,0:T(8,128)(2,1)S(1)} fusion(bf16[2,2,128,1024]{3,2,1,0:T(8,128)(2,1)} %lift_one.1), kind=kLoop, calls=%fused_computation.2 | loop fusion | bytes 524288 | tf_op jit(solution)/shard_map/stack;squeeze | solution.py:113
  11.8 0.1 pad_maximum_fusion
  11.8 3.0 %collective-permute-start.1 = (bf16[2,128,1024]{2,1,0:T(8,128)(2,1)S(1)}, bf16[2,128,1024]{2,1,0:T(8,128)(2,1)S(1)}, u32[]{:S(2)}, u32[]{:S(2)}) collective-permute-start(bf16[2,128,1024]{2,1,0:T(8,128)(2,1)S(1)} %pad_maximum_fusion), channel_id=1, source_target_pairs={{8,0},{16,8},{24,16},{32,24},{40,32},{48,40},{56,48},{64,56},{72,6... | collective-permute-start | bytes 1572872 | tf_op jit(solution)/shard_map/ppermute | solution.py:39
  14.8 0.0 collective-permute-done
  14.8 0.0 copy-done.2
  14.9 5.9 %all-to-all-done = bf16[4,2,384,128]{3,2,1,0:T(8,128)(2,1)S(1)} async-done(((bf16[4,2,384,128]{3,2,1,0:T(8,128)(2,1)}), bf16[4,2,384,128]{3,2,1,0:T(8,128)(2,1)S(1)}, u32[]{:S(2)}, u32[]{:S(2)}) %all-to-all-start) | async-done | bytes 786464 | tf_op jit(solution)/shard_map/all_to_all | solution.py:28
  20.7 1.0 %broadcast_in_dim.10 = bf16[4,2,384,128]{3,2,1,0:T(8,128)(2,1)} broadcast(bf16[2,384,128]{2,1,0:T(8,128)(2,1)S(1)} %pad_maximum_fusion.2), dimensions={1,2,3} | broadcast | bytes 983040 | tf_op jit(solution)/shard_map/broadcast_in_dim | solution.py:27
  21.7 4.6 %all-to-all-start.2 = ((bf16[4,2,384,128]{3,2,1,0:T(8,128)(2,1)}), bf16[4,2,384,128]{3,2,1,0:T(8,128)(2,1)S(1)}, u32[]{:S(2)}, u32[]{:S(2)}) async-start(bf16[4,2,384,128]{3,2,1,0:T(8,128)(2,1)} %broadcast_in_dim.10), calls=%async_computation.2 | async-start | bytes 1572864 | tf_op jit(solution)/shard_map/all_to_all | solution.py:28
  26.4 0.1 fusion.1
  26.4 4.5 %all-gather.1 = bf16[8,1,384,128]{3,2,1,0:T(8,128)(2,1)} all-gather(bf16[4,1,384,128]{3,2,1,0:T(8,128)(2,1)S(1)} %get-tuple-element.8), channel_id=3, replica_groups={{0,1},{2,3},{4,5},{6,7},{8,9},{10,11},{12,13},{14,15},{16,17},{18,19},{..., dimensions={0}, use_global_device_ids=true | all-gather | bytes 1179648 | tf_op jit(solution)/shard_map/all_gather | solution.py:33
  30.9 2.5 %all-gather = bf16[8,1,384,128]{3,2,1,0:T(8,128)(2,1)} all-gather(bf16[4,1,384,128]{3,2,1,0:T(8,128)(2,1)S(1)} %get-tuple-element.9), channel_id=2, replica_groups={{0,1},{2,3},{4,5},{6,7},{8,9},{10,11},{12,13},{14,15},{16,17},{18,19},{..., dimensions={0}, use_global_device_ids=true | all-gather | bytes 1179648 | tf_op jit(solution)/shard_map/all_gather | solution.py:33
  33.4 2.9 %shard_map.77 = bf16[384,128]{1,0:T(8,128)(2,1)} custom-call(bf16[2,4,384,128]{3,2,1,0:T(8,128)(2,1)} %bitcast.16, bf16[2,4,384,128]{3,2,1,0:T(8,128)(2,1)} %bitcast.19, bf16[384,128]{1,0:T(8,128)(2,1)} %get-tuple-element.13.side, bf16[2,2,128,1024]{3,2,1,0:T(8,128)(2,1)} %lift_one.1), custom_call_target="tpu_custom_call" | custom-call | flops 201326592 | bytes 2000000 | tf_op jit(solution)/shard_map/pallas_call | solution.py:56
  36.4 0.0 all-to-all-done.2
  36.4 1.7 %broadcast_in_dim.9 = bf16[4,384,128]{2,1,0:T(8,128)(2,1)} broadcast(bf16[384,128]{1,0:T(8,128)(2,1)} %shard_map.77), dimensions={1,2} | broadcast | bytes 491520 | tf_op jit(solution)/shard_map/broadcast_in_dim | solution.py:27
  38.1 4.2 %all-to-all-start.1 = ((bf16[4,384,128]{2,1,0:T(8,128)(2,1)}), bf16[4,384,128]{2,1,0:T(8,128)(2,1)S(1)}, u32[]{:S(2)}, u32[]{:S(2)}) async-start(bf16[4,384,128]{2,1,0:T(8,128)(2,1)} %broadcast_in_dim.9), calls=%async_computation.1 | async-start | bytes 786432 | tf_op jit(solution)/shard_map/all_to_all | solution.py:28
  42.3 0.1 fusion
  42.3 4.8 %all-gather.4 = bf16[8,1,384,128]{3,2,1,0:T(8,128)(2,1)} all-gather(bf16[4,1,384,128]{3,2,1,0:T(8,128)(2,1)S(1)} %get-tuple-element.6), channel_id=6, replica_groups={{0,1},{2,3},{4,5},{6,7},{8,9},{10,11},{12,13},{14,15},{16,17},{18,19},{..., dimensions={0}, use_global_device_ids=true | all-gather | bytes 1179648 | tf_op jit(solution)/shard_map/all_gather | solution.py:33
  47.2 2.5 %all-gather.3 = bf16[8,1,384,128]{3,2,1,0:T(8,128)(2,1)} all-gather(bf16[4,1,384,128]{3,2,1,0:T(8,128)(2,1)S(1)} %get-tuple-element.7), channel_id=5, replica_groups={{0,1},{2,3},{4,5},{6,7},{8,9},{10,11},{12,13},{14,15},{16,17},{18,19},{..., dimensions={0}, use_global_device_ids=true | all-gather | bytes 1179648 | tf_op jit(solution)/shard_map/all_gather | solution.py:33
  49.7 2.8 %shard_map.78.coarse = f32[384,128]{1,0:T(8,128)} custom-call(bf16[2,4,384,128]{3,2,1,0:T(8,128)(2,1)} %bitcast.27, bf16[2,4,384,128]{3,2,1,0:T(8,128)(2,1)} %bitcast.25, bf16[1,3,128,1024]{3,2,1,0:T(8,128)(2,1)} %solve.5), custom_call_target="tpu_custom_call" | custom-call | flops 201326592 | bytes 2000000 | tf_op jit(solution)/shard_map/pallas_call | solution.py:56
  52.5 0.0 all-to-all-done.1
  52.5 2.5 %all-gather.2 = bf16[8,384,128]{2,1,0:T(8,128)(2,1)} all-gather(bf16[4,384,128]{2,1,0:T(8,128)(2,1)S(1)} %all-to-all-done.1), channel_id=4, replica_groups={{0,1},{2,3},{4,5},{6,7},{8,9},{10,11},{12,13},{14,15},{16,17},{18,19},{..., dimensions={0}, use_global_device_ids=true | all-gather | bytes 1179648 | tf_op jit(solution)/shard_map/all_gather | solution.py:33
  55.0 2.4 %shard_map.79.centre = bf16[384,128]{1,0:T(8,128)(2,1)} custom-call(bf16[2,4,384,128]{3,2,1,0:T(8,128)(2,1)} %bitcast.22, bf16[1,3,128,1024]{3,2,1,0:T(8,128)(2,1)} %solve.5, f32[384,128]{1,0:T(8,128)} %shard_map.78.coarse), custom_call_target="tpu_custom_call" | custom-call | flops 100663296 | bytes 1000000 | tf_op jit(solution)/shard_map/pallas_call | solution.py:56
  57.4 1.7 %broadcast_in_dim.11 = bf16[4,384,128]{2,1,0:T(8,128)(2,1)} broadcast(bf16[384,128]{1,0:T(8,128)(2,1)} %shard_map.79.centre), dimensions={1,2} | broadcast | bytes 491520 | tf_op jit(solution)/shard_map/broadcast_in_dim | solution.py:27
  59.1 4.2 %all-to-all-start.3 = ((bf16[4,384,128]{2,1,0:T(8,128)(2,1)}), bf16[4,384,128]{2,1,0:T(8,128)(2,1)S(1)}, u32[]{:S(2)}, u32[]{:S(2)}) async-start(bf16[4,384,128]{2,1,0:T(8,128)(2,1)} %broadcast_in_dim.11), calls=%async_computation.3 | async-start | bytes 786432 | tf_op jit(solution)/shard_map/all_to_all | solution.py:28
  63.4 4.0 %shard_map.80 = (f32[384,128]{1,0:T(8,128)}, f32[384,128]{1,0:T(8,128)}) custom-call(bf16[2,4,384,128]{3,2,1,0:T(8,128)(2,1)} %bitcast.17, bf16[2,4,384,128]{3,2,1,0:T(8,128)(2,1)} %bitcast.20, bf16[2,4,384,128]{3,2,1,0:T(8,128)(2,1)} %bitcast.28, bf16[2,4,384,128]{3,2,1,0:T(8,128)(2,1)} %bitcast.26, bf16[2,3,128,1024]{3,2,1,0:T(8,128)(2,1)} %solve.7), custom_call_target="tpu_custom_call" | custom-call | flops 402653184 | bytes 4000000 | tf_op jit(solution)/shard_map/pallas_call | solution.py:56
  67.4 0.0 collective-permute-done.1.lifts
  67.4 0.0 copy-start.1
  67.4 0.8 copy-done.1
  68.2 2.7 %shard_map.82 = bf16[384,128]{1,0:T(8,128)(2,1)} custom-call(bf16[2,4,384,128]{3,2,1,0:T(8,128)(2,1)} %bitcast.21, bf16[2,4,384,128]{3,2,1,0:T(8,128)(2,1)} %bitcast.23, bf16[2,128,1024]{2,1,0:T(8,128)(2,1)} %copy-done.1), custom_call_target="tpu_custom_call" | custom-call | flops 201326592 | bytes 2000000 | tf_op jit(solution)/shard_map/pallas_call | solution.py:56
  70.9 5.6 %collective-permute-start.2 = (bf16[384,128]{1,0:T(8,128)(2,1)}, bf16[384,128]{1,0:T(8,128)(2,1)S(1)}, u32[]{:S(2)}, u32[]{:S(2)}) collective-permute-start(bf16[384,128]{1,0:T(8,128)(2,1)} %shard_map.82), channel_id=1, source_target_pairs={{0,8},{8,16},{16,24},{24,32},{32,40},{40,48},{48,56},{56,64},{64,7... | collective-permute-start | bytes 294920 | tf_op jit(solution)/shard_map/ppermute | solution.py:39
  76.5 3.1 %shard_map.81.total = f32[384,128]{1,0:T(8,128)} custom-call(bf16[2,4,384,128]{3,2,1,0:T(8,128)(2,1)} %bitcast.18, bf16[2,4,384,128]{3,2,1,0:T(8,128)(2,1)} %bitcast.24, bf16[384,128]{1,0:T(8,128)(2,1)} %get-tuple-element.10.side, bf16[2,2,128,1024]{3,2,1,0:T(8,128)(2,1)} %lift_one.1, bf16[1,2,128,1024]{3,2,1,0:T(8,128)(2,1)} %lift_two.1), custom_call_target="tpu_custom_call" | custom-call | flops 201326592 | bytes 2000000 | tf_op jit(solution)/shard_map/pallas_call | solution.py:56
  79.6 0.0 all-to-all-done.3
  79.6 3.3 %all-gather.5 = bf16[8,384,128]{2,1,0:T(8,128)(2,1)} all-gather(bf16[4,384,128]{2,1,0:T(8,128)(2,1)S(1)} %all-to-all-done.3), channel_id=7, replica_groups={{0,1},{2,3},{4,5},{6,7},{8,9},{10,11},{12,13},{14,15},{16,17},{18,19},{..., dimensions={0}, use_global_device_ids=true | all-gather | bytes 1179648 | tf_op jit(solution)/shard_map/all_gather | solution.py:33
  83.0 0.0 collective-permute-done.2.before
  83.0 0.0 copy-start.3
  83.0 0.6 copy-done.3
  83.6 3.2 %shard_map.83 = (bf16[4,384,128]{2,1,0:T(8,128)(2,1)}, bf16[1,384,128]{2,1,0:T(8,128)(2,1)}) custom-call(bf16[2,4,384,128]{3,2,1,0:T(8,128)(2,1)} %bitcast.29, bf16[2,3,128,1024]{3,2,1,0:T(8,128)(2,1)} %solve.7, f32[384,128]{1,0:T(8,128)} %get-tuple-element.4.two, f32[384,128]{1,0:T(8,128)} %get-tuple-element.5.four, bf16[384,128]{1,0:T(8,128)(2,1)} %bitcast.31, ...), custom_call_target="tpu_custom_call" | custom-call | flops 201326592 | bytes 2000000 | tf_op jit(solution)/shard_map/pallas_call | solution.py:56
  (3 shorter events, 0.1 us)
Async XLA Ops:
  0.6 14.2 %collective-permute-start = (bf16[384,128]{1,0:T(8,128)(2,1)}, bf16[384,128]{1,0:T(8,128)(2,1)S(1)}, u32[]{:S(2)}, u32[]{:S(2)}) collective-permute-start(bf16[384,128]{1,0:T(8,128)(2,1)} %bitcast.30), channel_id=1, source_target_pairs={{8,0},{16,8},{24,16},{32,24},{40,32},{48,40},{56,48},{64,56},{72,6... | collective-permute-start | bytes 294920 | tf_op jit(solution)/shard_map/ppermute | solution.py:39
  5.4 5.4 %copy-start = (bf16[1,2,128,1024]{3,2,1,0:T(8,128)(2,1)S(1)}, bf16[1,2,128,1024]{3,2,1,0:T(8,128)(2,1)}, u32[]{:S(2)}) copy-start(bf16[1,2,128,1024]{3,2,1,0:T(8,128)(2,1)} %lift_two.1) | copy-start | bytes 1572868
  6.4 8.5 %copy-start.2 = (bf16[1,384,128]{2,1,0:T(8,128)(2,1)S(1)}, bf16[1,384,128]{2,1,0:T(8,128)(2,1)}, u32[]{:S(2)}) copy-start(bf16[1,384,128]{2,1,0:T(8,128)(2,1)} %param.7) | copy-start | bytes 294916
  6.4 14.4 %all-to-all-start = ((bf16[4,2,384,128]{3,2,1,0:T(8,128)(2,1)}), bf16[4,2,384,128]{3,2,1,0:T(8,128)(2,1)S(1)}, u32[]{:S(2)}, u32[]{:S(2)}) async-start(bf16[4,2,384,128]{3,2,1,0:T(8,128)(2,1)} %broadcast_in_dim.8), calls=%async_computation | async-start | bytes 1572864 | tf_op jit(solution)/shard_map/all_to_all | solution.py:28
  11.8 55.6 %collective-permute-start.1 = (bf16[2,128,1024]{2,1,0:T(8,128)(2,1)S(1)}, bf16[2,128,1024]{2,1,0:T(8,128)(2,1)S(1)}, u32[]{:S(2)}, u32[]{:S(2)}) collective-permute-start(bf16[2,128,1024]{2,1,0:T(8,128)(2,1)S(1)} %pad_maximum_fusion), channel_id=1, source_target_pairs={{8,0},{16,8},{24,16},{32,24},{40,32},{48,40},{56,48},{64,56},{72,6... | collective-permute-start | bytes 1572872 | tf_op jit(solution)/shard_map/ppermute | solution.py:39
  21.7 14.6 %all-to-all-start.2 = ((bf16[4,2,384,128]{3,2,1,0:T(8,128)(2,1)}), bf16[4,2,384,128]{3,2,1,0:T(8,128)(2,1)S(1)}, u32[]{:S(2)}, u32[]{:S(2)}) async-start(bf16[4,2,384,128]{3,2,1,0:T(8,128)(2,1)} %broadcast_in_dim.10), calls=%async_computation.2 | async-start | bytes 1572864 | tf_op jit(solution)/shard_map/all_to_all | solution.py:28
  38.1 14.5 %all-to-all-start.1 = ((bf16[4,384,128]{2,1,0:T(8,128)(2,1)}), bf16[4,384,128]{2,1,0:T(8,128)(2,1)S(1)}, u32[]{:S(2)}, u32[]{:S(2)}) async-start(bf16[4,384,128]{2,1,0:T(8,128)(2,1)} %broadcast_in_dim.9), calls=%async_computation.1 | async-start | bytes 786432 | tf_op jit(solution)/shard_map/all_to_all | solution.py:28
  59.1 20.5 %all-to-all-start.3 = ((bf16[4,384,128]{2,1,0:T(8,128)(2,1)}), bf16[4,384,128]{2,1,0:T(8,128)(2,1)S(1)}, u32[]{:S(2)}, u32[]{:S(2)}) async-start(bf16[4,384,128]{2,1,0:T(8,128)(2,1)} %broadcast_in_dim.11), calls=%async_computation.3 | async-start | bytes 786432 | tf_op jit(solution)/shard_map/all_to_all | solution.py:28
  67.4 0.8 copy-start.1
  70.9 12.1 %collective-permute-start.2 = (bf16[384,128]{1,0:T(8,128)(2,1)}, bf16[384,128]{1,0:T(8,128)(2,1)S(1)}, u32[]{:S(2)}, u32[]{:S(2)}) collective-permute-start(bf16[384,128]{1,0:T(8,128)(2,1)} %shard_map.82), channel_id=1, source_target_pairs={{0,8},{8,16},{16,24},{24,32},{32,40},{40,48},{48,56},{56,64},{64,7... | collective-permute-start | bytes 294920 | tf_op jit(solution)/shard_map/ppermute | solution.py:39
  83.0 0.6 copy-start.3

commit v2 on v1

v2 whole, which is shorter than its diff:
```python
import jax
import jax.numpy as jnp
from jax import lax
from jax.experimental import pallas as pl
from jax.experimental.pallas import tpu as pltpu
from jax.sharding import PartitionSpec as P


ROWS = 384
HALF = 192
WIDTH = 128
BF16 = jnp.bfloat16
F32 = jnp.float32
VMEM = pl.BlockSpec(memory_space=pltpu.VMEM)
HBM = pl.BlockSpec(memory_space=pltpu.HBM)


def chips_of(peers):
    return [[i for i in range(peers) if i % 2 == core] for core in range(2)]


def over_chips(copies):
    groups = chips_of(lax.axis_size("col"))
    return lax.all_to_all(copies, "col", 0, 0, axis_index_groups=groups)


def from_partner(array):
    peers = lax.axis_size("col")
    return lax.ppermute(array, "col", [(i, i ^ 1) for i in range(peers)])


def passed_along(array, by):
    peers = lax.axis_size("rad")
    pairs = [(i, i + by) for i in range(peers) if 0 <= i + by < peers]
    return lax.ppermute(array, "rad", pairs)


def apply(vector, matrix):
    return lax.dot_general(
        vector, matrix, (((1,), (1,)), ((), ())), preferred_element_type=F32
    )


def core():
    return lax.rem(lax.axis_index("col"), 2)


def call(body, outs, *args, products=1, space=pltpu.VMEM):
    args = [pltpu.with_memory_space_constraint(arg, pltpu.VMEM) for arg in args]
    return pl.pallas_call(
        body,
        out_shape=[space(shape, dtype) for shape, dtype in outs],
        in_specs=[VMEM] * len(args),
        out_specs=[VMEM] * len(outs),
        compiler_params=pltpu.CompilerParams(vmem_limit_bytes=12 << 20),
        cost_estimate=pl.CostEstimate(
            flops=products * 2 * ROWS * 1024 * WIDTH,
            bytes_accessed=products * 1000000,
            transcendentals=0,
        ),
    )(*args)


PAIR = ((2, HALF, WIDTH), BF16)
TOTALS = ((2, HALF, WIDTH), F32)
COPIES = ((4, 2, HALF, WIDTH), BF16)


def from_eight(blocks, which):
    return jnp.concatenate([blocks[peer, which] for peer in range(8)], axis=1)


def from_four(blocks):
    return jnp.concatenate(
        [blocks[chip, side] for chip in range(4) for side in range(2)], axis=1
    )


def pack_body(sides, coarse, packed, held, arrived, sent):
    arrays = [sides.at[1], sides.at[3], coarse.at[0]]
    loads = [
        pltpu.make_async_copy(array, held.at[i], arrived.at[i])
        for i, array in enumerate(arrays)
    ]
    for load in loads:
        load.start()
    stores = []
    for i, load in enumerate(loads):
        load.wait()
        for peer in range(8):
            store = pltpu.make_async_copy(
                held.at[i, peer % 2], packed.at[peer, i], sent.at[i, peer]
            )
            store.start()
            stores.append(store)
    for store in stores:
        store.wait()


def pack(sides, coarse):
    return pl.pallas_call(
        pack_body,
        out_shape=pltpu.HBM((8, 3, HALF, WIDTH), BF16),
        in_specs=[HBM, HBM],
        out_specs=HBM,
        scratch_shapes=[
            pltpu.VMEM((3, 2, HALF, WIDTH), BF16),
            pltpu.SemaphoreType.DMA((3,)),
            pltpu.SemaphoreType.DMA((3, 8)),
        ],
        compiler_params=pltpu.CompilerParams(vmem_limit_bytes=4 << 20),
    )(
        pltpu.with_memory_space_constraint(sides, pltpu.HBM),
        pltpu.with_memory_space_constraint(coarse, pltpu.HBM),
    )


def spread(copies, own, partner):
    mine = core()
    for chip in range(4):
        copies[chip, mine] = own
        copies[chip, 1 - mine] = partner


def middle_body(odd, sides, sides_partner, lift, lift_partner, copies):
    second, fourth = from_eight(odd, 0), from_eight(odd, 1)
    results = []
    for side, matrices in ((sides, lift), (sides_partner, lift_partner)):
        total = side[2, core()].astype(F32) - apply(second, matrices[1, 0])
        results.append((total - apply(fourth, matrices[1, 1])).astype(BF16))
    spread(copies, *results)


def coarse_body(odd, following, solve, solve_partner, totals):
    here = from_eight(odd, 2)
    after = jnp.concatenate([following[peer] for peer in range(8)], axis=1)
    for i, matrices in enumerate((solve, solve_partner)):
        totals[i] = apply(here, matrices[0, 1]) + apply(after, matrices[0, 2])


def centre_body(middle, solve, solve_partner, coarse, copies):
    full = from_four(middle)
    results = [
        (apply(full, matrices[0, 0]) - coarse[i]).astype(BF16)
        for i, matrices in enumerate((solve, solve_partner))
    ]
    spread(copies, *results)


def onward_body(odd, middle, lifts, totals):
    fourth, full = from_eight(odd, 1), from_four(middle)
    for i in range(2):
        both = apply(fourth, lifts[2 * i]) + apply(full, lifts[2 * i + 1])
        totals[i] = both.astype(BF16)


def reduced_body(
    odd, middle, sides, sides_partner, one, one_partner, two, two_partner, totals
):
    second, full = from_eight(odd, 0), from_four(middle)
    for i, (side, first, last) in enumerate(
        ((sides, one, two), (sides_partner, one_partner, two_partner))
    ):
        both = apply(second, first[0, 1]) + apply(full, last[0, 1])
        totals[i] = side[0, core()].astype(F32) - both


def odd_body(odd, following, solve, solve_partner, two, four):
    second, fourth, here = (from_eight(odd, i) for i in range(3))
    after = jnp.concatenate([following[peer] for peer in range(8)], axis=1)
    for i, matrices in enumerate((solve, solve_partner)):
        two[i] = apply(second, matrices[0, 0]) - apply(here, matrices[0, 1])
        four[i] = apply(fourth, matrices[1, 0]) - apply(after, matrices[1, 2])


def final_body(
    centre, own, solve, solve_partner, two, four, totals, before, kept, given
):
    full = from_four(centre)
    for i, (matrices, out) in enumerate(((solve, kept), (solve_partner, given))):
        out[0] = (two[i] - apply(full, matrices[0, 2])).astype(BF16)
        out[1] = own[0, core() if i == 0 else 1 - core()]
        out[2] = (four[i] - apply(full, matrices[1, 1])).astype(BF16)
        out[3] = (totals[i] - before[i].astype(F32)).astype(BF16)


def place_body(coarse, kept, taken, solved, reduced):
    solved[0] = coarse[0]
    mine = core()
    for half, source in ((mine, kept), (1 - mine, taken)):
        for i in range(3):
            solved[i + 1, half] = source[i]
        reduced[0, half] = source[3]


def steps(right_sides, coarse_solution, lift_one, solve_one, lift_two, solve_two):
    sides = right_sides.reshape(4, 2, HALF, WIDTH)
    coarse = coarse_solution.reshape(1, 2, HALF, WIDTH)

    packed = pack(sides, coarse)
    odd = lax.all_to_all(packed, "col", 0, 0)
    sides_partner = from_partner(sides)
    one_partner = from_partner(lift_one)
    two_partner = from_partner(lift_two)
    solve_two_partner = from_partner(solve_two)
    solve_one_partner = from_partner(solve_one)
    lifts = jnp.stack(
        [lift_one[0, 0], lift_two[0, 0], one_partner[0, 0], two_partner[0, 0]]
    )
    lifts_next = passed_along(lifts, -1)
    following = passed_along(odd[:, 2], -1)

    (middle_copies,) = call(
        middle_body,
        [COPIES],
        odd,
        sides,
        sides_partner,
        lift_one,
        one_partner,
        products=2,
        space=pltpu.HBM,
    )
    middle = over_chips(middle_copies)
    (coarse_totals,) = call(
        coarse_body,
        [TOTALS],
        odd,
        following,
        solve_two,
        solve_two_partner,
        products=2,
    )
    two, four = call(
        odd_body,
        [TOTALS, TOTALS],
        odd,
        following,
        solve_one,
        solve_one_partner,
        products=4,
    )
    (centre_copies,) = call(
        centre_body,
        [COPIES],
        middle,
        solve_two,
        solve_two_partner,
        coarse_totals,
        space=pltpu.HBM,
    )
    centre = over_chips(centre_copies)
    (onward,) = call(onward_body, [PAIR], odd, middle, lifts_next, products=2)
    before = passed_along(onward, 1)
    (totals,) = call(
        reduced_body,
        [TOTALS],
        odd,
        middle,
        sides,
        sides_partner,
        lift_one,
        one_partner,
        lift_two,
        two_partner,
        products=2,
    )
    quads = ((4, HALF, WIDTH), BF16)
    kept, given = call(
        final_body,
        [quads, quads],
        centre,
        centre_copies,
        solve_one,
        solve_one_partner,
        two,
        four,
        totals,
        before,
        products=2,
    )
    solved, reduced = call(
        place_body,
        [((4, 2, HALF, WIDTH), BF16), ((1, 2, HALF, WIDTH), BF16)],
        coarse,
        kept,
        from_partner(given),
        space=jax.ShapeDtypeStruct,
    )
    return solved.reshape(4, ROWS, WIDTH), reduced.reshape(1, ROWS, WIDTH)


def solution(mesh):
    return jax.shard_map(
        steps,
        mesh=mesh,
        in_specs=(
            P("rad", None, "col"),
            P("rad", None, "col"),
            P("rad", None, "col", None),
            P("rad", None, "col", None),
            P("rad", None, "col", None),
            P("rad", None, "col", None),
        ),
        out_specs=(P("rad", None, "col"), P("rad", None, "col")),
        check_vma=False,
    )
```

time: 87.5 us -> 89.2 us (1.019)
  the two profiles are of different devices: /device:TPU:251 before, /device:TPU:1 now
where the time goes in v2:
time: 89.2 us; the launch traced here: 88.2 us
  starting transfers between devices  37.1 us (42%)
  waiting for transfers between devices  20.9 us (23%)
  Pallas kernels  19.3 us (22%)
  local copies, waits for them, and re-layouts  8.91 us (10%)
  other arithmetic  1.1 us (1%)
  between operations  0.9 us (1%)
    ppermute x6, starting transfers between devices, from_partner(): return lax.ppermute(array, 'col', [(i, i ^ 1) for i in range(peers)])  20.4 us
    pallas_call x8, Pallas kernels, call(): pl.pallas_call(body, out_shape=[space(shape, dtype) for shape, dtype in o...  17.2 us
    ppermute x3, waiting for transfers between devices, passed_along(): return lax.ppermute(array, 'rad', pairs)  15.2 us
    all_to_all x2, starting transfers between devices, over_chips(): return lax.all_to_all(copies, 'col', 0, 0, axis_index_groups=groups)  8.13 us
    unnamed x32, local copies, waits for them, and re-layouts  5.16 us
    all_to_all x1, waiting for transfers between devices, steps(): odd = lax.all_to_all(packed, 'col', 0, 0)  4.6 us
    ppermute x3, starting transfers between devices, passed_along(): return lax.ppermute(array, 'rad', pairs)  4.47 us
    all_to_all x1, starting transfers between devices, steps(): odd = lax.all_to_all(packed, 'col', 0, 0)  4.11 us
  transfers between devices with their start and end apart: 12, of which 3 were waited for; matrix products, arithmetic and copies ran while one was open for 5% of the time, Pallas kernels for 19%

profile of v2, /device:TPU:1, one launch (start us, length us, event | category | flops | bytes accessed | tf_op | source)
XLA Modules:
  0.0 88.2 jit_solution(17196522787403503529)
XLA Ops:
  0.6 8.8 %collective-permute-start.1 = (bf16[2,2,128,1024]{3,2,1,0:T(8,128)(2,1)}, bf16[2,2,128,1024]{3,2,1,0:T(8,128)(2,1)}, u32[]{:S(2)}, u32[]{:S(2)}) collective-permute-start(bf16[2,2,128,1024]{3,2,1,0:T(8,128)(2,1)} %one.1), channel_id=1, source_target_pairs={{0,1},{1,0},{2,3},{3,2},{4,5},{5,4},{6,7},{7,6},{8,9},{9,8},{10,11... | collective-permute-start | bytes 3145736 | tf_op jit(solution)/shard_map/ppermute | solution.py:29
  9.4 1.9 %collective-permute-start.5 = (bf16[1,2,128,1024]{3,2,1,0:T(8,128)(2,1)}, bf16[1,2,128,1024]{3,2,1,0:T(8,128)(2,1)}, u32[]{:S(2)}, u32[]{:S(2)}) collective-permute-start(bf16[1,2,128,1024]{3,2,1,0:T(8,128)(2,1)} %two.1), channel_id=1, source_target_pairs={{0,1},{1,0},{2,3},{3,2},{4,5},{5,4},{6,7},{7,6},{8,9},{9,8},{10,11... | collective-permute-start | bytes 1572872 | tf_op jit(solution)/shard_map/ppermute | solution.py:29
  11.3 2.2 %shard_map.77 = bf16[8,3,192,128]{3,2,1,0:T(8,128)(2,1)} custom-call(bf16[4,2,192,128]{3,2,1,0:T(8,128)(2,1)} %bitcast.14, bf16[1,2,192,128]{3,2,1,0:T(8,128)(2,1)} %bitcast.18), custom_call_target="tpu_custom_call" | custom-call | tf_op jit(solution)/shard_map/pallas_call | solution.py:101
  13.5 0.0 copy-start
  13.5 0.0 copy-start.7
  13.5 4.1 %all-to-all-start = ((bf16[8,3,192,128]{3,2,1,0:T(8,128)(2,1)}), bf16[8,3,192,128]{3,2,1,0:T(8,128)(2,1)S(1)}, u32[]{:S(2)}, u32[]{:S(2)}) async-start(bf16[8,3,192,128]{3,2,1,0:T(8,128)(2,1)} %shard_map.77), calls=%async_computation | async-start | bytes 2359296 | tf_op jit(solution)/shard_map/all_to_all | solution.py:201
  17.6 2.0 %collective-permute-start.4 = (bf16[2,3,128,1024]{3,2,1,0:T(8,128)(2,1)S(1)}, bf16[2,3,128,1024]{3,2,1,0:T(8,128)(2,1)}, u32[]{:S(2)}, u32[]{:S(2)}) collective-permute-start(bf16[2,3,128,1024]{3,2,1,0:T(8,128)(2,1)S(1)} %copy-done), channel_id=1, source_target_pairs={{0,1},{1,0},{2,3},{3,2},{4,5},{5,4},{6,7},{7,6},{8,9},{9,8},{10,11... | collective-permute-start | bytes 4718600 | tf_op jit(solution)/shard_map/ppermute | solution.py:29
  19.7 1.0 %slice_bitcast_fusion.4 = bf16[1,128,1024]{2,1,0:T(8,128)(2,1)S(1)} fusion(bf16[2,2,128,1024]{3,2,1,0:T(8,128)(2,1)} %one.1), kind=kLoop, calls=%fused_computation.5 | loop fusion | bytes 524288 | tf_op jit(solution)/shard_map/stack;squeeze | solution.py:207
  20.7 0.0 collective-permute-done.5.two_partner
  20.7 1.0 %slice_bitcast_fusion.1 = bf16[1,128,1024]{2,1,0:T(8,128)(2,1)S(1)} fusion(bf16[1,2,128,1024]{3,2,1,0:T(8,128)(2,1)} %collective-permute-done.5.two_partner), kind=kLoop, calls=%fused_computation.2 | loop fusion | bytes 524288 | tf_op jit(solution)/shard_map/stack;squeeze | solution.py:207
  21.6 0.0 copy-start.4
  21.6 0.0 collective-permute-done.1.lift_partner.one_partner
  21.7 1.0 %slice_bitcast_fusion.2 = bf16[1,128,1024]{2,1,0:T(8,128)(2,1)S(1)} fusion(bf16[2,2,128,1024]{3,2,1,0:T(8,128)(2,1)} %collective-permute-done.1.lift_partner.one_partner), kind=kLoop, calls=%fused_computation.3 | loop fusion | bytes 524288 | tf_op jit(solution)/shard_map/stack;squeeze | solution.py:207
  22.7 1.1 %pad_maximum_fusion = bf16[4,128,1024]{2,1,0:T(8,128)(2,1)} fusion(bf16[1,128,1024]{2,1,0:T(8,128)(2,1)S(1)} %slice_bitcast_fusion.1, bf16[1,128,1024]{2,1,0:T(8,128)(2,1)S(1)} %slice_bitcast_fusion.2, bf16[1,128,1024]{2,1,0:T(8,128)(2,1)S(1)} %slice_bitcast_fusion.3, bf16[1,128,1024]{2,1,0:T(8,128)(2,1)S(1)} %slice_bitcast_fusion.4), kind=kLoop, calls=%fused_computation | loop fusion | flops 1572864 | bytes 2097152 | tf_op jit(solution)/shard_map/stack | solution.py:207
  23.8 1.3 %collective-permute-start.6 = (bf16[4,128,1024]{2,1,0:T(8,128)(2,1)}, bf16[4,128,1024]{2,1,0:T(8,128)(2,1)}, u32[]{:S(2)}, u32[]{:S(2)}) collective-permute-start(bf16[4,128,1024]{2,1,0:T(8,128)(2,1)} %pad_maximum_fusion), channel_id=1, source_target_pairs={{8,0},{16,8},{24,16},{32,24},{40,32},{48,40},{56,48},{64,56},{72,6... | collective-permute-start | bytes 3145736 | tf_op jit(solution)/shard_map/ppermute | solution.py:35
  25.1 2.3 %collective-permute-start.2 = (bf16[1,3,128,1024]{3,2,1,0:T(8,128)(2,1)}, bf16[1,3,128,1024]{3,2,1,0:T(8,128)(2,1)}, u32[]{:S(2)}, u32[]{:S(2)}) collective-permute-start(bf16[1,3,128,1024]{3,2,1,0:T(8,128)(2,1)} %solve.5), channel_id=1, source_target_pairs={{0,1},{1,0},{2,3},{3,2},{4,5},{5,4},{6,7},{7,6},{8,9},{9,8},{10,11... | collective-permute-start | bytes 2359304 | tf_op jit(solution)/shard_map/ppermute | solution.py:29
  27.4 2.0 %collective-permute-start = (bf16[4,2,192,128]{3,2,1,0:T(8,128)(2,1)S(1)}, bf16[4,2,192,128]{3,2,1,0:T(8,128)(2,1)S(1)}, u32[]{:S(2)}, u32[]{:S(2)}) collective-permute-start(bf16[4,2,192,128]{3,2,1,0:T(8,128)(2,1)S(1)} %bitcast.15), channel_id=1, source_target_pairs={{0,1},{1,0},{2,3},{3,2},{4,5},{5,4},{6,7},{7,6},{8,9},{9,8},{10,11... | collective-permute-start | bytes 1179656 | tf_op jit(solution)/shard_map/ppermute | solution.py:29
  29.4 4.6 %all-to-all-done.odd = bf16[8,3,192,128]{3,2,1,0:T(8,128)(2,1)S(1)} async-done(((bf16[8,3,192,128]{3,2,1,0:T(8,128)(2,1)}), bf16[8,3,192,128]{3,2,1,0:T(8,128)(2,1)S(1)}, u32[]{:S(2)}, u32[]{:S(2)}) %all-to-all-start) | async-done | bytes 1179680 | tf_op jit(solution)/shard_map/all_to_all | solution.py:201
  34.0 0.8 slice_bitcast_fusion
  34.8 1.3 %collective-permute-start.3 = (bf16[8,192,128]{2,1,0:T(8,128)(2,1)}, bf16[8,192,128]{2,1,0:T(8,128)(2,1)}, u32[]{:S(2)}, u32[]{:S(2)}) collective-permute-start(bf16[8,192,128]{2,1,0:T(8,128)(2,1)} %slice_bitcast_fusion), channel_id=1, source_target_pairs={{8,0},{16,8},{24,16},{32,24},{40,32},{48,40},{56,48},{64,56},{72,6... | collective-permute-start | bytes 1179656 | tf_op jit(solution)/shard_map/ppermute | solution.py:35
  36.1 0.0 collective-permute-done.sides_partner
  36.1 0.0 copy-start.1
  36.1 1.2 %copy-done.1 = bf16[2,2,128,1024]{3,2,1,0:T(8,128)(2,1)S(1)} copy-done((bf16[2,2,128,1024]{3,2,1,0:T(8,128)(2,1)S(1)}, bf16[2,2,128,1024]{3,2,1,0:T(8,128)(2,1)}, u32[]{:S(2)}) %copy-start.1) | copy-done | bytes 1048600
  37.3 2.7 %shard_map.78 = bf16[4,2,192,128]{3,2,1,0:T(8,128)(2,1)} custom-call(bf16[8,3,192,128]{3,2,1,0:T(8,128)(2,1)S(1)} %all-to-all-done.odd, bf16[4,2,192,128]{3,2,1,0:T(8,128)(2,1)S(1)} %bitcast.16, bf16[4,2,192,128]{3,2,1,0:T(8,128)(2,1)S(1)} %collective-permute-done.sides_partner, bf16[2,2,128,1024]{3,2,1,0:T(8,128)(2,1)S(1)} %copy-done.1, ...), custom_call_target="tpu_custom_call" | custom-call | flops 201326592 | bytes 2000000 | tf_op jit(solution)/shard_map/pallas_call | solution.py:50
  40.0 3.5 %all-to-all-start.1 = ((bf16[4,2,192,128]{3,2,1,0:T(8,128)(2,1)}), bf16[4,2,192,128]{3,2,1,0:T(8,128)(2,1)S(1)}, u32[]{:S(2)}, u32[]{:S(2)}) async-start(bf16[4,2,192,128]{3,2,1,0:T(8,128)(2,1)} %shard_map.78), calls=%async_computation.1 | async-start | bytes 786432 | tf_op jit(solution)/shard_map/all_to_all | solution.py:24
  43.5 0.0 collective-permute-done.2.solve_partner
  43.5 15.2 %collective-permute-done.3.following = bf16[8,192,128]{2,1,0:T(8,128)(2,1)} collective-permute-done((bf16[8,192,128]{2,1,0:T(8,128)(2,1)}, bf16[8,192,128]{2,1,0:T(8,128)(2,1)}, u32[]{:S(2)}, u32[]{:S(2)}) %collective-permute-start.3) | collective-permute-done | bytes 393248 | tf_op jit(solution)/shard_map/ppermute | solution.py:35
  58.7 2.0 %shard_map.79.coarse = f32[2,192,128]{2,1,0:T(8,128)S(1)} custom-call(bf16[8,3,192,128]{3,2,1,0:T(8,128)(2,1)S(1)} %all-to-all-done.odd, bf16[8,192,128]{2,1,0:T(8,128)(2,1)} %collective-permute-done.3.following, bf16[1,3,128,1024]{3,2,1,0:T(8,128)(2,1)} %solve.5, bf16[1,3,128,1024]{3,2,1,0:T(8,128)(2,1)} %collective-permute-done.2.solve_partner), custom_call_target="tpu_custom_call" | custom-call | flops 201326592 | bytes 2000000 | tf_op jit(solution)/shard_map/pallas_call | solution.py:50
  60.8 0.7 copy-done.11
  61.5 0.0 all-to-all-done.1.middle
  61.5 0.9 %copy-done.12 = f32[2,192,128]{2,1,0:T(8,128)S(1)} copy-done((f32[2,192,128]{2,1,0:T(8,128)S(1)}, f32[2,192,128]{2,1,0:T(8,128)}, u32[]{:S(2)}) %copy-start.12) | copy-done | bytes 196632
  62.4 2.5 %shard_map.80.own = bf16[4,2,192,128]{3,2,1,0:T(8,128)(2,1)} custom-call(bf16[4,2,192,128]{3,2,1,0:T(8,128)(2,1)S(1)} %all-to-all-done.1.middle, bf16[1,3,128,1024]{3,2,1,0:T(8,128)(2,1)} %solve.5, bf16[1,3,128,1024]{3,2,1,0:T(8,128)(2,1)} %collective-permute-done.2.solve_partner, f32[2,192,128]{2,1,0:T(8,128)S(1)} %copy-done.12), custom_call_target="tpu_custom_call" | custom-call | flops 100663296 | bytes 1000000 | tf_op jit(solution)/shard_map/pallas_call | solution.py:50
  64.9 4.7 %all-to-all-start.2 = ((bf16[4,2,192,128]{3,2,1,0:T(8,128)(2,1)}), bf16[4,2,192,128]{3,2,1,0:T(8,128)(2,1)}, u32[]{:S(2)}, u32[]{:S(2)}) async-start(bf16[4,2,192,128]{3,2,1,0:T(8,128)(2,1)} %shard_map.80.own), calls=%async_computation.2 | async-start | bytes 786432 | tf_op jit(solution)/shard_map/all_to_all | solution.py:24
  69.6 0.0 collective-permute-done.6.lifts
  69.6 2.6 %shard_map.83 = bf16[2,192,128]{2,1,0:T(8,128)(2,1)} custom-call(bf16[8,3,192,128]{3,2,1,0:T(8,128)(2,1)S(1)} %all-to-all-done.odd, bf16[4,2,192,128]{3,2,1,0:T(8,128)(2,1)S(1)} %all-to-all-done.1.middle, bf16[4,128,1024]{2,1,0:T(8,128)(2,1)} %collective-permute-done.6.lifts), custom_call_target="tpu_custom_call" | custom-call | flops 201326592 | bytes 2000000 | tf_op jit(solution)/shard_map/pallas_call | solution.py:50
  72.2 1.9 %collective-permute-start.7 = (bf16[2,192,128]{2,1,0:T(8,128)(2,1)}, bf16[2,192,128]{2,1,0:T(8,128)(2,1)}, u32[]{:S(2)}, u32[]{:S(2)}) collective-permute-start(bf16[2,192,128]{2,1,0:T(8,128)(2,1)} %shard_map.83), channel_id=1, source_target_pairs={{0,8},{8,16},{16,24},{24,32},{32,40},{40,48},{48,56},{56,64},{64,7... | collective-permute-start | bytes 294920 | tf_op jit(solution)/shard_map/ppermute | solution.py:35
  74.1 1.9 %shard_map.82.totals = f32[2,192,128]{2,1,0:T(8,128)S(1)} custom-call(bf16[8,3,192,128]{3,2,1,0:T(8,128)(2,1)S(1)} %all-to-all-done.odd, bf16[4,2,192,128]{3,2,1,0:T(8,128)(2,1)S(1)} %all-to-all-done.1.middle, bf16[4,2,192,128]{3,2,1,0:T(8,128)(2,1)S(1)} %bitcast.17, bf16[4,2,192,128]{3,2,1,0:T(8,128)(2,1)S(1)} %copy-done.6, ...), custom_call_target="tpu_custom_call" | custom-call | flops 201326592 | bytes 2000000 | tf_op jit(solution)/shard_map/pallas_call | solution.py:50
  76.0 0.7 copy-done.9
  76.7 0.0 collective-permute-done.4.solve_partner
  76.7 2.6 %shard_map.81 = (f32[2,192,128]{2,1,0:T(8,128)S(1)}, f32[2,192,128]{2,1,0:T(8,128)S(1)}) custom-call(bf16[8,3,192,128]{3,2,1,0:T(8,128)(2,1)S(1)} %all-to-all-done.odd, bf16[8,192,128]{2,1,0:T(8,128)(2,1)} %collective-permute-done.3.following, bf16[2,3,128,1024]{3,2,1,0:T(8,128)(2,1)S(1)} %copy-done, ...), custom_call_target="tpu_custom_call" | custom-call | flops 402653184 | bytes 4000000 | tf_op jit(solution)/shard_map/pallas_call | solution.py:50
  79.3 0.7 copy-done.14
  80.0 0.0 all-to-all-done.2.centre
  80.0 0.0 collective-permute-done.7.before
  80.0 0.9 %copy-done.15 = f32[2,192,128]{2,1,0:T(8,128)S(1)} copy-done((f32[2,192,128]{2,1,0:T(8,128)S(1)}, f32[2,192,128]{2,1,0:T(8,128)}, u32[]{:S(2)}) %copy-start.15) | copy-done | bytes 196632
  80.9 2.1 %shard_map.84 = (bf16[4,192,128]{2,1,0:T(8,128)(2,1)S(1)}, bf16[4,192,128]{2,1,0:T(8,128)(2,1)S(1)}) custom-call(bf16[4,2,192,128]{3,2,1,0:T(8,128)(2,1)} %all-to-all-done.2.centre, bf16[4,2,192,128]{3,2,1,0:T(8,128)(2,1)S(1)} %copy-done.3, bf16[2,3,128,1024]{3,2,1,0:T(8,128)(2,1)S(1)} %copy-done, ...), custom_call_target="tpu_custom_call" | custom-call | flops 201326592 | bytes 2000000 | tf_op jit(solution)/shard_map/pallas_call | solution.py:50
  83.0 3.3 %collective-permute-start.8 = (bf16[4,192,128]{2,1,0:T(8,128)(2,1)S(1)}, bf16[4,192,128]{2,1,0:T(8,128)(2,1)S(1)}, u32[]{:S(2)}, u32[]{:S(2)}) collective-permute-start(bf16[4,192,128]{2,1,0:T(8,128)(2,1)S(1)} %get-tuple-element.11), channel_id=1, source_target_pairs={{0,1},{1,0},{2,3},{3,2},{4,5},{5,4},{6,7},{7,6},{8,9},{9,8},{10,11... | collective-permute-start | bytes 589832 | tf_op jit(solution)/shard_map/ppermute | solution.py:29
  86.4 1.0 %collective-permute-done.8.taken = bf16[4,192,128]{2,1,0:T(8,128)(2,1)S(1)} collective-permute-done((bf16[4,192,128]{2,1,0:T(8,128)(2,1)S(1)}, bf16[4,192,128]{2,1,0:T(8,128)(2,1)S(1)}, u32[]{:S(2)}, u32[]{:S(2)}) %collective-permute-start.8) | collective-permute-done | bytes 196640 | tf_op jit(solution)/shard_map/ppermute | solution.py:29
  87.4 0.8 shard_map.85
  (23 shorter events, 0.1 us)
Async XLA Ops:
  0.6 21.0 %collective-permute-start.1 = (bf16[2,2,128,1024]{3,2,1,0:T(8,128)(2,1)}, bf16[2,2,128,1024]{3,2,1,0:T(8,128)(2,1)}, u32[]{:S(2)}, u32[]{:S(2)}) collective-permute-start(bf16[2,2,128,1024]{3,2,1,0:T(8,128)(2,1)} %one.1), channel_id=1, source_target_pairs={{0,1},{1,0},{2,3},{3,2},{4,5},{5,4},{6,7},{7,6},{8,9},{9,8},{10,11... | collective-permute-start | bytes 3145736 | tf_op jit(solution)/shard_map/ppermute | solution.py:29
  9.4 11.3 %collective-permute-start.5 = (bf16[1,2,128,1024]{3,2,1,0:T(8,128)(2,1)}, bf16[1,2,128,1024]{3,2,1,0:T(8,128)(2,1)}, u32[]{:S(2)}, u32[]{:S(2)}) collective-permute-start(bf16[1,2,128,1024]{3,2,1,0:T(8,128)(2,1)} %two.1), channel_id=1, source_target_pairs={{0,1},{1,0},{2,3},{3,2},{4,5},{5,4},{6,7},{7,6},{8,9},{9,8},{10,11... | collective-permute-start | bytes 1572872 | tf_op jit(solution)/shard_map/ppermute | solution.py:29
  13.5 4.1 %copy-start = (bf16[2,3,128,1024]{3,2,1,0:T(8,128)(2,1)S(1)}, bf16[2,3,128,1024]{3,2,1,0:T(8,128)(2,1)}, u32[]{:S(2)}) copy-start(bf16[2,3,128,1024]{3,2,1,0:T(8,128)(2,1)} %solve.7) | copy-start | bytes 4718596
  13.5 6.2 %copy-start.7 = (bf16[1,2,128,1024]{3,2,1,0:T(8,128)(2,1)S(1)}, bf16[1,2,128,1024]{3,2,1,0:T(8,128)(2,1)}, u32[]{:S(2)}) copy-start(bf16[1,2,128,1024]{3,2,1,0:T(8,128)(2,1)} %two.1) | copy-start | bytes 1572868
  13.5 20.5 %all-to-all-start = ((bf16[8,3,192,128]{3,2,1,0:T(8,128)(2,1)}), bf16[8,3,192,128]{3,2,1,0:T(8,128)(2,1)S(1)}, u32[]{:S(2)}, u32[]{:S(2)}) async-start(bf16[8,3,192,128]{3,2,1,0:T(8,128)(2,1)} %shard_map.77), calls=%async_computation | async-start | bytes 2359296 | tf_op jit(solution)/shard_map/all_to_all | solution.py:201
  17.6 59.1 %collective-permute-start.4 = (bf16[2,3,128,1024]{3,2,1,0:T(8,128)(2,1)S(1)}, bf16[2,3,128,1024]{3,2,1,0:T(8,128)(2,1)}, u32[]{:S(2)}, u32[]{:S(2)}) collective-permute-start(bf16[2,3,128,1024]{3,2,1,0:T(8,128)(2,1)S(1)} %copy-done), channel_id=1, source_target_pairs={{0,1},{1,0},{2,3},{3,2},{4,5},{5,4},{6,7},{7,6},{8,9},{9,8},{10,11... | collective-permute-start | bytes 4718600 | tf_op jit(solution)/shard_map/ppermute | solution.py:29
  21.6 5.7 %copy-start.4 = (bf16[4,384,128]{2,1,0:T(8,128)(2,1)S(1)}, bf16[4,384,128]{2,1,0:T(8,128)(2,1)}, u32[]{:S(2)}) copy-start(bf16[4,384,128]{2,1,0:T(8,128)(2,1)} %param.6) | copy-start | bytes 1179652
  23.8 45.8 %collective-permute-start.6 = (bf16[4,128,1024]{2,1,0:T(8,128)(2,1)}, bf16[4,128,1024]{2,1,0:T(8,128)(2,1)}, u32[]{:S(2)}, u32[]{:S(2)}) collective-permute-start(bf16[4,128,1024]{2,1,0:T(8,128)(2,1)} %pad_maximum_fusion), channel_id=1, source_target_pairs={{8,0},{16,8},{24,16},{32,24},{40,32},{48,40},{56,48},{64,56},{72,6... | collective-permute-start | bytes 3145736 | tf_op jit(solution)/shard_map/ppermute | solution.py:35
  25.1 18.4 %collective-permute-start.2 = (bf16[1,3,128,1024]{3,2,1,0:T(8,128)(2,1)}, bf16[1,3,128,1024]{3,2,1,0:T(8,128)(2,1)}, u32[]{:S(2)}, u32[]{:S(2)}) collective-permute-start(bf16[1,3,128,1024]{3,2,1,0:T(8,128)(2,1)} %solve.5), channel_id=1, source_target_pairs={{0,1},{1,0},{2,3},{3,2},{4,5},{5,4},{6,7},{7,6},{8,9},{9,8},{10,11... | collective-permute-start | bytes 2359304 | tf_op jit(solution)/shard_map/ppermute | solution.py:29
  27.4 8.7 %collective-permute-start = (bf16[4,2,192,128]{3,2,1,0:T(8,128)(2,1)S(1)}, bf16[4,2,192,128]{3,2,1,0:T(8,128)(2,1)S(1)}, u32[]{:S(2)}, u32[]{:S(2)}) collective-permute-start(bf16[4,2,192,128]{3,2,1,0:T(8,128)(2,1)S(1)} %bitcast.15), channel_id=1, source_target_pairs={{0,1},{1,0},{2,3},{3,2},{4,5},{5,4},{6,7},{7,6},{8,9},{9,8},{10,11... | collective-permute-start | bytes 1179656 | tf_op jit(solution)/shard_map/ppermute | solution.py:29
  34.8 23.9 %collective-permute-start.3 = (bf16[8,192,128]{2,1,0:T(8,128)(2,1)}, bf16[8,192,128]{2,1,0:T(8,128)(2,1)}, u32[]{:S(2)}, u32[]{:S(2)}) collective-permute-start(bf16[8,192,128]{2,1,0:T(8,128)(2,1)} %slice_bitcast_fusion), channel_id=1, source_target_pairs={{8,0},{16,8},{24,16},{32,24},{40,32},{48,40},{56,48},{64,56},{72,6... | collective-permute-start | bytes 1179656 | tf_op jit(solution)/shard_map/ppermute | solution.py:35
  36.1 1.2 %copy-start.1 = (bf16[2,2,128,1024]{3,2,1,0:T(8,128)(2,1)S(1)}, bf16[2,2,128,1024]{3,2,1,0:T(8,128)(2,1)}, u32[]{:S(2)}) copy-start(bf16[2,2,128,1024]{3,2,1,0:T(8,128)(2,1)} %one.1) | copy-start | bytes 3145732
  37.3 2.7 %copy-start.5 = (bf16[4,2,192,128]{3,2,1,0:T(8,128)(2,1)}, bf16[4,2,192,128]{3,2,1,0:T(8,128)(2,1)S(1)}, u32[]{:S(2)}) copy-start(bf16[4,2,192,128]{3,2,1,0:T(8,128)(2,1)S(1)} %collective-permute-done.sides_partner) | copy-start | bytes 1179652
  40.0 21.5 %all-to-all-start.1 = ((bf16[4,2,192,128]{3,2,1,0:T(8,128)(2,1)}), bf16[4,2,192,128]{3,2,1,0:T(8,128)(2,1)S(1)}, u32[]{:S(2)}, u32[]{:S(2)}) async-start(bf16[4,2,192,128]{3,2,1,0:T(8,128)(2,1)} %shard_map.78), calls=%async_computation.1 | async-start | bytes 786432 | tf_op jit(solution)/shard_map/all_to_all | solution.py:24
  60.8 0.7 copy-start.11
  61.5 0.9 %copy-start.12 = (f32[2,192,128]{2,1,0:T(8,128)S(1)}, f32[2,192,128]{2,1,0:T(8,128)}, u32[]{:S(2)}) copy-start(f32[2,192,128]{2,1,0:T(8,128)} %copy-done.11) | copy-start | bytes 589828
  64.9 15.1 %all-to-all-start.2 = ((bf16[4,2,192,128]{3,2,1,0:T(8,128)(2,1)}), bf16[4,2,192,128]{3,2,1,0:T(8,128)(2,1)}, u32[]{:S(2)}, u32[]{:S(2)}) async-start(bf16[4,2,192,128]{3,2,1,0:T(8,128)(2,1)} %shard_map.80.own), calls=%async_computation.2 | async-start | bytes 786432 | tf_op jit(solution)/shard_map/all_to_all | solution.py:24
  69.6 4.5 %copy-start.2 = (bf16[2,2,128,1024]{3,2,1,0:T(8,128)(2,1)S(1)}, bf16[2,2,128,1024]{3,2,1,0:T(8,128)(2,1)}, u32[]{:S(2)}) copy-start(bf16[2,2,128,1024]{3,2,1,0:T(8,128)(2,1)} %one.1) | copy-start | bytes 3145732
  69.6 4.5 %copy-start.6 = (bf16[4,2,192,128]{3,2,1,0:T(8,128)(2,1)S(1)}, bf16[4,2,192,128]{3,2,1,0:T(8,128)(2,1)}, u32[]{:S(2)}) copy-start(bf16[4,2,192,128]{3,2,1,0:T(8,128)(2,1)} %copy-done.5) | copy-start | bytes 1179652
  69.6 4.5 %copy-start.8 = (bf16[1,2,128,1024]{3,2,1,0:T(8,128)(2,1)S(1)}, bf16[1,2,128,1024]{3,2,1,0:T(8,128)(2,1)}, u32[]{:S(2)}) copy-start(bf16[1,2,128,1024]{3,2,1,0:T(8,128)(2,1)} %two.1) | copy-start | bytes 1572868
  72.2 7.8 %collective-permute-start.7 = (bf16[2,192,128]{2,1,0:T(8,128)(2,1)}, bf16[2,192,128]{2,1,0:T(8,128)(2,1)}, u32[]{:S(2)}, u32[]{:S(2)}) collective-permute-start(bf16[2,192,128]{2,1,0:T(8,128)(2,1)} %shard_map.83), channel_id=1, source_target_pairs={{0,8},{8,16},{16,24},{24,32},{32,40},{40,48},{48,56},{56,64},{64,7... | collective-permute-start | bytes 294920 | tf_op jit(solution)/shard_map/ppermute | solution.py:35
  76.0 0.7 copy-start.9
  76.7 3.3 %copy-start.3 = (bf16[4,2,192,128]{3,2,1,0:T(8,128)(2,1)S(1)}, bf16[4,2,192,128]{3,2,1,0:T(8,128)(2,1)}, u32[]{:S(2)}) copy-start(bf16[4,2,192,128]{3,2,1,0:T(8,128)(2,1)} %shard_map.80.own) | copy-start | bytes 1179652
  76.7 3.3 %copy-start.10 = (f32[2,192,128]{2,1,0:T(8,128)S(1)}, f32[2,192,128]{2,1,0:T(8,128)}, u32[]{:S(2)}) copy-start(f32[2,192,128]{2,1,0:T(8,128)} %copy-done.9) | copy-start | bytes 589828
  79.3 0.7 copy-start.14
  80.0 0.9 %copy-start.15 = (f32[2,192,128]{2,1,0:T(8,128)S(1)}, f32[2,192,128]{2,1,0:T(8,128)}, u32[]{:S(2)}) copy-start(f32[2,192,128]{2,1,0:T(8,128)} %copy-done.14) | copy-start | bytes 589828
  80.9 6.5 %copy-start.13 = (bf16[1,384,128]{2,1,0:T(8,128)(2,1)S(1)}, bf16[1,384,128]{2,1,0:T(8,128)(2,1)}, u32[]{:S(2)}) copy-start(bf16[1,384,128]{2,1,0:T(8,128)(2,1)} %param.7) | copy-start | bytes 294916
  83.0 4.4 %collective-permute-start.8 = (bf16[4,192,128]{2,1,0:T(8,128)(2,1)S(1)}, bf16[4,192,128]{2,1,0:T(8,128)(2,1)S(1)}, u32[]{:S(2)}, u32[]{:S(2)}) collective-permute-start(bf16[4,192,128]{2,1,0:T(8,128)(2,1)S(1)} %get-tuple-element.11), channel_id=1, source_target_pairs={{0,1},{1,0},{2,3},{3,2},{4,5},{5,4},{6,7},{7,6},{8,9},{9,8},{10,11... | collective-permute-start | bytes 589832 | tf_op jit(solution)/shard_map/ppermute | solution.py:29

commit v3 on v2

v3 whole, which is shorter than its diff:
```python
import jax
import jax.numpy as jnp
from jax import lax
from jax.experimental import pallas as pl
from jax.experimental.pallas import tpu as pltpu
from jax.sharding import PartitionSpec as P


ROWS = 384
HALF = 192
WIDTH = 128
BF16 = jnp.bfloat16
F32 = jnp.float32
VMEM = pl.BlockSpec(memory_space=pltpu.VMEM)
HBM = pl.BlockSpec(memory_space=pltpu.HBM)


def chips_of(peers):
    return [[i for i in range(peers) if i % 2 == core] for core in range(2)]


def over_chips(copies):
    groups = chips_of(lax.axis_size("col"))
    return lax.all_to_all(copies, "col", 0, 0, axis_index_groups=groups)


def from_partner(array):
    peers = lax.axis_size("col")
    return lax.ppermute(array, "col", [(i, i ^ 1) for i in range(peers)])


def passed_along(array, by):
    peers = lax.axis_size("rad")
    pairs = [(i, i + by) for i in range(peers) if 0 <= i + by < peers]
    return lax.ppermute(array, "rad", pairs)


def apply(vector, matrix):
    return lax.dot_general(
        vector, matrix, (((1,), (1,)), ((), ())), preferred_element_type=F32
    )


def core():
    return lax.rem(lax.axis_index("col"), 2)


class Part:
    def __init__(self, array, index=()):
        self.array, self.index = array, index
        self.shape = array.shape[len(index) :]

    def load(self, source, held, sem):
        index = tuple(i() if callable(i) else i for i in self.index)
        self.held, self.ready = held, False
        self.copy = pltpu.make_async_copy(
            source.at[index] if index else source, held, sem
        )
        self.copy.start()

    def __getitem__(self, index):
        if not self.ready:
            self.copy.wait()
            self.ready = True
        return self.held[index]


def call(body, outs, whole, parts, products=1, space=pltpu.HBM):
    count, pieces = len(whole), len(parts)

    def kernel(*refs):
        sources = refs[count : count + pieces]
        results = refs[count + pieces : count + pieces + len(outs)]
        held, sems = refs[count + pieces + len(outs) : -1], refs[-1]
        for i, part in enumerate(parts):
            part.load(sources[i], held[i], sems.at[i])
        body(*refs[:count], *parts, *results)

    return pl.pallas_call(
        kernel,
        out_shape=[space(shape, dtype) for shape, dtype in outs],
        in_specs=[VMEM] * count + [HBM] * pieces,
        out_specs=[VMEM] * len(outs),
        scratch_shapes=[pltpu.VMEM(part.shape, part.array.dtype) for part in parts]
        + [pltpu.SemaphoreType.DMA((pieces,))],
        compiler_params=pltpu.CompilerParams(vmem_limit_bytes=12 << 20),
        cost_estimate=pl.CostEstimate(
            flops=products * 2 * ROWS * 1024 * WIDTH,
            bytes_accessed=products * 1000000,
            transcendentals=0,
        ),
    )(
        *[pltpu.with_memory_space_constraint(array, pltpu.VMEM) for array in whole],
        *[pltpu.with_memory_space_constraint(p.array, pltpu.HBM) for p in parts],
    )


PAIR = ((2, HALF, WIDTH), BF16)
TOTALS = ((2, HALF, WIDTH), F32)
COPIES = ((4, 2, HALF, WIDTH), BF16)


def from_eight(blocks, which):
    return jnp.concatenate([blocks[peer, which] for peer in range(8)], axis=1)


def from_four(blocks):
    return jnp.concatenate(
        [blocks[chip, side] for chip in range(4) for side in range(2)], axis=1
    )


def pack_body(sides, coarse, packed, held, arrived, sent):
    arrays = [sides.at[1], sides.at[3], coarse.at[0]]
    loads = [
        pltpu.make_async_copy(array, held.at[i], arrived.at[i])
        for i, array in enumerate(arrays)
    ]
    for load in loads:
        load.start()
    stores = []
    for i, load in enumerate(loads):
        load.wait()
        for peer in range(8):
            store = pltpu.make_async_copy(
                held.at[i, peer % 2], packed.at[peer, i], sent.at[i, peer]
            )
            store.start()
            stores.append(store)
    for store in stores:
        store.wait()


def pack(sides, coarse):
    return pl.pallas_call(
        pack_body,
        out_shape=pltpu.HBM((8, 3, HALF, WIDTH), BF16),
        in_specs=[HBM, HBM],
        out_specs=HBM,
        scratch_shapes=[
            pltpu.VMEM((3, 2, HALF, WIDTH), BF16),
            pltpu.SemaphoreType.DMA((3,)),
            pltpu.SemaphoreType.DMA((3, 8)),
        ],
        compiler_params=pltpu.CompilerParams(vmem_limit_bytes=4 << 20),
    )(
        pltpu.with_memory_space_constraint(sides, pltpu.HBM),
        pltpu.with_memory_space_constraint(coarse, pltpu.HBM),
    )


def spread(copies, own, partner):
    mine = core()
    for chip in range(4):
        copies[chip, mine] = own
        copies[chip, 1 - mine] = partner


def from_following(following):
    return jnp.concatenate([following[peer] for peer in range(8)], axis=1)


def middle_body(odd, one, one_partner, side, side_partner, copies):
    second, fourth = from_eight(odd, 0), from_eight(odd, 1)
    results = []
    for begun, matrices in ((side, one), (side_partner, one_partner)):
        both = apply(second, matrices[0]) + apply(fourth, matrices[1])
        results.append((begun[...].astype(F32) - both).astype(BF16))
    spread(copies, *results)


def coarse_body(odd, solve, solve_partner, following, totals):
    here = from_eight(odd, 2)
    for i, matrices in enumerate((solve, solve_partner)):
        totals[i] = apply(here, matrices[1])
    after = from_following(following)
    for i, matrices in enumerate((solve, solve_partner)):
        totals[i] += apply(after, matrices[2])


def centre_body(middle, solve, solve_partner, coarse, copies):
    full = from_four(middle)
    results = [
        (apply(full, matrix[...]) - coarse[i]).astype(BF16)
        for i, matrix in enumerate((solve, solve_partner))
    ]
    spread(copies, *results)


def onward_body(odd, middle, lifts, lifts_partner, totals):
    fourth, full = from_eight(odd, 1), from_four(middle)
    for i, matrices in enumerate((lifts, lifts_partner)):
        both = apply(fourth, matrices[0]) + apply(full, matrices[1])
        totals[i] = both.astype(BF16)


def reduced_body(
    odd, middle, one, one_partner, two, two_partner, side, side_partner, totals
):
    second, full = from_eight(odd, 0), from_four(middle)
    for i, (begun, first, last) in enumerate(
        ((side, one, two), (side_partner, one_partner, two_partner))
    ):
        both = apply(second, first[...]) + apply(full, last[...])
        totals[i] = begun[...].astype(F32) - both


def odd_body(odd, one, one_partner, three, three_partner, following, totals):
    second, fourth, here = (from_eight(odd, i) for i in range(3))
    for i, matrices in enumerate((one, one_partner)):
        totals[0, i] = apply(second, matrices[0]) - apply(here, matrices[1])
    after = from_following(following)
    for i, matrices in enumerate((three, three_partner)):
        totals[1, i] = apply(fourth, matrices[0]) - apply(after, matrices[2])


def final_body(
    centre, one, one_partner, three, three_partner, odd, own, totals, before,
    kept, given,
):
    full = from_four(centre)
    mine = core()
    for i, (first, last, out) in enumerate(
        ((one, three, kept), (one_partner, three_partner, given))
    ):
        out[0] = (odd[0, i] - apply(full, first[...])).astype(BF16)
        out[1] = own[mine if i == 0 else 1 - mine]
        out[2] = (odd[1, i] - apply(full, last[...])).astype(BF16)
        out[3] = (totals[i] - before[i].astype(F32)).astype(BF16)


def place_body(taken, coarse, kept, solved, reduced):
    mine = core()
    solved[0] = coarse[...]
    for i in range(3):
        solved[i + 1, mine] = kept[i]
        solved[i + 1, 1 - mine] = taken[1 - mine, i]
    reduced[0, mine] = kept[3]
    reduced[0, 1 - mine] = taken[1 - mine, 3]


def steps(right_sides, coarse_solution, lift_one, solve_one, lift_two, solve_two):
    sides = right_sides.reshape(4, 2, HALF, WIDTH)
    coarse = coarse_solution.reshape(1, 2, HALF, WIDTH)
    packed = pack(sides, coarse)
    odd = lax.all_to_all(packed, "col", 0, 0)
    lifts = jnp.stack([lift_one[0, 0], lift_two[0, 0]])
    lifts_next = passed_along(lifts, -1)
    one_partner = from_partner(lift_one)
    sides_partner = from_partner(sides)
    solve_two_partner = from_partner(solve_two)
    solve_one_partner = from_partner(solve_one)
    two_partner = from_partner(lift_two)
    following = passed_along(odd[:, 2], -1)
    lifts_partner = from_partner(lifts_next)

    (middle_copies,) = call(
        middle_body,
        [COPIES],
        [odd],
        [
            Part(lift_one, (1,)),
            Part(one_partner, (1,)),
            Part(sides, (2, core)),
            Part(sides_partner, (2, core)),
        ],
        products=2,
    )
    middle = over_chips(middle_copies)
    (coarse_totals,) = call(
        coarse_body,
        [TOTALS],
        [odd],
        [Part(solve_two, (0,)), Part(solve_two_partner, (0,)), Part(following)],
        products=2,
    )
    (odd_totals,) = call(
        odd_body,
        [((2, 2, HALF, WIDTH), F32)],
        [odd],
        [
            Part(solve_one, (0,)),
            Part(solve_one_partner, (0,)),
            Part(solve_one, (1,)),
            Part(solve_one_partner, (1,)),
            Part(following),
        ],
        products=4,
    )
    (centre_copies,) = call(
        centre_body,
        [COPIES],
        [middle],
        [
            Part(solve_two, (0, 0)),
            Part(solve_two_partner, (0, 0)),
            Part(coarse_totals),
        ],
    )
    centre = over_chips(centre_copies)
    (onward,) = call(
        onward_body,
        [PAIR],
        [odd, middle],
        [Part(lifts_next), Part(lifts_partner)],
        products=2,
    )
    before = passed_along(onward, 1)
    (totals,) = call(
        reduced_body,
        [TOTALS],
        [odd, middle],
        [
            Part(lift_one, (0, 1)),
            Part(one_partner, (0, 1)),
            Part(lift_two, (0, 1)),
            Part(two_partner, (0, 1)),
            Part(sides, (0, core)),
            Part(sides_partner, (0, core)),
        ],
        products=2,
    )
    quads = ((4, HALF, WIDTH), BF16)
    kept, given = call(
        final_body,
        [quads, quads],
        [centre],
        [
            Part(solve_one, (0, 2)),
            Part(solve_one_partner, (0, 2)),
            Part(solve_one, (1, 1)),
            Part(solve_one_partner, (1, 1)),
            Part(odd_totals),
            Part(centre_copies, (0,)),
            Part(totals),
            Part(before),
        ],
        products=2,
    )
    cores = [[i, i + 1] for i in range(0, lax.axis_size("col"), 2)]
    taken = lax.all_gather(given, "col", axis=0, axis_index_groups=cores)
    solved, reduced = call(
        place_body,
        [((4, 2, HALF, WIDTH), BF16), ((1, 2, HALF, WIDTH), BF16)],
        [taken],
        [Part(coarse, (0,)), Part(kept)],
    )
    return solved.reshape(4, ROWS, WIDTH), reduced.reshape(1, ROWS, WIDTH)


def solution(mesh):
    return jax.shard_map(
        steps,
        mesh=mesh,
        in_specs=(
            P("rad", None, "col"),
            P("rad", None, "col"),
            P("rad", None, "col", None),
            P("rad", None, "col", None),
            P("rad", None, "col", None),
            P("rad", None, "col", None),
        ),
        out_specs=(P("rad", None, "col"), P("rad", None, "col")),
        check_vma=False,
    )
```

time: 89.2 us -> 81.5 us (0.914)
  waiting for transfers between devices: 20.9 us -> 10.1 us
  Pallas kernels: 19.3 us -> 24.9 us
  local copies, waits for them, and re-layouts: 8.91 us -> 3.49 us
  blocking collectives: 0 us -> 3.24 us
    ppermute x3, waiting for transfers between devices: 15.2 us -> 4.4 us  [passed_along(): return lax.ppermute(array, 'rad', pairs)]
    all_to_all x1, starting transfers between devices: 4.11 us -> 10.4 us  [steps(): odd = lax.all_to_all(packed, 'col', 0, 0)]
    ppermute x6, starting transfers between devices: 20.4 us -> 14.4 us  [from_partner(): return lax.ppermute(array, 'col', [(i, i ^ 1) for i in range(peers)])]
    pallas_call x8, Pallas kernels: 17.2 us -> 22.7 us  [call(): pl.pallas_call(kernel, out_shape=[space(shape, dtype) for shape, dtype in...]
    unnamed x32 -> x6, local copies, waits for them, and re-layouts: 5.16 us -> 0.78 us
    all_gather x0 -> x1, blocking collectives: none -> 3.24 us  [steps(): taken = lax.all_gather(given, 'col', axis=0, axis_index_groups=cores)]
    all_to_all x2, waiting for transfers between devices: 0.01 us -> 2.19 us  [over_chips(): return lax.all_to_all(copies, 'col', 0, 0, axis_index_groups=groups)]
    all_to_all x1, waiting for transfers between devices: 4.6 us -> 3.45 us  [steps(): odd = lax.all_to_all(packed, 'col', 0, 0)]
  transfers between devices with their start and end apart: 12 -> 12, of which waited for: 3 -> 3; matrix products, arithmetic and copies ran while one was open for 5% -> 4% of each run, Pallas kernels for 19% -> 22%
where the time goes in v3:
time: 81.5 us; the launch traced here: 80.7 us
  starting transfers between devices  37.3 us (46%)
  Pallas kernels  24.9 us (31%)
  waiting for transfers between devices  10.1 us (12%)
  local copies, waits for them, and re-layouts  3.49 us (4%)
  blocking collectives  3.24 us (4%)
  other arithmetic  0.88 us (1%)
  between operations  0.86 us (1%)
    pallas_call x8, Pallas kernels, call(): pl.pallas_call(kernel, out_shape=[space(shape, dtype) for shape, dtype in...  22.7 us
    ppermute x6, starting transfers between devices, from_partner(): return lax.ppermute(array, 'col', [(i, i ^ 1) for i in range(peers)])  14.4 us
    all_to_all x1, starting transfers between devices, steps(): odd = lax.all_to_all(packed, 'col', 0, 0)  10.4 us
    all_to_all x2, starting transfers between devices, over_chips(): return lax.all_to_all(copies, 'col', 0, 0, axis_index_groups=groups)  7.89 us
    ppermute x3, starting transfers between devices, passed_along(): return lax.ppermute(array, 'rad', pairs)  4.49 us
    ppermute x3, waiting for transfers between devices, passed_along(): return lax.ppermute(array, 'rad', pairs)  4.4 us
    all_to_all x1, waiting for transfers between devices, steps(): odd = lax.all_to_all(packed, 'col', 0, 0)  3.45 us
    all_gather x1, blocking collectives, steps(): taken = lax.all_gather(given, 'col', axis=0, axis_index_groups=cores)  3.24 us
  transfers between devices with their start and end apart: 12, of which 3 were waited for; matrix products, arithmetic and copies ran while one was open for 4% of the time, Pallas kernels for 22%

profile of v3, /device:TPU:1, one launch (start us, length us, event | category | flops | bytes accessed | tf_op | source)
XLA Modules:
  0.0 80.7 jit_solution(1414750092982721635)
XLA Ops:
  0.6 2.2 %shard_map.77 = bf16[8,3,192,128]{3,2,1,0:T(8,128)(2,1)} custom-call(bf16[4,2,192,128]{3,2,1,0:T(8,128)(2,1)} %bitcast.12, bf16[1,2,192,128]{3,2,1,0:T(8,128)(2,1)} %bitcast.16), custom_call_target="tpu_custom_call" | custom-call | tf_op jit(solution)/shard_map/pallas_call | solution.py:135
  2.8 0.0 copy-start
  2.8 10.4 %all-to-all-start = ((bf16[8,3,192,128]{3,2,1,0:T(8,128)(2,1)}), bf16[8,3,192,128]{3,2,1,0:T(8,128)(2,1)S(1)}, u32[]{:S(2)}, u32[]{:S(2)}) async-start(bf16[8,3,192,128]{3,2,1,0:T(8,128)(2,1)} %shard_map.77), calls=%async_computation | async-start | bytes 2359296 | tf_op jit(solution)/shard_map/all_to_all | solution.py:246
  13.3 0.0 copy-start.1
  13.3 2.2 %collective-permute-start = (bf16[2,2,128,1024]{3,2,1,0:T(8,128)(2,1)}, bf16[2,2,128,1024]{3,2,1,0:T(8,128)(2,1)}, u32[]{:S(2)}, u32[]{:S(2)}) collective-permute-start(bf16[2,2,128,1024]{3,2,1,0:T(8,128)(2,1)} %refs_2_.1), channel_id=1, source_target_pairs={{0,1},{1,0},{2,3},{3,2},{4,5},{5,4},{6,7},{7,6},{8,9},{9,8},{10,11... | collective-permute-start | bytes 3145736 | tf_op jit(solution)/shard_map/ppermute | solution.py:29
  15.4 0.0 copy-done
  15.4 2.3 %collective-permute-start.4 = (bf16[2,3,128,1024]{3,2,1,0:T(8,128)(2,1)S(1)}, bf16[2,3,128,1024]{3,2,1,0:T(8,128)(2,1)}, u32[]{:S(2)}, u32[]{:S(2)}) collective-permute-start(bf16[2,3,128,1024]{3,2,1,0:T(8,128)(2,1)S(1)} %copy-done), channel_id=1, source_target_pairs={{0,1},{1,0},{2,3},{3,2},{4,5},{5,4},{6,7},{7,6},{8,9},{9,8},{10,11... | collective-permute-start | bytes 4718600 | tf_op jit(solution)/shard_map/ppermute | solution.py:29
  17.7 1.0 %slice_bitcast_fusion.2 = bf16[1,128,1024]{2,1,0:T(8,128)(2,1)S(1)} fusion(bf16[2,2,128,1024]{3,2,1,0:T(8,128)(2,1)} %refs_2_.1), kind=kLoop, calls=%fused_computation.3 | loop fusion | bytes 524288 | tf_op jit(solution)/shard_map/stack;squeeze | solution.py:247
  18.7 1.0 %slice_bitcast_fusion.1 = bf16[1,128,1024]{2,1,0:T(8,128)(2,1)S(1)} fusion(bf16[1,2,128,1024]{3,2,1,0:T(8,128)(2,1)} %refs_4_.1), kind=kLoop, calls=%fused_computation.2 | loop fusion | bytes 524288 | tf_op jit(solution)/shard_map/stack;squeeze | solution.py:247
  19.7 0.9 %pad_maximum_fusion = bf16[2,128,1024]{2,1,0:T(8,128)(2,1)} fusion(bf16[1,128,1024]{2,1,0:T(8,128)(2,1)S(1)} %slice_bitcast_fusion.1, bf16[1,128,1024]{2,1,0:T(8,128)(2,1)S(1)} %slice_bitcast_fusion.2), kind=kLoop, calls=%fused_computation | loop fusion | flops 262144 | bytes 1048576 | tf_op jit(solution)/shard_map/stack | solution.py:247
  20.6 1.3 %collective-permute-start.6 = (bf16[2,128,1024]{2,1,0:T(8,128)(2,1)}, bf16[2,128,1024]{2,1,0:T(8,128)(2,1)}, u32[]{:S(2)}, u32[]{:S(2)}) collective-permute-start(bf16[2,128,1024]{2,1,0:T(8,128)(2,1)} %pad_maximum_fusion), channel_id=1, source_target_pairs={{8,0},{16,8},{24,16},{32,24},{40,32},{48,40},{56,48},{64,56},{72,6... | collective-permute-start | bytes 1572872 | tf_op jit(solution)/shard_map/ppermute | solution.py:35
  21.9 0.0 copy-done.1
  21.9 2.0 %collective-permute-start.1 = (bf16[4,2,192,128]{3,2,1,0:T(8,128)(2,1)S(1)}, bf16[4,2,192,128]{3,2,1,0:T(8,128)(2,1)}, u32[]{:S(2)}, u32[]{:S(2)}) collective-permute-start(bf16[4,2,192,128]{3,2,1,0:T(8,128)(2,1)S(1)} %bitcast.15), channel_id=1, source_target_pairs={{0,1},{1,0},{2,3},{3,2},{4,5},{5,4},{6,7},{7,6},{8,9},{9,8},{10,11... | collective-permute-start | bytes 1179656 | tf_op jit(solution)/shard_map/ppermute | solution.py:29
  23.9 2.3 %collective-permute-start.2 = (bf16[1,3,128,1024]{3,2,1,0:T(8,128)(2,1)}, bf16[1,3,128,1024]{3,2,1,0:T(8,128)(2,1)}, u32[]{:S(2)}, u32[]{:S(2)}) collective-permute-start(bf16[1,3,128,1024]{3,2,1,0:T(8,128)(2,1)} %refs_1_.7), channel_id=1, source_target_pairs={{0,1},{1,0},{2,3},{3,2},{4,5},{5,4},{6,7},{7,6},{8,9},{9,8},{10,11... | collective-permute-start | bytes 2359304 | tf_op jit(solution)/shard_map/ppermute | solution.py:29
  26.2 3.5 %all-to-all-done.refs_0_ = bf16[8,3,192,128]{3,2,1,0:T(8,128)(2,1)S(1)} async-done(((bf16[8,3,192,128]{3,2,1,0:T(8,128)(2,1)}), bf16[8,3,192,128]{3,2,1,0:T(8,128)(2,1)S(1)}, u32[]{:S(2)}, u32[]{:S(2)}) %all-to-all-start) | async-done | bytes 1179680 | tf_op jit(solution)/shard_map/all_to_all | solution.py:246
  29.7 0.8 slice_bitcast_fusion
  30.4 0.0 collective-permute-done.1.refs_4_.refs_7_
  30.4 1.3 %collective-permute-start.3 = (bf16[8,192,128]{2,1,0:T(8,128)(2,1)}, bf16[8,192,128]{2,1,0:T(8,128)(2,1)S(1)}, u32[]{:S(2)}, u32[]{:S(2)}) collective-permute-start(bf16[8,192,128]{2,1,0:T(8,128)(2,1)} %slice_bitcast_fusion), channel_id=1, source_target_pairs={{8,0},{16,8},{24,16},{32,24},{40,32},{48,40},{56,48},{64,56},{72,6... | collective-permute-start | bytes 1179656 | tf_op jit(solution)/shard_map/ppermute | solution.py:35
  31.7 4.4 %collective-permute-done.6.refs_2_ = bf16[2,128,1024]{2,1,0:T(8,128)(2,1)} collective-permute-done((bf16[2,128,1024]{2,1,0:T(8,128)(2,1)}, bf16[2,128,1024]{2,1,0:T(8,128)(2,1)}, u32[]{:S(2)}, u32[]{:S(2)}) %collective-permute-start.6) | collective-permute-done | bytes 524320 | tf_op jit(solution)/shard_map/ppermute | solution.py:35
  36.1 3.5 %collective-permute-start.7 = (bf16[2,128,1024]{2,1,0:T(8,128)(2,1)}, bf16[2,128,1024]{2,1,0:T(8,128)(2,1)}, u32[]{:S(2)}, u32[]{:S(2)}) collective-permute-start(bf16[2,128,1024]{2,1,0:T(8,128)(2,1)} %collective-permute-done.6.refs_2_), channel_id=1, source_target_pairs={{0,1},{1,0},{2,3},{3,2},{4,5},{5,4},{6,7},{7,6},{8,9},{9,8},{10,11... | collective-permute-start | bytes 1572872 | tf_op jit(solution)/shard_map/ppermute | solution.py:29
  39.6 0.0 collective-permute-done.refs_2_.refs_3_
  39.6 3.0 %shard_map.78 = bf16[4,2,192,128]{3,2,1,0:T(8,128)(2,1)} custom-call(bf16[8,3,192,128]{3,2,1,0:T(8,128)(2,1)S(1)} %all-to-all-done.refs_0_, bf16[2,2,128,1024]{3,2,1,0:T(8,128)(2,1)} %refs_2_.1, bf16[2,2,128,1024]{3,2,1,0:T(8,128)(2,1)} %collective-permute-done.refs_2_.refs_3_, bf16[4,2,192,128]{3,2,1,0:T(8,128)(2,1)} %bitcast.13, ...), custom_call_target="tpu_custom_call" | custom-call | flops 201326592 | bytes 2000000 | tf_op jit(solution)/shard_map/pallas_call | solution.py:79
  42.6 4.4 %all-to-all-start.1 = ((bf16[4,2,192,128]{3,2,1,0:T(8,128)(2,1)}), bf16[4,2,192,128]{3,2,1,0:T(8,128)(2,1)S(1)}, u32[]{:S(2)}, u32[]{:S(2)}) async-start(bf16[4,2,192,128]{3,2,1,0:T(8,128)(2,1)} %shard_map.78), calls=%async_computation.1 | async-start | bytes 786432 | tf_op jit(solution)/shard_map/all_to_all | solution.py:24
  47.0 2.2 %collective-permute-start.5 = (bf16[1,2,128,1024]{3,2,1,0:T(8,128)(2,1)}, bf16[1,2,128,1024]{3,2,1,0:T(8,128)(2,1)}, u32[]{:S(2)}, u32[]{:S(2)}) collective-permute-start(bf16[1,2,128,1024]{3,2,1,0:T(8,128)(2,1)} %refs_4_.1), channel_id=1, source_target_pairs={{0,1},{1,0},{2,3},{3,2},{4,5},{5,4},{6,7},{7,6},{8,9},{9,8},{10,11... | collective-permute-start | bytes 1572872 | tf_op jit(solution)/shard_map/ppermute | solution.py:29
  49.2 0.0 collective-permute-done.2.refs_2_
  49.2 0.0 collective-permute-done.3.refs_3_.refs_5_
  49.2 0.0 copy-start.2
  49.3 0.8 copy-done.2
  50.0 2.7 %shard_map.79.refs_3_ = f32[2,192,128]{2,1,0:T(8,128)} custom-call(bf16[8,3,192,128]{3,2,1,0:T(8,128)(2,1)S(1)} %all-to-all-done.refs_0_, bf16[1,3,128,1024]{3,2,1,0:T(8,128)(2,1)} %refs_1_.7, bf16[1,3,128,1024]{3,2,1,0:T(8,128)(2,1)} %collective-permute-done.2.refs_2_, bf16[8,192,128]{2,1,0:T(8,128)(2,1)} %copy-done.2), custom_call_target="tpu_custom_call" | custom-call | flops 201326592 | bytes 2000000 | tf_op jit(solution)/shard_map/pallas_call | solution.py:79
  52.7 2.2 %all-to-all-done.1.refs_0_.refs_1_ = bf16[4,2,192,128]{3,2,1,0:T(8,128)(2,1)S(1)} async-done(((bf16[4,2,192,128]{3,2,1,0:T(8,128)(2,1)}), bf16[4,2,192,128]{3,2,1,0:T(8,128)(2,1)S(1)}, u32[]{:S(2)}, u32[]{:S(2)}) %all-to-all-start.1) | async-done | bytes 393248 | tf_op jit(solution)/shard_map/all_to_all | solution.py:24
  54.9 2.4 %shard_map.80.refs_6_ = bf16[4,2,192,128]{3,2,1,0:T(8,128)(2,1)} custom-call(bf16[4,2,192,128]{3,2,1,0:T(8,128)(2,1)S(1)} %all-to-all-done.1.refs_0_.refs_1_, bf16[1,3,128,1024]{3,2,1,0:T(8,128)(2,1)} %refs_1_.7, bf16[1,3,128,1024]{3,2,1,0:T(8,128)(2,1)} %collective-permute-done.2.refs_2_, f32[2,192,128]{2,1,0:T(8,128)} %shard_map.79.refs_3_), custom_call_target="tpu_custom_call" | custom-call | flops 100663296 | bytes 1000000 | tf_op jit(solution)/shard_map/pallas_call | solution.py:79
  57.3 3.5 %all-to-all-start.2 = ((bf16[4,2,192,128]{3,2,1,0:T(8,128)(2,1)}), bf16[4,2,192,128]{3,2,1,0:T(8,128)(2,1)S(1)}, u32[]{:S(2)}, u32[]{:S(2)}) async-start(bf16[4,2,192,128]{3,2,1,0:T(8,128)(2,1)} %shard_map.80.refs_6_), calls=%async_computation.2 | async-start | bytes 786432 | tf_op jit(solution)/shard_map/all_to_all | solution.py:24
  60.8 0.0 collective-permute-done.7.refs_3_
  60.8 2.8 %shard_map.83 = bf16[2,192,128]{2,1,0:T(8,128)(2,1)} custom-call(bf16[8,3,192,128]{3,2,1,0:T(8,128)(2,1)S(1)} %all-to-all-done.refs_0_, bf16[4,2,192,128]{3,2,1,0:T(8,128)(2,1)S(1)} %all-to-all-done.1.refs_0_.refs_1_, bf16[2,128,1024]{2,1,0:T(8,128)(2,1)} %collective-permute-done.6.refs_2_, bf16[2,128,1024]{2,1,0:T(8,128)(2,1)} %collective-permute-done.7.refs_3_), custom_call_target="tpu_custom_call" | custom-call | flops 201326592 | bytes 2000000 | tf_op jit(solution)/shard_map/pallas_call | solution.py:79
  63.6 1.9 %collective-permute-start.8 = (bf16[2,192,128]{2,1,0:T(8,128)(2,1)}, bf16[2,192,128]{2,1,0:T(8,128)(2,1)}, u32[]{:S(2)}, u32[]{:S(2)}) collective-permute-start(bf16[2,192,128]{2,1,0:T(8,128)(2,1)} %shard_map.83), channel_id=1, source_target_pairs={{0,8},{8,16},{16,24},{24,32},{32,40},{40,48},{48,56},{56,64},{64,7... | collective-permute-start | bytes 294920 | tf_op jit(solution)/shard_map/ppermute | solution.py:35
  65.6 0.0 collective-permute-done.5.refs_5_
  65.6 3.0 %shard_map.82.refs_7_ = f32[2,192,128]{2,1,0:T(8,128)} custom-call(bf16[8,3,192,128]{3,2,1,0:T(8,128)(2,1)S(1)} %all-to-all-done.refs_0_, bf16[4,2,192,128]{3,2,1,0:T(8,128)(2,1)S(1)} %all-to-all-done.1.refs_0_.refs_1_, bf16[2,2,128,1024]{3,2,1,0:T(8,128)(2,1)} %refs_2_.1, bf16[2,2,128,1024]{3,2,1,0:T(8,128)(2,1)} %collective-permute-done.refs_2_.refs_3_, ...), custom_call_target="tpu_custom_call" | custom-call | flops 201326592 | bytes 2000000 | tf_op jit(solution)/shard_map/pallas_call | solution.py:79
  68.6 0.0 collective-permute-done.4.refs_2_.refs_4_
  68.6 3.5 %shard_map.81.refs_5_ = f32[2,2,192,128]{3,2,1,0:T(8,128)} custom-call(bf16[8,3,192,128]{3,2,1,0:T(8,128)(2,1)S(1)} %all-to-all-done.refs_0_, bf16[2,3,128,1024]{3,2,1,0:T(8,128)(2,1)} %refs_3_.3, bf16[2,3,128,1024]{3,2,1,0:T(8,128)(2,1)} %collective-permute-done.4.refs_2_.refs_4_, bf16[2,3,128,1024]{3,2,1,0:T(8,128)(2,1)} %refs_3_.3, ...), custom_call_target="tpu_custom_call" | custom-call | flops 402653184 | bytes 4000000 | tf_op jit(solution)/shard_map/pallas_call | solution.py:79
  72.1 0.0 collective-permute-done.8.refs_8_
  72.1 0.0 all-to-all-done.2.refs_0_
  72.1 3.5 %shard_map.84 = (bf16[4,192,128]{2,1,0:T(8,128)(2,1)}, bf16[4,192,128]{2,1,0:T(8,128)(2,1)}) custom-call(bf16[4,2,192,128]{3,2,1,0:T(8,128)(2,1)S(1)} %all-to-all-done.2.refs_0_, bf16[2,3,128,1024]{3,2,1,0:T(8,128)(2,1)} %refs_3_.3, bf16[2,3,128,1024]{3,2,1,0:T(8,128)(2,1)} %collective-permute-done.4.refs_2_.refs_4_, bf16[2,3,128,1024]{3,2,1,0:T(8,128)(2,1)} %refs_3_.3, ...), custom_call_target="tpu_custom_call" | custom-call | flops 201326592 | bytes 2000000 | tf_op jit(solution)/shard_map/pallas_call | solution.py:79
  75.7 3.2 %all-gather = bf16[8,192,128]{2,1,0:T(8,128)(2,1)S(1)} all-gather(bf16[4,192,128]{2,1,0:T(8,128)(2,1)} %get-tuple-element.6), channel_id=2, replica_groups={{0,1},{2,3},{4,5},{6,7},{8,9},{10,11},{12,13},{14,15},{16,17},{18,19},{..., dimensions={0}, use_global_device_ids=true | all-gather | bytes 589824 | tf_op jit(solution)/shard_map/all_gather | solution.py:341
  78.9 1.8 %shard_map.85 = (bf16[4,2,192,128]{3,2,1,0:T(8,128)(2,1)}, bf16[1,2,192,128]{3,2,1,0:T(8,128)(2,1)}) custom-call(bf16[2,4,192,128]{3,2,1,0:T(8,128)(2,1)S(1)} %bitcast.11, bf16[1,2,192,128]{3,2,1,0:T(8,128)(2,1)} %bitcast.17, bf16[4,192,128]{2,1,0:T(8,128)(2,1)} %get-tuple-element.7.refs_2_), custom_call_target="tpu_custom_call" | custom-call | flops 100663296 | bytes 1000000 | tf_op jit(solution)/shard_map/pallas_call | solution.py:79
Async XLA Ops:
  2.8 12.6 %copy-start = (bf16[2,3,128,1024]{3,2,1,0:T(8,128)(2,1)S(1)}, bf16[2,3,128,1024]{3,2,1,0:T(8,128)(2,1)}, u32[]{:S(2)}) copy-start(bf16[2,3,128,1024]{3,2,1,0:T(8,128)(2,1)} %refs_3_.3) | copy-start | bytes 4718596
  2.8 26.8 %all-to-all-start = ((bf16[8,3,192,128]{3,2,1,0:T(8,128)(2,1)}), bf16[8,3,192,128]{3,2,1,0:T(8,128)(2,1)S(1)}, u32[]{:S(2)}, u32[]{:S(2)}) async-start(bf16[8,3,192,128]{3,2,1,0:T(8,128)(2,1)} %shard_map.77), calls=%async_computation | async-start | bytes 2359296 | tf_op jit(solution)/shard_map/all_to_all | solution.py:246
  13.3 8.6 %copy-start.1 = (bf16[4,384,128]{2,1,0:T(8,128)(2,1)S(1)}, bf16[4,384,128]{2,1,0:T(8,128)(2,1)}, u32[]{:S(2)}) copy-start(bf16[4,384,128]{2,1,0:T(8,128)(2,1)} %param.6) | copy-start | bytes 1179652
  13.3 26.3 %collective-permute-start = (bf16[2,2,128,1024]{3,2,1,0:T(8,128)(2,1)}, bf16[2,2,128,1024]{3,2,1,0:T(8,128)(2,1)}, u32[]{:S(2)}, u32[]{:S(2)}) collective-permute-start(bf16[2,2,128,1024]{3,2,1,0:T(8,128)(2,1)} %refs_2_.1), channel_id=1, source_target_pairs={{0,1},{1,0},{2,3},{3,2},{4,5},{5,4},{6,7},{7,6},{8,9},{9,8},{10,11... | collective-permute-start | bytes 3145736 | tf_op jit(solution)/shard_map/ppermute | solution.py:29
  15.4 53.1 %collective-permute-start.4 = (bf16[2,3,128,1024]{3,2,1,0:T(8,128)(2,1)S(1)}, bf16[2,3,128,1024]{3,2,1,0:T(8,128)(2,1)}, u32[]{:S(2)}, u32[]{:S(2)}) collective-permute-start(bf16[2,3,128,1024]{3,2,1,0:T(8,128)(2,1)S(1)} %copy-done), channel_id=1, source_target_pairs={{0,1},{1,0},{2,3},{3,2},{4,5},{5,4},{6,7},{7,6},{8,9},{9,8},{10,11... | collective-permute-start | bytes 4718600 | tf_op jit(solution)/shard_map/ppermute | solution.py:29
  20.6 15.6 %collective-permute-start.6 = (bf16[2,128,1024]{2,1,0:T(8,128)(2,1)}, bf16[2,128,1024]{2,1,0:T(8,128)(2,1)}, u32[]{:S(2)}, u32[]{:S(2)}) collective-permute-start(bf16[2,128,1024]{2,1,0:T(8,128)(2,1)} %pad_maximum_fusion), channel_id=1, source_target_pairs={{8,0},{16,8},{24,16},{32,24},{40,32},{48,40},{56,48},{64,56},{72,6... | collective-permute-start | bytes 1572872 | tf_op jit(solution)/shard_map/ppermute | solution.py:35
  21.9 8.6 %collective-permute-start.1 = (bf16[4,2,192,128]{3,2,1,0:T(8,128)(2,1)S(1)}, bf16[4,2,192,128]{3,2,1,0:T(8,128)(2,1)}, u32[]{:S(2)}, u32[]{:S(2)}) collective-permute-start(bf16[4,2,192,128]{3,2,1,0:T(8,128)(2,1)S(1)} %bitcast.15), channel_id=1, source_target_pairs={{0,1},{1,0},{2,3},{3,2},{4,5},{5,4},{6,7},{7,6},{8,9},{9,8},{10,11... | collective-permute-start | bytes 1179656 | tf_op jit(solution)/shard_map/ppermute | solution.py:29
  23.9 25.3 %collective-permute-start.2 = (bf16[1,3,128,1024]{3,2,1,0:T(8,128)(2,1)}, bf16[1,3,128,1024]{3,2,1,0:T(8,128)(2,1)}, u32[]{:S(2)}, u32[]{:S(2)}) collective-permute-start(bf16[1,3,128,1024]{3,2,1,0:T(8,128)(2,1)} %refs_1_.7), channel_id=1, source_target_pairs={{0,1},{1,0},{2,3},{3,2},{4,5},{5,4},{6,7},{7,6},{8,9},{9,8},{10,11... | collective-permute-start | bytes 2359304 | tf_op jit(solution)/shard_map/ppermute | solution.py:29
  30.4 18.8 %collective-permute-start.3 = (bf16[8,192,128]{2,1,0:T(8,128)(2,1)}, bf16[8,192,128]{2,1,0:T(8,128)(2,1)S(1)}, u32[]{:S(2)}, u32[]{:S(2)}) collective-permute-start(bf16[8,192,128]{2,1,0:T(8,128)(2,1)} %slice_bitcast_fusion), channel_id=1, source_target_pairs={{8,0},{16,8},{24,16},{32,24},{40,32},{48,40},{56,48},{64,56},{72,6... | collective-permute-start | bytes 1179656 | tf_op jit(solution)/shard_map/ppermute | solution.py:35
  36.1 24.7 %collective-permute-start.7 = (bf16[2,128,1024]{2,1,0:T(8,128)(2,1)}, bf16[2,128,1024]{2,1,0:T(8,128)(2,1)}, u32[]{:S(2)}, u32[]{:S(2)}) collective-permute-start(bf16[2,128,1024]{2,1,0:T(8,128)(2,1)} %collective-permute-done.6.refs_2_), channel_id=1, source_target_pairs={{0,1},{1,0},{2,3},{3,2},{4,5},{5,4},{6,7},{7,6},{8,9},{9,8},{10,11... | collective-permute-start | bytes 1572872 | tf_op jit(solution)/shard_map/ppermute | solution.py:29
  42.6 12.3 %all-to-all-start.1 = ((bf16[4,2,192,128]{3,2,1,0:T(8,128)(2,1)}), bf16[4,2,192,128]{3,2,1,0:T(8,128)(2,1)S(1)}, u32[]{:S(2)}, u32[]{:S(2)}) async-start(bf16[4,2,192,128]{3,2,1,0:T(8,128)(2,1)} %shard_map.78), calls=%async_computation.1 | async-start | bytes 786432 | tf_op jit(solution)/shard_map/all_to_all | solution.py:24
  47.0 18.6 %collective-permute-start.5 = (bf16[1,2,128,1024]{3,2,1,0:T(8,128)(2,1)}, bf16[1,2,128,1024]{3,2,1,0:T(8,128)(2,1)}, u32[]{:S(2)}, u32[]{:S(2)}) collective-permute-start(bf16[1,2,128,1024]{3,2,1,0:T(8,128)(2,1)} %refs_4_.1), channel_id=1, source_target_pairs={{0,1},{1,0},{2,3},{3,2},{4,5},{5,4},{6,7},{7,6},{8,9},{9,8},{10,11... | collective-permute-start | bytes 1572872 | tf_op jit(solution)/shard_map/ppermute | solution.py:29
  49.2 0.8 copy-start.2
  57.3 14.8 %all-to-all-start.2 = ((bf16[4,2,192,128]{3,2,1,0:T(8,128)(2,1)}), bf16[4,2,192,128]{3,2,1,0:T(8,128)(2,1)S(1)}, u32[]{:S(2)}, u32[]{:S(2)}) async-start(bf16[4,2,192,128]{3,2,1,0:T(8,128)(2,1)} %shard_map.80.refs_6_), calls=%async_computation.2 | async-start | bytes 786432 | tf_op jit(solution)/shard_map/all_to_all | solution.py:24
  63.6 8.5 %collective-permute-start.8 = (bf16[2,192,128]{2,1,0:T(8,128)(2,1)}, bf16[2,192,128]{2,1,0:T(8,128)(2,1)}, u32[]{:S(2)}, u32[]{:S(2)}) collective-permute-start(bf16[2,192,128]{2,1,0:T(8,128)(2,1)} %shard_map.83), channel_id=1, source_target_pairs={{0,8},{8,16},{16,24},{24,32},{32,40},{40,48},{48,56},{56,64},{64,7... | collective-permute-start | bytes 294920 | tf_op jit(solution)/shard_map/ppermute | solution.py:35

commit v4 on v3

v4 whole, which is shorter than its diff:
```python
import jax
import jax.numpy as jnp
from jax import lax
from jax.experimental import pallas as pl
from jax.experimental.pallas import tpu as pltpu
from jax.sharding import PartitionSpec as P


ANY = pl.BlockSpec(memory_space=pl.ANY)
ROWS = 384
HALF = 192
WIDTH = 128
BF16 = jnp.bfloat16
F32 = jnp.float32
VMEM = pl.BlockSpec(memory_space=pltpu.VMEM)
HBM = pl.BlockSpec(memory_space=pltpu.HBM)


def chips_of(peers):
    return [[i for i in range(peers) if i % 2 == core] for core in range(2)]


def over_chips(copies):
    groups = chips_of(lax.axis_size("col"))
    return lax.all_to_all(copies, "col", 0, 0, axis_index_groups=groups)


def from_partner(array):
    peers = lax.axis_size("col")
    return lax.ppermute(array, "col", [(i, i ^ 1) for i in range(peers)])


def passed_along(array, by):
    peers = lax.axis_size("rad")
    pairs = [(i, i + by) for i in range(peers) if 0 <= i + by < peers]
    return lax.ppermute(array, "rad", pairs)


def apply(vector, matrix):
    return lax.dot_general(
        vector, matrix, (((1,), (1,)), ((), ())), preferred_element_type=F32
    )


def core():
    return lax.rem(lax.axis_index("col"), 2)


class Pieces:
    def __init__(self, sems):
        self.sems, self.copies = sems, []

    def load(self, source, held):
        sem = self.sems.at[len(self.copies)]
        copy = pltpu.make_async_copy(source, held, sem)
        copy.start()
        self.copies.append(copy)
        return copy

    def both(self, own, partner, held):
        return (
            self.load(own, held.at[pl.ds(0, WIDTH)]),
            self.load(partner, held.at[pl.ds(WIDTH, WIDTH)]),
        )

    def wait(self):
        for copy in self.copies:
            copy.wait()


def call(body, outs, whole, parts=(), scratch=(), copies=0, products=1, free=()):
    return pl.pallas_call(
        body,
        out_shape=[space(shape, dtype) for space, shape, dtype in outs],
        in_specs=[VMEM] * len(whole)
        + [HBM] * len(parts)
        + [ANY] * len(free),
        out_specs=[VMEM] * len(outs),
        scratch_shapes=[pltpu.VMEM(*one) for one in scratch]
        + [pltpu.SemaphoreType.DMA((max(copies, 1),))],
        compiler_params=pltpu.CompilerParams(vmem_limit_bytes=12 << 20),
        cost_estimate=pl.CostEstimate(
            flops=products * 2 * ROWS * 1024 * WIDTH,
            bytes_accessed=products * 1000000,
            transcendentals=0,
        ),
    )(
        *[pltpu.with_memory_space_constraint(x, pltpu.VMEM) for x in whole],
        *[pltpu.with_memory_space_constraint(x, pltpu.HBM) for x in parts],
        *free,
    )


IN_VMEM, IN_HBM = pltpu.VMEM, pltpu.HBM
PAIR = (2, HALF, WIDTH)
COPIES = (4, 2, HALF, WIDTH)
MERGED = (2 * WIDTH, 1024)


def from_eight(blocks, which):
    return jnp.concatenate([blocks[peer, which] for peer in range(8)], axis=1)


def from_four(blocks):
    return jnp.concatenate(
        [blocks[chip, side] for chip in range(4) for side in range(2)], axis=1
    )


def pack_body(sides, coarse, packed, held, arrived, sent):
    arrays = [sides.at[1], sides.at[3], coarse.at[0]]
    loads = [
        pltpu.make_async_copy(array, held.at[i], arrived.at[i])
        for i, array in enumerate(arrays)
    ]
    for load in loads:
        load.start()
    stores = []
    for i, load in enumerate(loads):
        load.wait()
        for peer in range(8):
            store = pltpu.make_async_copy(
                held.at[i, peer % 2], packed.at[peer, i], sent.at[i, peer]
            )
            store.start()
            stores.append(store)
    for store in stores:
        store.wait()


def pack(sides, coarse):
    return pl.pallas_call(
        pack_body,
        out_shape=pltpu.HBM((8, 3, HALF, WIDTH), BF16),
        in_specs=[HBM, HBM],
        out_specs=HBM,
        scratch_shapes=[
            pltpu.VMEM((3, 2, HALF, WIDTH), BF16),
            pltpu.SemaphoreType.DMA((3,)),
            pltpu.SemaphoreType.DMA((3, 8)),
        ],
        compiler_params=pltpu.CompilerParams(vmem_limit_bytes=4 << 20),
    )(
        pltpu.with_memory_space_constraint(sides, pltpu.HBM),
        pltpu.with_memory_space_constraint(coarse, pltpu.HBM),
    )


def from_following(following):
    return jnp.concatenate([following[peer] for peer in range(8)], axis=1)


def own_and_partner(total):
    return total[:, :WIDTH], total[:, WIDTH:]


def spread(copies, results):
    mine = core()
    for chip in range(4):
        copies[chip, mine] = results[0]
        copies[chip, 1 - mine] = results[1]


def lifts_body(one, two, out, sems):
    pieces = Pieces(sems)
    pieces.load(one.at[0, 0], out.at[0])
    pieces.load(two.at[0, 0], out.at[1])
    pieces.wait()


def prepare_body(one, one_partner, sides, sides_partner, matrices, begun, sems):
    pieces, mine = Pieces(sems), core()
    for i in range(2):
        pieces.both(one.at[1, i], one_partner.at[1, i], matrices.at[i])
    pieces.load(sides.at[2, mine], begun.at[0])
    pieces.load(sides_partner.at[2, mine], begun.at[1])
    pieces.wait()


def middle_body(odd, matrices, begun, copies, sems):
    total = apply(from_eight(odd, 0), matrices[0])
    total += apply(from_eight(odd, 1), matrices[1])
    spread(
        copies,
        [
            (begun[i].astype(F32) - part).astype(BF16)
            for i, part in enumerate(own_and_partner(total))
        ],
    )


def early_body(
    odd, one, one_partner, solve, solve_partner, last, last_partner,
    inverse, coarse, ends, lifted, held, sems,
):
    pieces = Pieces(sems)
    waits = [
        pieces.both(own.at[index], partner.at[index], held.at[i])
        for i, (own, partner, index) in enumerate(
            (
                (last, last_partner, (0, 1)),
                (solve, solve_partner, (0, 0)),
                (solve, solve_partner, (0, 1)),
                (solve, solve_partner, (1, 0)),
                (one, one_partner, (0, 1)),
            )
        )
    ]
    waits.append(pieces.both(last.at[0, 0], last_partner.at[0, 0], inverse))

    def product(vector, i):
        for copy in waits[i]:
            copy.wait()
        return apply(vector, held[i])

    second, fourth, here = (from_eight(odd, i) for i in range(3))
    coarse[...] = product(here, 0)
    ends[0] = product(second, 1) - product(here, 2)
    ends[1] = product(fourth, 3)
    lifted[...] = product(second, 4)
    for copy in waits[5]:
        copy.wait()


def late_body(
    odd, coarse, solve, solve_partner, last, last_partner, lifts, lifts_partner,
    following, totals, end, onward, held, arrived, sems,
):
    pieces = Pieces(sems)
    waits = [
        pieces.both(own.at[index], partner.at[index], held.at[i])
        for i, (own, partner, index) in enumerate(
            (
                (lifts, lifts_partner, (0,)),
                (last, last_partner, (0, 2)),
                (solve, solve_partner, (1, 2)),
            )
        )
    ]
    arrival = pieces.load(following, arrived)

    def product(vector, i):
        for copy in waits[i]:
            copy.wait()
        return apply(vector, held[i])

    onward[...] = product(from_eight(odd, 1), 0)
    arrival.wait()
    after = from_following(arrived)
    totals[...] = coarse[...] + product(after, 1)
    end[...] = product(after, 2)


def centre_body(middle, inverse, coarse, copies, sems):
    total = apply(from_four(middle), inverse[...]) - coarse[...]
    spread(copies, [part.astype(BF16) for part in own_and_partner(total)])


def onward_body(middle, begun, lifts, lifts_partner, totals, held, sems):
    pieces = Pieces(sems)
    pieces.both(lifts.at[1], lifts_partner.at[1], held)
    full = from_four(middle)
    pieces.wait()
    total = begun[...] + apply(full, held[...])
    for i, part in enumerate(own_and_partner(total)):
        totals[i] = part.astype(BF16)


def reduced_body(
    middle, two, solve, solve_partner, sides, sides_partner, lifted, ends, end, coarse,
    two_partner, total, matrices, begun, kept, held, sides_held, late, sems,
):
    pieces, mine = Pieces(sems), core()
    pieces.both(two.at[0, 1], two_partner.at[0, 1], held)
    pieces.load(sides.at[0, mine], sides_held.at[0])
    pieces.load(sides_partner.at[0, mine], sides_held.at[1])
    pieces.load(lifted, late.at[0])
    pieces.load(end, late.at[1])
    pieces.load(ends, begun)
    pieces.both(solve.at[0, 2], solve_partner.at[0, 2], matrices.at[0])
    pieces.both(solve.at[1, 1], solve_partner.at[1, 1], matrices.at[1])
    pieces.load(coarse.at[0], kept)
    full = from_four(middle)
    pieces.wait()
    both = late[0] + apply(full, held[...])
    for i, part in enumerate(own_and_partner(both)):
        total[i] = sides_held[i].astype(F32) - part
    begun[1] -= late[1]


def final_body(centre, matrices, begun, total, before, kept, given, sems):
    full = from_four(centre)
    chip, mine = lax.div(lax.axis_index("col"), 2), core()
    first = begun[0] - apply(full, matrices[0])
    last = begun[1] - apply(full, matrices[1])
    for i, out in enumerate((kept, given)):
        out[0] = own_and_partner(first)[i].astype(BF16)
        out[1] = centre[chip, mine if i == 0 else 1 - mine]
        out[2] = own_and_partner(last)[i].astype(BF16)
        out[3] = (total[i] - before[i].astype(F32)).astype(BF16)


def place_body(taken, coarse, kept, solved, reduced, sems):
    mine = core()
    solved[0] = coarse[...]
    for i in range(3):
        solved[i + 1, mine] = kept[i]
        solved[i + 1, 1 - mine] = taken[1 - mine, i]
    reduced[0, mine] = kept[3]
    reduced[0, 1 - mine] = taken[1 - mine, 3]


def steps(right_sides, coarse_solution, lift_one, solve_one, lift_two, solve_two):
    sides = right_sides.reshape(4, 2, HALF, WIDTH)
    coarse = coarse_solution.reshape(1, 2, HALF, WIDTH)
    packed = pack(sides, coarse)
    odd = lax.all_to_all(packed, "col", 0, 0)
    (lifts,) = call(
        lifts_body,
        [(IN_HBM, (2, WIDTH, 1024), BF16)],
        [],
        [lift_one, lift_two],
        copies=2,
    )
    lifts_next = passed_along(lifts, -1)
    one_partner = from_partner(lift_one)
    sides_partner = from_partner(sides)
    solve_two_partner = from_partner(solve_two)
    solve_one_partner = from_partner(solve_one)
    two_partner = from_partner(lift_two)
    following = passed_along(odd[:, 2], -1)
    lifts_partner = from_partner(lifts_next)

    lift_matrices, begun = call(
        prepare_body,
        [(IN_VMEM, (2, *MERGED), BF16), (IN_VMEM, PAIR, BF16)],
        [],
        [lift_one, one_partner, sides],
        copies=6,
        free=[sides_partner],
    )
    (middle_copies,) = call(
        middle_body,
        [(IN_HBM, COPIES, BF16)],
        [odd, lift_matrices, begun],
        products=2,
    )
    middle = over_chips(middle_copies)
    flat = (HALF, 2 * WIDTH)
    inverse, coarse_begun, ends, lifted = call(
        early_body,
        [
            (IN_VMEM, MERGED, BF16),
            (IN_VMEM, flat, F32),
            (IN_HBM, (2, *flat), F32),
            (IN_HBM, flat, F32),
        ],
        [odd],
        [
            lift_one,
            one_partner,
            solve_one,
            solve_one_partner,
            solve_two,
            solve_two_partner,
        ],
        [((5, *MERGED), BF16)],
        copies=12,
        products=5,
    )
    coarse_total, end, onward_begun = call(
        late_body,
        [(IN_VMEM, flat, F32), (IN_HBM, flat, F32), (IN_VMEM, flat, F32)],
        [odd, coarse_begun],
        [
            solve_one,
            solve_one_partner,
            solve_two,
            solve_two_partner,
            lifts_next,
        ],
        [((3, *MERGED), BF16), ((8, HALF, WIDTH), BF16)],
        free=[lifts_partner, following],
        copies=7,
        products=3,
    )
    (centre_copies,) = call(
        centre_body, [(IN_HBM, COPIES, BF16)], [middle, inverse, coarse_total]
    )
    centre = over_chips(centre_copies)
    (onward,) = call(
        onward_body,
        [(IN_VMEM, PAIR, BF16)],
        [middle, onward_begun],
        [lifts_next],
        [(MERGED, BF16)],
        free=[lifts_partner],
        copies=2,
    )
    before = passed_along(onward, 1)
    total, solve_matrices, ends_begun, coarse_kept = call(
        reduced_body,
        [
            (IN_VMEM, PAIR, F32),
            (IN_VMEM, (2, *MERGED), BF16),
            (IN_VMEM, (2, *flat), F32),
            (IN_VMEM, PAIR, BF16),
        ],
        [middle],
        [
            lift_two,
            solve_one,
            solve_one_partner,
            sides,
            sides_partner,
            lifted,
            ends,
            end,
            coarse,
        ],
        [(MERGED, BF16), (PAIR, BF16), ((2, *flat), F32)],
        copies=12,
        products=2,
        free=[two_partner],
    )
    kept, given = call(
        final_body,
        [(IN_VMEM, (4, HALF, WIDTH), BF16)] * 2,
        [centre, solve_matrices, ends_begun, total, before],
        products=2,
    )
    cores = [[i, i + 1] for i in range(0, lax.axis_size("col"), 2)]
    taken = lax.all_gather(given, "col", axis=0, axis_index_groups=cores)
    solved, reduced = call(
        place_body,
        [
            (IN_HBM, (4, 2, HALF, WIDTH), BF16),
            (IN_HBM, (1, 2, HALF, WIDTH), BF16),
        ],
        [taken, coarse_kept, kept],
    )
    return solved.reshape(4, ROWS, WIDTH), reduced.reshape(1, ROWS, WIDTH)


def solution(mesh):
    return jax.shard_map(
        steps,
        mesh=mesh,
        in_specs=(
            P("rad", None, "col"),
            P("rad", None, "col"),
            P("rad", None, "col", None),
            P("rad", None, "col", None),
            P("rad", None, "col", None),
            P("rad", None, "col", None),
        ),
        out_specs=(P("rad", None, "col"), P("rad", None, "col")),
        check_vma=False,
    )
```

time: 81.5 us -> 80.9 us (level)
  the two profiles are of different devices: /device:TPU:1 before, /device:TPU:259 now
where the time goes in v4:
time: 80.9 us; the launch traced here: 80.2 us
  starting transfers between devices  42 us (52%)
  Pallas kernels  19.4 us (24%)
  waiting for transfers between devices  11.6 us (14%)
  blocking collectives  3.16 us (4%)
  local copies, waits for them, and re-layouts  3.12 us (4%)
  between operations  0.87 us (1%)
    pallas_call x10, Pallas kernels, call(): pl.pallas_call(body, out_shape=[space(shape, dtype) for space, shape, dty...  17.2 us
    ppermute x6, starting transfers between devices, from_partner(): return lax.ppermute(array, 'col', [(i, i ^ 1) for i in range(peers)])  14.9 us
    ppermute x3, starting transfers between devices, passed_along(): return lax.ppermute(array, 'rad', pairs)  13.5 us
    ppermute x3, waiting for transfers between devices, passed_along(): return lax.ppermute(array, 'rad', pairs)  11.6 us
    all_to_all x2, starting transfers between devices, over_chips(): return lax.all_to_all(copies, 'col', 0, 0, axis_index_groups=groups)  8.49 us
    all_to_all x1, starting transfers between devices, steps(): odd = lax.all_to_all(packed, 'col', 0, 0)  5.12 us
    all_gather x1, blocking collectives, steps(): taken = lax.all_gather(given, 'col', axis=0, axis_index_groups=cores)  3.16 us
    unnamed x12, local copies, waits for them, and re-layouts  2.34 us
  transfers between devices with their start and end apart: 12, of which 2 were waited for; matrix products, arithmetic and copies ran while one was open for 1% of the time, Pallas kernels for 20%

profile of v4, /device:TPU:259, one launch (start us, length us, event | category | flops | bytes accessed | tf_op | source)
XLA Modules:
  0.0 80.2 jit_solution(1777650032535619477)
XLA Ops:
  0.6 2.2 %shard_map.77 = bf16[8,3,192,128]{3,2,1,0:T(8,128)(2,1)} custom-call(bf16[4,2,192,128]{3,2,1,0:T(8,128)(2,1)} %bitcast.10, bf16[1,2,192,128]{3,2,1,0:T(8,128)(2,1)} %bitcast.14), custom_call_target="tpu_custom_call" | custom-call | tf_op jit(solution)/shard_map/pallas_call | solution.py:132
  2.8 5.1 %all-to-all-start = ((bf16[8,3,192,128]{3,2,1,0:T(8,128)(2,1)}), bf16[8,3,192,128]{3,2,1,0:T(8,128)(2,1)S(1)}, u32[]{:S(2)}, u32[]{:S(2)}) async-start(bf16[8,3,192,128]{3,2,1,0:T(8,128)(2,1)} %shard_map.77), calls=%async_computation | async-start | bytes 2359296 | tf_op jit(solution)/shard_map/all_to_all | solution.py:317
  8.0 0.0 copy-start.5
  8.0 2.4 %collective-permute-start.2 = (bf16[2,3,128,1024]{3,2,1,0:T(8,128)(2,1)}, bf16[2,3,128,1024]{3,2,1,0:T(8,128)(2,1)}, u32[]{:S(2)}, u32[]{:S(2)}) collective-permute-start(bf16[2,3,128,1024]{3,2,1,0:T(8,128)(2,1)} %solve.5), channel_id=1, source_target_pairs={{0,1},{1,0},{2,3},{3,2},{4,5},{5,4},{6,7},{7,6},{8,9},{9,8},{10,11... | collective-permute-start | bytes 4718600 | tf_op jit(solution)/shard_map/ppermute | solution.py:30
  10.4 2.0 %collective-permute-start = (bf16[2,2,128,1024]{3,2,1,0:T(8,128)(2,1)}, bf16[2,2,128,1024]{3,2,1,0:T(8,128)(2,1)}, u32[]{:S(2)}, u32[]{:S(2)}) collective-permute-start(bf16[2,2,128,1024]{3,2,1,0:T(8,128)(2,1)} %one.5), channel_id=1, source_target_pairs={{0,1},{1,0},{2,3},{3,2},{4,5},{5,4},{6,7},{7,6},{8,9},{9,8},{10,11... | collective-permute-start | bytes 3145736 | tf_op jit(solution)/shard_map/ppermute | solution.py:30
  12.4 1.9 %shard_map.81 = bf16[2,128,1024]{2,1,0:T(8,128)(2,1)} custom-call(bf16[2,2,128,1024]{3,2,1,0:T(8,128)(2,1)} %one.5, bf16[1,2,128,1024]{3,2,1,0:T(8,128)(2,1)} %two.3), custom_call_target="tpu_custom_call" | custom-call | flops 100663296 | bytes 1000000 | tf_op jit(solution)/shard_map/pallas_call | solution.py:72
  14.3 4.2 %collective-permute-start.4 = (bf16[2,128,1024]{2,1,0:T(8,128)(2,1)}, bf16[2,128,1024]{2,1,0:T(8,128)(2,1)}, u32[]{:S(2)}, u32[]{:S(2)}) collective-permute-start(bf16[2,128,1024]{2,1,0:T(8,128)(2,1)} %shard_map.81), channel_id=1, source_target_pairs={{8,0},{16,8},{24,16},{32,24},{40,32},{48,40},{56,48},{64,56},{72,6... | collective-permute-start | bytes 1572872 | tf_op jit(solution)/shard_map/ppermute | solution.py:36
  18.5 2.6 %collective-permute-start.3 = (bf16[1,3,128,1024]{3,2,1,0:T(8,128)(2,1)}, bf16[1,3,128,1024]{3,2,1,0:T(8,128)(2,1)}, u32[]{:S(2)}, u32[]{:S(2)}) collective-permute-start(bf16[1,3,128,1024]{3,2,1,0:T(8,128)(2,1)} %last.3), channel_id=1, source_target_pairs={{0,1},{1,0},{2,3},{3,2},{4,5},{5,4},{6,7},{7,6},{8,9},{9,8},{10,11... | collective-permute-start | bytes 2359304 | tf_op jit(solution)/shard_map/ppermute | solution.py:30
  21.1 0.0 copy-done.5
  21.1 1.9 %collective-permute-start.1 = (bf16[4,2,192,128]{3,2,1,0:T(8,128)(2,1)S(1)}, bf16[4,2,192,128]{3,2,1,0:T(8,128)(2,1)S(1)}, u32[]{:S(2)}, u32[]{:S(2)}) collective-permute-start(bf16[4,2,192,128]{3,2,1,0:T(8,128)(2,1)S(1)} %bitcast.13), channel_id=1, source_target_pairs={{0,1},{1,0},{2,3},{3,2},{4,5},{5,4},{6,7},{7,6},{8,9},{9,8},{10,11... | collective-permute-start | bytes 1179656 | tf_op jit(solution)/shard_map/ppermute | solution.py:30
  23.0 6.6 %collective-permute-done.4.lifts = bf16[2,128,1024]{2,1,0:T(8,128)(2,1)} collective-permute-done((bf16[2,128,1024]{2,1,0:T(8,128)(2,1)}, bf16[2,128,1024]{2,1,0:T(8,128)(2,1)}, u32[]{:S(2)}, u32[]{:S(2)}) %collective-permute-start.4) | collective-permute-done | bytes 524320 | tf_op jit(solution)/shard_map/ppermute | solution.py:36
  29.7 3.1 %collective-permute-start.5 = (bf16[2,128,1024]{2,1,0:T(8,128)(2,1)}, bf16[2,128,1024]{2,1,0:T(8,128)(2,1)S(1)}, u32[]{:S(2)}, u32[]{:S(2)}) collective-permute-start(bf16[2,128,1024]{2,1,0:T(8,128)(2,1)} %collective-permute-done.4.lifts), channel_id=1, source_target_pairs={{0,1},{1,0},{2,3},{3,2},{4,5},{5,4},{6,7},{7,6},{8,9},{9,8},{10,11... | collective-permute-start | bytes 1572872 | tf_op jit(solution)/shard_map/ppermute | solution.py:30
  32.8 0.0 all-to-all-done.odd
  32.9 0.8 slice_bitcast_fusion
  33.6 0.0 collective-permute-done.1.sides_partner
  33.6 7.4 %collective-permute-start.6 = (bf16[8,192,128]{2,1,0:T(8,128)(2,1)}, bf16[8,192,128]{2,1,0:T(8,128)(2,1)S(1)}, u32[]{:S(2)}, u32[]{:S(2)}) collective-permute-start(bf16[8,192,128]{2,1,0:T(8,128)(2,1)} %slice_bitcast_fusion), channel_id=1, source_target_pairs={{8,0},{16,8},{24,16},{32,24},{40,32},{48,40},{56,48},{64,56},{72,6... | collective-permute-start | bytes 1179656 | tf_op jit(solution)/shard_map/ppermute | solution.py:36
  41.1 0.0 collective-permute-done.one_partner
  41.1 1.2 %shard_map.78 = (bf16[2,256,1024]{2,1,0:T(8,128)(2,1)S(1)}, bf16[2,192,128]{2,1,0:T(8,128)(2,1)S(1)}) custom-call(bf16[2,2,128,1024]{3,2,1,0:T(8,128)(2,1)} %one.5, bf16[2,2,128,1024]{3,2,1,0:T(8,128)(2,1)} %collective-permute-done.one_partner, bf16[4,2,192,128]{3,2,1,0:T(8,128)(2,1)} %bitcast.11, ...), custom_call_target="tpu_custom_call" | custom-call | flops 100663296 | bytes 1000000 | tf_op jit(solution)/shard_map/pallas_call | solution.py:72
  42.3 0.0 copy-done
  42.3 1.3 %shard_map.79 = bf16[4,2,192,128]{3,2,1,0:T(8,128)(2,1)} custom-call(bf16[8,3,192,128]{3,2,1,0:T(8,128)(2,1)S(1)} %all-to-all-done.odd, bf16[2,256,1024]{2,1,0:T(8,128)(2,1)S(1)} %get-tuple-element.19.matrices, bf16[2,192,128]{2,1,0:T(8,128)(2,1)S(1)} %get-tuple-element.20.begun), custom_call_target="tpu_custom_call" | custom-call | flops 201326592 | bytes 2000000 | tf_op jit(solution)/shard_map/pallas_call | solution.py:72
  43.6 4.2 %all-to-all-start.1 = ((bf16[4,2,192,128]{3,2,1,0:T(8,128)(2,1)}), bf16[4,2,192,128]{3,2,1,0:T(8,128)(2,1)S(1)}, u32[]{:S(2)}, u32[]{:S(2)}) async-start(bf16[4,2,192,128]{3,2,1,0:T(8,128)(2,1)} %shard_map.79), calls=%async_computation.1 | async-start | bytes 786432 | tf_op jit(solution)/shard_map/all_to_all | solution.py:25
  47.9 2.8 %collective-permute-start.7 = (bf16[1,2,128,1024]{3,2,1,0:T(8,128)(2,1)}, bf16[1,2,128,1024]{3,2,1,0:T(8,128)(2,1)S(1)}, u32[]{:S(2)}, u32[]{:S(2)}) collective-permute-start(bf16[1,2,128,1024]{3,2,1,0:T(8,128)(2,1)} %two.3), channel_id=1, source_target_pairs={{0,1},{1,0},{2,3},{3,2},{4,5},{5,4},{6,7},{7,6},{8,9},{9,8},{10,11... | collective-permute-start | bytes 1572872 | tf_op jit(solution)/shard_map/ppermute | solution.py:30
  50.6 0.0 collective-permute-done.3.last_partner
  50.6 0.0 collective-permute-done.2.solve_partner
  50.6 4.1 %shard_map.80 = (bf16[256,1024]{1,0:T(8,128)(2,1)S(1)}, f32[192,256]{1,0:T(8,128)S(1)}, f32[2,192,256]{2,1,0:T(8,128)}, f32[192,256]{1,0:T(8,128)}) custom-call(bf16[8,3,192,128]{3,2,1,0:T(8,128)(2,1)S(1)} %all-to-all-done.odd, bf16[2,2,128,1024]{3,2,1,0:T(8,128)(2,1)} %one.5, bf16[2,2,128,1024]{3,2,1,0:T(8,128)(2,1)} %collective-permute-done.one_partner, ...), custom_call_target="tpu_custom_call" | custom-call | flops 503316480 | bytes 5000000 | tf_op jit(solution)/shard_map/pallas_call | solution.py:72
  54.7 0.0 collective-permute-done.5.lifts_partner
  54.8 0.0 collective-permute-done.6.following
  54.8 2.9 %shard_map.82 = (f32[192,256]{1,0:T(8,128)S(1)}, f32[192,256]{1,0:T(8,128)}, f32[192,256]{1,0:T(8,128)S(1)}) custom-call(bf16[8,3,192,128]{3,2,1,0:T(8,128)(2,1)S(1)} %all-to-all-done.odd, f32[192,256]{1,0:T(8,128)S(1)} %get-tuple-element.22.coarse, bf16[2,3,128,1024]{3,2,1,0:T(8,128)(2,1)} %solve.5, ...), custom_call_target="tpu_custom_call" | custom-call | flops 301989888 | bytes 3000000 | tf_op jit(solution)/shard_map/pallas_call | solution.py:72
  57.7 0.0 copy-start.1
  57.7 0.7 copy-done.1
  58.4 0.0 copy-start.3
  58.4 0.7 copy-done.3
  59.1 0.0 all-to-all-done.1.middle
  59.1 0.0 copy-start.2
  59.1 0.0 copy-start.4
  59.1 1.0 %copy-done.4 = f32[192,256]{1,0:T(8,128)S(1)} copy-done((f32[192,256]{1,0:T(8,128)S(1)}, f32[192,256]{1,0:T(8,128)}, u32[]{:S(2)}) %copy-start.4) | copy-done | bytes 196632
  60.1 1.1 %shard_map.83 = bf16[4,2,192,128]{3,2,1,0:T(8,128)(2,1)} custom-call(bf16[4,2,192,128]{3,2,1,0:T(8,128)(2,1)S(1)} %all-to-all-done.1.middle, bf16[256,1024]{1,0:T(8,128)(2,1)S(1)} %get-tuple-element.21.inverse, f32[192,256]{1,0:T(8,128)S(1)} %copy-done.4), custom_call_target="tpu_custom_call" | custom-call | flops 100663296 | bytes 1000000 | tf_op jit(solution)/shard_map/pallas_call | solution.py:72
  61.2 4.2 %all-to-all-start.2 = ((bf16[4,2,192,128]{3,2,1,0:T(8,128)(2,1)}), bf16[4,2,192,128]{3,2,1,0:T(8,128)(2,1)S(1)}, u32[]{:S(2)}, u32[]{:S(2)}) async-start(bf16[4,2,192,128]{3,2,1,0:T(8,128)(2,1)} %shard_map.83), calls=%async_computation.2 | async-start | bytes 786432 | tf_op jit(solution)/shard_map/all_to_all | solution.py:25
  65.4 0.0 copy-done.2
  65.4 1.3 %shard_map.85 = bf16[2,192,128]{2,1,0:T(8,128)(2,1)S(1)} custom-call(bf16[4,2,192,128]{3,2,1,0:T(8,128)(2,1)S(1)} %all-to-all-done.1.middle, f32[192,256]{1,0:T(8,128)S(1)} %copy-done.2, bf16[2,128,1024]{2,1,0:T(8,128)(2,1)} %collective-permute-done.4.lifts, bf16[2,128,1024]{2,1,0:T(8,128)(2,1)S(1)} %collective-permute-done.5.lifts_partner), custom_call_target="tpu_custom_call" | custom-call | flops 100663296 | bytes 1000000 | tf_op jit(solution)/shard_map/pallas_call | solution.py:72
  66.7 1.9 %collective-permute-start.8 = (bf16[2,192,128]{2,1,0:T(8,128)(2,1)S(1)}, bf16[2,192,128]{2,1,0:T(8,128)(2,1)S(1)}, u32[]{:S(2)}, u32[]{:S(2)}) collective-permute-start(bf16[2,192,128]{2,1,0:T(8,128)(2,1)S(1)} %shard_map.85), channel_id=1, source_target_pairs={{0,8},{8,16},{16,24},{24,32},{32,40},{40,48},{48,56},{56,64},{64,7... | collective-permute-start | bytes 294920 | tf_op jit(solution)/shard_map/ppermute | solution.py:36
  68.6 0.0 collective-permute-done.7.two_partner
  68.6 2.1 %shard_map.84 = (f32[2,192,128]{2,1,0:T(8,128)S(1)}, bf16[2,256,1024]{2,1,0:T(8,128)(2,1)S(1)}, f32[2,192,256]{2,1,0:T(8,128)S(1)}, bf16[2,192,128]{2,1,0:T(8,128)(2,1)S(1)}) custom-call(bf16[4,2,192,128]{3,2,1,0:T(8,128)(2,1)S(1)} %all-to-all-done.1.middle, bf16[1,2,128,1024]{3,2,1,0:T(8,128)(2,1)} %two.3, bf16[2,3,128,1024]{3,2,1,0:T(8,128)(2,1)} %solve.5, ...), custom_call_target="tpu_custom_call" | custom-call | flops 201326592 | bytes 2000000 | tf_op jit(solution)/shard_map/pallas_call | solution.py:72
  70.7 5.0 %collective-permute-done.8.before = bf16[2,192,128]{2,1,0:T(8,128)(2,1)S(1)} collective-permute-done((bf16[2,192,128]{2,1,0:T(8,128)(2,1)S(1)}, bf16[2,192,128]{2,1,0:T(8,128)(2,1)S(1)}, u32[]{:S(2)}, u32[]{:S(2)}) %collective-permute-start.8) | collective-permute-done | bytes 98336 | tf_op jit(solution)/shard_map/ppermute | solution.py:36
  75.7 0.0 all-to-all-done.2.centre
  75.7 0.5 shard_map.86
  76.2 3.2 %all-gather = bf16[8,192,128]{2,1,0:T(8,128)(2,1)S(1)} all-gather(bf16[4,192,128]{2,1,0:T(8,128)(2,1)S(1)} %get-tuple-element.31), channel_id=2, replica_groups={{0,1},{2,3},{4,5},{6,7},{8,9},{10,11},{12,13},{14,15},{16,17},{18,19},{..., dimensions={0}, use_global_device_ids=true | all-gather | bytes 589824 | tf_op jit(solution)/shard_map/all_gather | solution.py:433
  79.4 0.8 %shard_map.87 = (bf16[4,2,192,128]{3,2,1,0:T(8,128)(2,1)}, bf16[1,2,192,128]{3,2,1,0:T(8,128)(2,1)}) custom-call(bf16[2,4,192,128]{3,2,1,0:T(8,128)(2,1)S(1)} %bitcast.9, bf16[2,192,128]{2,1,0:T(8,128)(2,1)S(1)} %get-tuple-element.32.coarse, bf16[4,192,128]{2,1,0:T(8,128)(2,1)S(1)} %get-tuple-element.33.kept), custom_call_target="tpu_custom_call" | custom-call | flops 100663296 | bytes 1000000 | tf_op jit(solution)/shard_map/pallas_call | solution.py:72
  (1 shorter events, 0.0 us)
Async XLA Ops:
  2.8 30.0 %all-to-all-start = ((bf16[8,3,192,128]{3,2,1,0:T(8,128)(2,1)}), bf16[8,3,192,128]{3,2,1,0:T(8,128)(2,1)S(1)}, u32[]{:S(2)}, u32[]{:S(2)}) async-start(bf16[8,3,192,128]{3,2,1,0:T(8,128)(2,1)} %shard_map.77), calls=%async_computation | async-start | bytes 2359296 | tf_op jit(solution)/shard_map/all_to_all | solution.py:317
  8.0 13.1 %copy-start.5 = (bf16[4,384,128]{2,1,0:T(8,128)(2,1)S(1)}, bf16[4,384,128]{2,1,0:T(8,128)(2,1)}, u32[]{:S(2)}) copy-start(bf16[4,384,128]{2,1,0:T(8,128)(2,1)} %param.6) | copy-start | bytes 1179652
  8.0 42.7 %collective-permute-start.2 = (bf16[2,3,128,1024]{3,2,1,0:T(8,128)(2,1)}, bf16[2,3,128,1024]{3,2,1,0:T(8,128)(2,1)}, u32[]{:S(2)}, u32[]{:S(2)}) collective-permute-start(bf16[2,3,128,1024]{3,2,1,0:T(8,128)(2,1)} %solve.5), channel_id=1, source_target_pairs={{0,1},{1,0},{2,3},{3,2},{4,5},{5,4},{6,7},{7,6},{8,9},{9,8},{10,11... | collective-permute-start | bytes 4718600 | tf_op jit(solution)/shard_map/ppermute | solution.py:30
  10.4 30.7 %collective-permute-start = (bf16[2,2,128,1024]{3,2,1,0:T(8,128)(2,1)}, bf16[2,2,128,1024]{3,2,1,0:T(8,128)(2,1)}, u32[]{:S(2)}, u32[]{:S(2)}) collective-permute-start(bf16[2,2,128,1024]{3,2,1,0:T(8,128)(2,1)} %one.5), channel_id=1, source_target_pairs={{0,1},{1,0},{2,3},{3,2},{4,5},{5,4},{6,7},{7,6},{8,9},{9,8},{10,11... | collective-permute-start | bytes 3145736 | tf_op jit(solution)/shard_map/ppermute | solution.py:30
  14.3 15.4 %collective-permute-start.4 = (bf16[2,128,1024]{2,1,0:T(8,128)(2,1)}, bf16[2,128,1024]{2,1,0:T(8,128)(2,1)}, u32[]{:S(2)}, u32[]{:S(2)}) collective-permute-start(bf16[2,128,1024]{2,1,0:T(8,128)(2,1)} %shard_map.81), channel_id=1, source_target_pairs={{8,0},{16,8},{24,16},{32,24},{40,32},{48,40},{56,48},{64,56},{72,6... | collective-permute-start | bytes 1572872 | tf_op jit(solution)/shard_map/ppermute | solution.py:36
  18.5 32.1 %collective-permute-start.3 = (bf16[1,3,128,1024]{3,2,1,0:T(8,128)(2,1)}, bf16[1,3,128,1024]{3,2,1,0:T(8,128)(2,1)}, u32[]{:S(2)}, u32[]{:S(2)}) collective-permute-start(bf16[1,3,128,1024]{3,2,1,0:T(8,128)(2,1)} %last.3), channel_id=1, source_target_pairs={{0,1},{1,0},{2,3},{3,2},{4,5},{5,4},{6,7},{7,6},{8,9},{9,8},{10,11... | collective-permute-start | bytes 2359304 | tf_op jit(solution)/shard_map/ppermute | solution.py:30
  21.1 12.5 %collective-permute-start.1 = (bf16[4,2,192,128]{3,2,1,0:T(8,128)(2,1)S(1)}, bf16[4,2,192,128]{3,2,1,0:T(8,128)(2,1)S(1)}, u32[]{:S(2)}, u32[]{:S(2)}) collective-permute-start(bf16[4,2,192,128]{3,2,1,0:T(8,128)(2,1)S(1)} %bitcast.13), channel_id=1, source_target_pairs={{0,1},{1,0},{2,3},{3,2},{4,5},{5,4},{6,7},{7,6},{8,9},{9,8},{10,11... | collective-permute-start | bytes 1179656 | tf_op jit(solution)/shard_map/ppermute | solution.py:30
  29.7 25.1 %collective-permute-start.5 = (bf16[2,128,1024]{2,1,0:T(8,128)(2,1)}, bf16[2,128,1024]{2,1,0:T(8,128)(2,1)S(1)}, u32[]{:S(2)}, u32[]{:S(2)}) collective-permute-start(bf16[2,128,1024]{2,1,0:T(8,128)(2,1)} %collective-permute-done.4.lifts), channel_id=1, source_target_pairs={{0,1},{1,0},{2,3},{3,2},{4,5},{5,4},{6,7},{7,6},{8,9},{9,8},{10,11... | collective-permute-start | bytes 1572872 | tf_op jit(solution)/shard_map/ppermute | solution.py:30
  33.6 8.7 %copy-start = (bf16[4,2,192,128]{3,2,1,0:T(8,128)(2,1)}, bf16[4,2,192,128]{3,2,1,0:T(8,128)(2,1)S(1)}, u32[]{:S(2)}) copy-start(bf16[4,2,192,128]{3,2,1,0:T(8,128)(2,1)S(1)} %collective-permute-done.1.sides_partner) | copy-start | bytes 1179652
  33.6 21.1 %collective-permute-start.6 = (bf16[8,192,128]{2,1,0:T(8,128)(2,1)}, bf16[8,192,128]{2,1,0:T(8,128)(2,1)S(1)}, u32[]{:S(2)}, u32[]{:S(2)}) collective-permute-start(bf16[8,192,128]{2,1,0:T(8,128)(2,1)} %slice_bitcast_fusion), channel_id=1, source_target_pairs={{8,0},{16,8},{24,16},{32,24},{40,32},{48,40},{56,48},{64,56},{72,6... | collective-permute-start | bytes 1179656 | tf_op jit(solution)/shard_map/ppermute | solution.py:36
  43.6 15.5 %all-to-all-start.1 = ((bf16[4,2,192,128]{3,2,1,0:T(8,128)(2,1)}), bf16[4,2,192,128]{3,2,1,0:T(8,128)(2,1)S(1)}, u32[]{:S(2)}, u32[]{:S(2)}) async-start(bf16[4,2,192,128]{3,2,1,0:T(8,128)(2,1)} %shard_map.79), calls=%async_computation.1 | async-start | bytes 786432 | tf_op jit(solution)/shard_map/all_to_all | solution.py:25
  47.9 20.8 %collective-permute-start.7 = (bf16[1,2,128,1024]{3,2,1,0:T(8,128)(2,1)}, bf16[1,2,128,1024]{3,2,1,0:T(8,128)(2,1)S(1)}, u32[]{:S(2)}, u32[]{:S(2)}) collective-permute-start(bf16[1,2,128,1024]{3,2,1,0:T(8,128)(2,1)} %two.3), channel_id=1, source_target_pairs={{0,1},{1,0},{2,3},{3,2},{4,5},{5,4},{6,7},{7,6},{8,9},{9,8},{10,11... | collective-permute-start | bytes 1572872 | tf_op jit(solution)/shard_map/ppermute | solution.py:30
  57.7 0.7 copy-start.1
  58.4 0.7 copy-start.3
  59.1 6.3 %copy-start.2 = (f32[192,256]{1,0:T(8,128)S(1)}, f32[192,256]{1,0:T(8,128)}, u32[]{:S(2)}) copy-start(f32[192,256]{1,0:T(8,128)} %copy-done.1) | copy-start | bytes 589828
  59.1 1.0 %copy-start.4 = (f32[192,256]{1,0:T(8,128)S(1)}, f32[192,256]{1,0:T(8,128)}, u32[]{:S(2)}) copy-start(f32[192,256]{1,0:T(8,128)} %copy-done.3) | copy-start | bytes 589828
  61.2 14.5 %all-to-all-start.2 = ((bf16[4,2,192,128]{3,2,1,0:T(8,128)(2,1)}), bf16[4,2,192,128]{3,2,1,0:T(8,128)(2,1)S(1)}, u32[]{:S(2)}, u32[]{:S(2)}) async-start(bf16[4,2,192,128]{3,2,1,0:T(8,128)(2,1)} %shard_map.83), calls=%async_computation.2 | async-start | bytes 786432 | tf_op jit(solution)/shard_map/all_to_all | solution.py:25
  66.7 9.0 %collective-permute-start.8 = (bf16[2,192,128]{2,1,0:T(8,128)(2,1)S(1)}, bf16[2,192,128]{2,1,0:T(8,128)(2,1)S(1)}, u32[]{:S(2)}, u32[]{:S(2)}) collective-permute-start(bf16[2,192,128]{2,1,0:T(8,128)(2,1)S(1)} %shard_map.85), channel_id=1, source_target_pairs={{0,8},{8,16},{16,24},{24,32},{32,40},{40,48},{48,56},{56,64},{64,7... | collective-permute-start | bytes 294920 | tf_op jit(solution)/shard_map/ppermute | solution.py:36

commit v5 on v4

--- a/solution.py
+++ b/solution.py
@@ -95,6 +95,7 @@
 PAIR = (2, HALF, WIDTH)
 COPIES = (4, 2, HALF, WIDTH)
 MERGED = (2 * WIDTH, 1024)
+STRIPS, STRIP = 4, 48
 
 
 def from_eight(blocks, which):
@@ -161,19 +162,73 @@
         copies[chip, 1 - mine] = results[1]
 
 
-def lifts_body(one, two, out, sems):
+def bundle_body(
+    one, two, solve_one, solve_two, sides, bundle, lifts, held, lifts_held, arrived, sent
+):
+    other = 1 - core()
+    incoming, outgoing = Pieces(arrived), Pieces(sent)
+    groups = (
+        (one.at[0, 0], lifts_held.at[0], lifts.at[0]),
+        (two.at[0, 0], lifts_held.at[1], lifts.at[1]),
+        (one.at[1], held.at[pl.ds(0, 2)], bundle.at[pl.ds(0, 2)]),
+        (one.at[0, 1], held.at[2], bundle.at[2]),
+        (two.at[0, 1], held.at[3], bundle.at[3]),
+        (solve_two.at[0], held.at[pl.ds(4, 3)], bundle.at[pl.ds(4, 3)]),
+        (solve_one.at[0], held.at[pl.ds(7, 3)], bundle.at[pl.ds(7, 3)]),
+        (solve_one.at[1], held.at[pl.ds(10, 3)], bundle.at[pl.ds(10, 3)]),
+    )
+    loads = [incoming.load(source, place) for source, place, _ in groups]
+    rows = []
+    for j in range(2 * STRIPS):
+        strip = sides.at[2 * (j // STRIPS), other, pl.ds(STRIP * (j % STRIPS), STRIP)]
+        rows.append(incoming.load(strip, strip_of(held, j)))
+    for load, (_, place, target) in zip(loads, groups):
+        load.wait()
+        outgoing.load(place, target)
+    for row in rows:
+        row.wait()
+    outgoing.load(held.at[13, pl.ds(0, STRIP)], bundle.at[13, pl.ds(0, STRIP)])
+    outgoing.wait()
+
+
+def strip_of(bundle, j):
+    return bundle.at[13, pl.ds(0, STRIP), pl.ds(WIDTH * j, WIDTH)]
+
+
+def bundled(*arrays):
+    return pl.pallas_call(
+        bundle_body,
+        out_shape=[
+            pltpu.HBM((14, WIDTH, 1024), BF16),
+            pltpu.HBM((2, WIDTH, 1024), BF16),
+        ],
+        in_specs=[HBM] * len(arrays),
+        out_specs=[HBM] * 2,
+        scratch_shapes=[
+            pltpu.VMEM((14, WIDTH, 1024), BF16),
+            pltpu.VMEM((2, WIDTH, 1024), BF16),
+            pltpu.SemaphoreType.DMA((8 + 2 * STRIPS,)),
+            pltpu.SemaphoreType.DMA((9,)),
+        ],
+        compiler_params=pltpu.CompilerParams(vmem_limit_bytes=12 << 20),
+        cost_estimate=pl.CostEstimate(
+            flops=0, bytes_accessed=9000000, transcendentals=0
+        ),
+    )(*[pltpu.with_memory_space_constraint(x, pltpu.HBM) for x in arrays])
+
+
+def load_sides(pieces, which, sides, bundle, held):
+    pieces.load(sides.at[2 * which, core()], held.at[0])
+    for j in range(STRIPS):
+        place = held.at[1, pl.ds(STRIP * j, STRIP)]
+        pieces.load(strip_of(bundle, STRIPS * which + j), place)
+
+
+def prepare_body(one, bundle, sides, matrices, begun, sems):
     pieces = Pieces(sems)
-    pieces.load(one.at[0, 0], out.at[0])
-    pieces.load(two.at[0, 0], out.at[1])
-    pieces.wait()
-
-
-def prepare_body(one, one_partner, sides, sides_partner, matrices, begun, sems):
-    pieces, mine = Pieces(sems), core()
     for i in range(2):
-        pieces.both(one.at[1, i], one_partner.at[1, i], matrices.at[i])
-    pieces.load(sides.at[2, mine], begun.at[0])
-    pieces.load(sides_partner.at[2, mine], begun.at[1])
+        pieces.both(one.at[1, i], bundle.at[i], matrices.at[i])
+    load_sides(pieces, 1, sides, bundle, begun)
     pieces.wait()
 
 
@@ -190,23 +245,25 @@
 
 
 def early_body(
-    odd, one, one_partner, solve, solve_partner, last, last_partner,
-    inverse, coarse, ends, lifted, held, sems,
+    odd, one, solve, last, bundle, lifts, lifts_partner,
+    inverses, coarse, early, onward, held, sems,
 ):
     pieces = Pieces(sems)
     waits = [
-        pieces.both(own.at[index], partner.at[index], held.at[i])
-        for i, (own, partner, index) in enumerate(
+        pieces.both(own, partner, held.at[i])
+        for i, (own, partner) in enumerate(
             (
-                (last, last_partner, (0, 1)),
-                (solve, solve_partner, (0, 0)),
-                (solve, solve_partner, (0, 1)),
-                (solve, solve_partner, (1, 0)),
-                (one, one_partner, (0, 1)),
+                (last.at[0, 1], bundle.at[5]),
+                (solve.at[0, 0], bundle.at[7]),
+                (solve.at[0, 1], bundle.at[8]),
+                (solve.at[1, 0], bundle.at[10]),
+                (one.at[0, 1], bundle.at[2]),
+                (lifts.at[0], lifts_partner.at[0]),
             )
         )
     ]
-    waits.append(pieces.both(last.at[0, 0], last_partner.at[0, 0], inverse))
+    rest = pieces.both(last.at[0, 0], bundle.at[4], inverses.at[0])
+    rest += pieces.both(last.at[0, 2], bundle.at[6], inverses.at[1])
 
     def product(vector, i):
         for copy in waits[i]:
@@ -215,77 +272,55 @@
 
     second, fourth, here = (from_eight(odd, i) for i in range(3))
     coarse[...] = product(here, 0)
-    ends[0] = product(second, 1) - product(here, 2)
-    ends[1] = product(fourth, 3)
-    lifted[...] = product(second, 4)
-    for copy in waits[5]:
+    early[0] = product(second, 1) - product(here, 2)
+    early[1] = product(fourth, 3)
+    early[2] = product(second, 4)
+    onward[...] = product(fourth, 5)
+    for copy in rest:
         copy.wait()
 
 
-def late_body(
-    odd, coarse, solve, solve_partner, last, last_partner, lifts, lifts_partner,
-    following, totals, end, onward, held, arrived, sems,
+def centre_body(middle, inverses, following, coarse, copies, held, sems):
+    pieces = Pieces(sems)
+    pieces.load(coarse, held)
+    total = apply(from_four(middle), inverses[0])
+    total -= apply(from_following(following), inverses[1])
+    pieces.wait()
+    total -= held[...]
+    spread(copies, [part.astype(BF16) for part in own_and_partner(total)])
+
+
+def onward_body(middle, begun, lifts, lifts_partner, totals, held, begun_held, sems):
+    pieces = Pieces(sems)
+    pieces.both(lifts.at[1], lifts_partner.at[1], held)
+    pieces.load(begun, begun_held)
+    full = from_four(middle)
+    pieces.wait()
+    total = begun_held[...] + apply(full, held[...])
+    for i, part in enumerate(own_and_partner(total)):
+        totals[i] = part.astype(BF16)
+
+
+def reduced_body(
+    middle, early, two, solve, sides, coarse, bundle, following,
+    total, matrices, begun, kept, held, arrived, sides_held, early_held, sems,
 ):
     pieces = Pieces(sems)
-    waits = [
-        pieces.both(own.at[index], partner.at[index], held.at[i])
-        for i, (own, partner, index) in enumerate(
-            (
-                (lifts, lifts_partner, (0,)),
-                (last, last_partner, (0, 2)),
-                (solve, solve_partner, (1, 2)),
-            )
-        )
-    ]
-    arrival = pieces.load(following, arrived)
-
-    def product(vector, i):
-        for copy in waits[i]:
-            copy.wait()
-        return apply(vector, held[i])
-
-    onward[...] = product(from_eight(odd, 1), 0)
-    arrival.wait()
-    after = from_following(arrived)
-    totals[...] = coarse[...] + product(after, 1)
-    end[...] = product(after, 2)
-
-
-def centre_body(middle, inverse, coarse, copies, sems):
-    total = apply(from_four(middle), inverse[...]) - coarse[...]
-    spread(copies, [part.astype(BF16) for part in own_and_partner(total)])
-
-
-def onward_body(middle, begun, lifts, lifts_partner, totals, held, sems):
-    pieces = Pieces(sems)
-    pieces.both(lifts.at[1], lifts_partner.at[1], held)
-    full = from_four(middle)
-    pieces.wait()
-    total = begun[...] + apply(full, held[...])
-    for i, part in enumerate(own_and_partner(total)):
-        totals[i] = part.astype(BF16)
-
-
-def reduced_body(
-    middle, two, solve, solve_partner, sides, sides_partner, lifted, ends, end, coarse,
-    two_partner, total, matrices, begun, kept, held, sides_held, late, sems,
-):
-    pieces, mine = Pieces(sems), core()
-    pieces.both(two.at[0, 1], two_partner.at[0, 1], held)
-    pieces.load(sides.at[0, mine], sides_held.at[0])
-    pieces.load(sides_partner.at[0, mine], sides_held.at[1])
-    pieces.load(lifted, late.at[0])
-    pieces.load(end, late.at[1])
-    pieces.load(ends, begun)
-    pieces.both(solve.at[0, 2], solve_partner.at[0, 2], matrices.at[0])
-    pieces.both(solve.at[1, 1], solve_partner.at[1, 1], matrices.at[1])
+    pieces.both(two.at[0, 1], bundle.at[3], held.at[0])
+    pieces.both(solve.at[1, 2], bundle.at[12], held.at[1])
+    pieces.load(following, arrived)
+    pieces.load(early, early_held)
+    load_sides(pieces, 0, sides, bundle, sides_held)
+    pieces.both(solve.at[0, 2], bundle.at[9], matrices.at[0])
+    pieces.both(solve.at[1, 1], bundle.at[11], matrices.at[1])
     pieces.load(coarse.at[0], kept)
     full = from_four(middle)
     pieces.wait()
-    both = late[0] + apply(full, held[...])
+    begun[0] = early_held[0]
+    both = early_held[2] + apply(full, held[0])
     for i, part in enumerate(own_and_partner(both)):
         total[i] = sides_held[i].astype(F32) - part
-    begun[1] -= late[1]
+    begun[1] = early_held[1] - apply(from_following(arrived), held[1])
 
 
 def final_body(centre, matrices, begun, total, before, kept, given, sems):
@@ -315,19 +350,9 @@
     coarse = coarse_solution.reshape(1, 2, HALF, WIDTH)
     packed = pack(sides, coarse)
     odd = lax.all_to_all(packed, "col", 0, 0)
-    (lifts,) = call(
-        lifts_body,
-        [(IN_HBM, (2, WIDTH, 1024), BF16)],
-        [],
-        [lift_one, lift_two],
-        copies=2,
-    )
+    bundle, lifts = bundled(lift_one, lift_two, solve_one, solve_two, sides)
     lifts_next = passed_along(lifts, -1)
-    one_partner = from_partner(lift_one)
-    sides_partner = from_partner(sides)
-    solve_two_partner = from_partner(solve_two)
-    solve_one_partner = from_partner(solve_one)
-    two_partner = from_partner(lift_two)
+    bundle = from_partner(bundle)
     following = passed_along(odd[:, 2], -1)
     lifts_partner = from_partner(lifts_next)
 
@@ -335,9 +360,8 @@
         prepare_body,
         [(IN_VMEM, (2, *MERGED), BF16), (IN_VMEM, PAIR, BF16)],
         [],
-        [lift_one, one_partner, sides],
-        copies=6,
-        free=[sides_partner],
+        [lift_one, bundle, sides],
+        copies=9,
     )
     (middle_copies,) = call(
         middle_body,
@@ -347,55 +371,39 @@
     )
     middle = over_chips(middle_copies)
     flat = (HALF, 2 * WIDTH)
-    inverse, coarse_begun, ends, lifted = call(
+    inverses, coarse_begun, early, onward_begun = call(
         early_body,
         [
-            (IN_VMEM, MERGED, BF16),
-            (IN_VMEM, flat, F32),
-            (IN_HBM, (2, *flat), F32),
+            (IN_VMEM, (2, *MERGED), BF16),
             (IN_HBM, flat, F32),
+            (IN_HBM, (3, *flat), F32),
+            (IN_HBM, flat, F32),
         ],
         [odd],
-        [
-            lift_one,
-            one_partner,
-            solve_one,
-            solve_one_partner,
-            solve_two,
-            solve_two_partner,
-        ],
-        [((5, *MERGED), BF16)],
-        copies=12,
-        products=5,
-    )
-    coarse_total, end, onward_begun = call(
-        late_body,
-        [(IN_VMEM, flat, F32), (IN_HBM, flat, F32), (IN_VMEM, flat, F32)],
-        [odd, coarse_begun],
-        [
-            solve_one,
-            solve_one_partner,
-            solve_two,
-            solve_two_partner,
-            lifts_next,
-        ],
-        [((3, *MERGED), BF16), ((8, HALF, WIDTH), BF16)],
-        free=[lifts_partner, following],
-        copies=7,
-        products=3,
+        [lift_one, solve_one, solve_two, bundle, lifts_next],
+        [((6, *MERGED), BF16)],
+        copies=16,
+        products=6,
+        free=[lifts_partner],
     )
     (centre_copies,) = call(
-        centre_body, [(IN_HBM, COPIES, BF16)], [middle, inverse, coarse_total]
+        centre_body,
+        [(IN_HBM, COPIES, BF16)],
+        [middle, inverses, following],
+        [coarse_begun],
+        [(flat, F32)],
+        copies=1,
+        products=2,
     )
     centre = over_chips(centre_copies)
     (onward,) = call(
         onward_body,
         [(IN_VMEM, PAIR, BF16)],
-        [middle, onward_begun],
-        [lifts_next],
-        [(MERGED, BF16)],
+        [middle],
+        [onward_begun, lifts_next],
+        [(MERGED, BF16), (flat, F32)],
         free=[lifts_partner],
-        copies=2,
+        copies=3,
     )
     before = passed_along(onward, 1)
     total, solve_matrices, ends_begun, coarse_kept = call(
@@ -407,21 +415,16 @@
             (IN_VMEM, PAIR, BF16),
         ],
         [middle],
+        [early, lift_two, solve_one, sides, coarse, bundle],
         [
-            lift_two,
-            solve_one,
-            solve_one_partner,
-            sides,
-            sides_partner,
-            lifted,
-            ends,
-            end,
-            coarse,
-        ],
-        [(MERGED, BF16), (PAIR, BF16), ((2, *flat), F32)],
-        copies=12,
-        products=2,
-        free=[two_partner],
+            ((2, *MERGED), BF16),
+            ((8, HALF, WIDTH), BF16),
+            (PAIR, BF16),
+            ((3, *flat), F32),
+        ],
+        copies=16,
+        products=3,
+        free=[following],
     )
     kept, given = call(
         final_body,

time: 80.9 us -> 76.7 us (0.948)
  starting transfers between devices: 42 us -> 32.8 us
  waiting for transfers between devices: 11.6 us -> 16.7 us
  local copies, waits for them, and re-layouts: 3.12 us -> 0.8 us
  blocking collectives: 3.16 us -> 4.58 us
  Pallas kernels: 19.4 us -> 20.5 us
    ppermute x6 -> x2, starting transfers between devices: 14.9 us -> 5.73 us  [from_partner(): return lax.ppermute(array, 'col', [(i, i ^ 1) for i in range(peers)])]
    pallas_call x0 -> x1, Pallas kernels: none -> 3.8 us  [bundled(): pl.pallas_call(bundle_body, out_shape=[pltpu.HBM((14, WIDTH, 1024), BF16)...]
    ppermute x3, waiting for transfers between devices: 11.6 us -> 15.1 us  [passed_along(): return lax.ppermute(array, 'rad', pairs)]
    pallas_call x10 -> x8, Pallas kernels: 17.2 us -> 14.4 us  [call(): pl.pallas_call(body, out_shape=[space(shape, dtype) for space, shape, dty...]
    unnamed x12 -> x4, local copies, waits for them, and re-layouts: 2.34 us -> 0.01 us
    all_to_all x2, waiting for transfers between devices: 0.01 us -> 1.55 us  [over_chips(): return lax.all_to_all(copies, 'col', 0, 0, axis_index_groups=groups)]
    all_gather x1, blocking collectives: 3.16 us -> 4.58 us  [steps(): taken = lax.all_gather(given, 'col', axis=0, axis_index_groups=cores)]
  transfers between devices with their start and end apart: 12 -> 8, of which waited for: 2 -> 3; matrix products, arithmetic and copies ran while one was open for 1% -> 1% of each run, Pallas kernels for 20% -> 18%
where the time goes in v5:
time: 76.7 us; the launch traced here: 76.2 us
  starting transfers between devices  32.8 us (43%)
  Pallas kernels  20.5 us (27%)
  waiting for transfers between devices  16.7 us (22%)
  blocking collectives  4.58 us (6%)
  local copies, waits for them, and re-layouts  0.8 us (1%)
  between operations  0.79 us (1%)
    ppermute x3, waiting for transfers between devices, passed_along(): return lax.ppermute(array, 'rad', pairs)  15.1 us
    pallas_call x8, Pallas kernels, call(): pl.pallas_call(body, out_shape=[space(shape, dtype) for space, shape, dty...  14.4 us
    ppermute x3, starting transfers between devices, passed_along(): return lax.ppermute(array, 'rad', pairs)  13.5 us
    all_to_all x2, starting transfers between devices, over_chips(): return lax.all_to_all(copies, 'col', 0, 0, axis_index_groups=groups)  8.87 us
    ppermute x2, starting transfers between devices, from_partner(): return lax.ppermute(array, 'col', [(i, i ^ 1) for i in range(peers)])  5.73 us
    all_to_all x1, starting transfers between devices, steps(): odd = lax.all_to_all(packed, 'col', 0, 0)  4.69 us
    all_gather x1, blocking collectives, steps(): taken = lax.all_gather(given, 'col', axis=0, axis_index_groups=cores)  4.58 us
    pallas_call x1, Pallas kernels, bundled(): pl.pallas_call(bundle_body, out_shape=[pltpu.HBM((14, WIDTH, 1024), BF16)...  3.8 us
  transfers between devices with their start and end apart: 8, of which 3 were waited for; matrix products, arithmetic and copies ran while one was open for 1% of the time, Pallas kernels for 18%

profile of v5, /device:TPU:259, one launch (start us, length us, event | category | flops | bytes accessed | tf_op | source)
XLA Modules:
  0.0 76.2 jit_solution(3038451778447227630)
XLA Ops:
  0.6 3.8 %shard_map.78 = (bf16[14,128,1024]{2,1,0:T(8,128)(2,1)}, bf16[2,128,1024]{2,1,0:T(8,128)(2,1)}) custom-call(bf16[2,2,128,1024]{3,2,1,0:T(8,128)(2,1)} %one.5, bf16[1,2,128,1024]{3,2,1,0:T(8,128)(2,1)} %two.3, bf16[2,3,128,1024]{3,2,1,0:T(8,128)(2,1)} %solve.3, bf16[1,3,128,1024]{3,2,1,0:T(8,128)(2,1)} %last.1, bf16[4,2,192,128]{3,2,1,0:T(8,128)(2,1)} %bitcast.10), custom_call_target="tpu_custom_call" | custom-call | bytes 9000000 | tf_op jit(solution)/shard_map/pallas_call | solution.py:199
  4.4 2.6 %collective-permute-start = (bf16[14,128,1024]{2,1,0:T(8,128)(2,1)}, bf16[14,128,1024]{2,1,0:T(8,128)(2,1)}, u32[]{:S(2)}, u32[]{:S(2)}) collective-permute-start(bf16[14,128,1024]{2,1,0:T(8,128)(2,1)} %get-tuple-element.18), channel_id=1, source_target_pairs={{0,1},{1,0},{2,3},{3,2},{4,5},{5,4},{6,7},{7,6},{8,9},{9,8},{10,11... | collective-permute-start | bytes 11010056 | tf_op jit(solution)/shard_map/ppermute | solution.py:30
  7.0 2.3 %shard_map.77 = bf16[8,3,192,128]{3,2,1,0:T(8,128)(2,1)} custom-call(bf16[4,2,192,128]{3,2,1,0:T(8,128)(2,1)} %bitcast.11, bf16[1,2,192,128]{3,2,1,0:T(8,128)(2,1)} %bitcast.14), custom_call_target="tpu_custom_call" | custom-call | tf_op jit(solution)/shard_map/pallas_call | solution.py:133
  9.3 0.0 copy-start.1
  9.3 4.7 %all-to-all-start = ((bf16[8,3,192,128]{3,2,1,0:T(8,128)(2,1)}), bf16[8,3,192,128]{3,2,1,0:T(8,128)(2,1)S(1)}, u32[]{:S(2)}, u32[]{:S(2)}) async-start(bf16[8,3,192,128]{3,2,1,0:T(8,128)(2,1)} %shard_map.77), calls=%async_computation | async-start | bytes 2359296 | tf_op jit(solution)/shard_map/all_to_all | solution.py:352
  14.0 0.0 copy-done.1
  14.0 4.2 %collective-permute-start.1 = (bf16[2,128,1024]{2,1,0:T(8,128)(2,1)S(1)}, bf16[2,128,1024]{2,1,0:T(8,128)(2,1)S(1)}, u32[]{:S(2)}, u32[]{:S(2)}) collective-permute-start(bf16[2,128,1024]{2,1,0:T(8,128)(2,1)S(1)} %copy-done.1), channel_id=1, source_target_pairs={{8,0},{16,8},{24,16},{32,24},{40,32},{48,40},{56,48},{64,56},{72,6... | collective-permute-start | bytes 1572872 | tf_op jit(solution)/shard_map/ppermute | solution.py:36
  18.2 10.9 %collective-permute-done.1.lifts = bf16[2,128,1024]{2,1,0:T(8,128)(2,1)S(1)} collective-permute-done((bf16[2,128,1024]{2,1,0:T(8,128)(2,1)S(1)}, bf16[2,128,1024]{2,1,0:T(8,128)(2,1)S(1)}, u32[]{:S(2)}, u32[]{:S(2)}) %collective-permute-start.1) | collective-permute-done | bytes 524320 | tf_op jit(solution)/shard_map/ppermute | solution.py:36
  29.1 0.0 copy-start
  29.1 3.1 %collective-permute-start.2 = (bf16[2,128,1024]{2,1,0:T(8,128)(2,1)S(1)}, bf16[2,128,1024]{2,1,0:T(8,128)(2,1)S(1)}, u32[]{:S(2)}, u32[]{:S(2)}) collective-permute-start(bf16[2,128,1024]{2,1,0:T(8,128)(2,1)S(1)} %collective-permute-done.1.lifts), channel_id=1, source_target_pairs={{0,1},{1,0},{2,3},{3,2},{4,5},{5,4},{6,7},{7,6},{8,9},{9,8},{10,11... | collective-permute-start | bytes 1572872 | tf_op jit(solution)/shard_map/ppermute | solution.py:30
  32.2 0.0 all-to-all-done.odd
  32.2 0.8 %slice_bitcast_fusion = bf16[8,192,128]{2,1,0:T(8,128)(2,1)} fusion(bf16[8,3,192,128]{3,2,1,0:T(8,128)(2,1)S(1)} %all-to-all-done.odd), kind=kLoop, calls=%fused_computation | loop fusion | bytes 786432 | tf_op jit(solution)/shard_map/squeeze | solution.py:356
  33.0 7.4 %collective-permute-start.3 = (bf16[8,192,128]{2,1,0:T(8,128)(2,1)}, bf16[8,192,128]{2,1,0:T(8,128)(2,1)S(1)}, u32[]{:S(2)}, u32[]{:S(2)}) collective-permute-start(bf16[8,192,128]{2,1,0:T(8,128)(2,1)} %slice_bitcast_fusion), channel_id=1, source_target_pairs={{8,0},{16,8},{24,16},{32,24},{40,32},{48,40},{56,48},{64,56},{72,6... | collective-permute-start | bytes 1179656 | tf_op jit(solution)/shard_map/ppermute | solution.py:36
  40.5 0.0 collective-permute-done.bundle
  40.5 1.3 %shard_map.79 = (bf16[2,256,1024]{2,1,0:T(8,128)(2,1)S(1)}, bf16[2,192,128]{2,1,0:T(8,128)(2,1)S(1)}) custom-call(bf16[2,2,128,1024]{3,2,1,0:T(8,128)(2,1)} %one.5, bf16[14,128,1024]{2,1,0:T(8,128)(2,1)} %collective-permute-done.bundle, bf16[4,2,192,128]{3,2,1,0:T(8,128)(2,1)} %bitcast.12), custom_call_target="tpu_custom_call" | custom-call | flops 100663296 | bytes 1000000 | tf_op jit(solution)/shard_map/pallas_call | solution.py:72
  41.7 0.0 copy-done
  41.8 1.3 %shard_map.80 = bf16[4,2,192,128]{3,2,1,0:T(8,128)(2,1)} custom-call(bf16[8,3,192,128]{3,2,1,0:T(8,128)(2,1)S(1)} %all-to-all-done.odd, bf16[2,256,1024]{2,1,0:T(8,128)(2,1)S(1)} %get-tuple-element.19.matrices, bf16[2,192,128]{2,1,0:T(8,128)(2,1)S(1)} %get-tuple-element.20.begun), custom_call_target="tpu_custom_call" | custom-call | flops 201326592 | bytes 2000000 | tf_op jit(solution)/shard_map/pallas_call | solution.py:72
  43.0 4.2 %all-to-all-start.1 = ((bf16[4,2,192,128]{3,2,1,0:T(8,128)(2,1)}), bf16[4,2,192,128]{3,2,1,0:T(8,128)(2,1)S(1)}, u32[]{:S(2)}, u32[]{:S(2)}) async-start(bf16[4,2,192,128]{3,2,1,0:T(8,128)(2,1)} %shard_map.80), calls=%async_computation.1 | async-start | bytes 786432 | tf_op jit(solution)/shard_map/all_to_all | solution.py:25
  47.3 0.0 collective-permute-done.2.lifts_partner
  47.3 4.8 %shard_map.81 = (bf16[2,256,1024]{2,1,0:T(8,128)(2,1)S(1)}, f32[192,256]{1,0:T(8,128)}, f32[3,192,256]{2,1,0:T(8,128)}, f32[192,256]{1,0:T(8,128)}) custom-call(bf16[8,3,192,128]{3,2,1,0:T(8,128)(2,1)S(1)} %all-to-all-done.odd, bf16[2,2,128,1024]{3,2,1,0:T(8,128)(2,1)} %one.5, bf16[2,3,128,1024]{3,2,1,0:T(8,128)(2,1)} %solve.3, ...), custom_call_target="tpu_custom_call" | custom-call | flops 603979776 | bytes 6000000 | tf_op jit(solution)/shard_map/pallas_call | solution.py:72
  52.1 0.0 collective-permute-done.3.following
  52.2 1.5 %all-to-all-done.1.middle = bf16[4,2,192,128]{3,2,1,0:T(8,128)(2,1)S(1)} async-done(((bf16[4,2,192,128]{3,2,1,0:T(8,128)(2,1)}), bf16[4,2,192,128]{3,2,1,0:T(8,128)(2,1)S(1)}, u32[]{:S(2)}, u32[]{:S(2)}) %all-to-all-start.1) | async-done | bytes 393248 | tf_op jit(solution)/shard_map/all_to_all | solution.py:25
  53.7 1.9 %shard_map.82 = bf16[4,2,192,128]{3,2,1,0:T(8,128)(2,1)} custom-call(bf16[4,2,192,128]{3,2,1,0:T(8,128)(2,1)S(1)} %all-to-all-done.1.middle, bf16[2,256,1024]{2,1,0:T(8,128)(2,1)S(1)} %get-tuple-element.22.inverses, bf16[8,192,128]{2,1,0:T(8,128)(2,1)S(1)} %collective-permute-done.3.following, f32[192,256]{1,0:T(8,128)} %get-tuple-element.23.coarse), custom_call_target="tpu_custom_call" | custom-call | flops 201326592 | bytes 2000000 | tf_op jit(solution)/shard_map/pallas_call | solution.py:72
  55.6 4.6 %all-to-all-start.2 = ((bf16[4,2,192,128]{3,2,1,0:T(8,128)(2,1)}), bf16[4,2,192,128]{3,2,1,0:T(8,128)(2,1)S(1)}, u32[]{:S(2)}, u32[]{:S(2)}) async-start(bf16[4,2,192,128]{3,2,1,0:T(8,128)(2,1)} %shard_map.82), calls=%async_computation.2 | async-start | bytes 786432 | tf_op jit(solution)/shard_map/all_to_all | solution.py:25
  60.2 1.4 %shard_map.84 = bf16[2,192,128]{2,1,0:T(8,128)(2,1)S(1)} custom-call(bf16[4,2,192,128]{3,2,1,0:T(8,128)(2,1)S(1)} %all-to-all-done.1.middle, f32[192,256]{1,0:T(8,128)} %get-tuple-element.28.begun, bf16[2,128,1024]{2,1,0:T(8,128)(2,1)} %copy-done, bf16[2,128,1024]{2,1,0:T(8,128)(2,1)S(1)} %collective-permute-done.2.lifts_partner), custom_call_target="tpu_custom_call" | custom-call | flops 100663296 | bytes 1000000 | tf_op jit(solution)/shard_map/pallas_call | solution.py:72
  61.6 1.9 %collective-permute-start.4 = (bf16[2,192,128]{2,1,0:T(8,128)(2,1)S(1)}, bf16[2,192,128]{2,1,0:T(8,128)(2,1)S(1)}, u32[]{:S(2)}, u32[]{:S(2)}) collective-permute-start(bf16[2,192,128]{2,1,0:T(8,128)(2,1)S(1)} %shard_map.84), channel_id=1, source_target_pairs={{0,8},{8,16},{16,24},{24,32},{32,40},{40,48},{48,56},{56,64},{64,7... | collective-permute-start | bytes 294920 | tf_op jit(solution)/shard_map/ppermute | solution.py:36
  63.5 2.5 %shard_map.83 = (f32[2,192,128]{2,1,0:T(8,128)S(1)}, bf16[2,256,1024]{2,1,0:T(8,128)(2,1)S(1)}, f32[2,192,256]{2,1,0:T(8,128)S(1)}, bf16[2,192,128]{2,1,0:T(8,128)(2,1)S(1)}) custom-call(bf16[4,2,192,128]{3,2,1,0:T(8,128)(2,1)S(1)} %all-to-all-done.1.middle, f32[3,192,256]{2,1,0:T(8,128)} %get-tuple-element.24.early, bf16[1,2,128,1024]{3,2,1,0:T(8,128)(2,1)} %two.3, ...), custom_call_target="tpu_custom_call" | custom-call | flops 301989888 | bytes 3000000 | tf_op jit(solution)/shard_map/pallas_call | solution.py:72
  66.0 4.3 %collective-permute-done.4.before = bf16[2,192,128]{2,1,0:T(8,128)(2,1)S(1)} collective-permute-done((bf16[2,192,128]{2,1,0:T(8,128)(2,1)S(1)}, bf16[2,192,128]{2,1,0:T(8,128)(2,1)S(1)}, u32[]{:S(2)}, u32[]{:S(2)}) %collective-permute-start.4) | collective-permute-done | bytes 98336 | tf_op jit(solution)/shard_map/ppermute | solution.py:36
  70.2 0.0 all-to-all-done.2.centre
  70.2 0.5 shard_map.85
  70.8 4.6 %all-gather = bf16[8,192,128]{2,1,0:T(8,128)(2,1)S(1)} all-gather(bf16[4,192,128]{2,1,0:T(8,128)(2,1)S(1)} %get-tuple-element.29), channel_id=2, replica_groups={{0,1},{2,3},{4,5},{6,7},{8,9},{10,11},{12,13},{14,15},{16,17},{18,19},{..., dimensions={0}, use_global_device_ids=true | all-gather | bytes 589824 | tf_op jit(solution)/shard_map/all_gather | solution.py:436
  75.3 0.8 %shard_map.86 = (bf16[4,2,192,128]{3,2,1,0:T(8,128)(2,1)}, bf16[1,2,192,128]{3,2,1,0:T(8,128)(2,1)}) custom-call(bf16[2,4,192,128]{3,2,1,0:T(8,128)(2,1)S(1)} %bitcast.9, bf16[2,192,128]{2,1,0:T(8,128)(2,1)S(1)} %get-tuple-element.30.coarse, bf16[4,192,128]{2,1,0:T(8,128)(2,1)S(1)} %get-tuple-element.31.kept), custom_call_target="tpu_custom_call" | custom-call | flops 100663296 | bytes 1000000 | tf_op jit(solution)/shard_map/pallas_call | solution.py:72
Async XLA Ops:
  4.4 36.0 %collective-permute-start = (bf16[14,128,1024]{2,1,0:T(8,128)(2,1)}, bf16[14,128,1024]{2,1,0:T(8,128)(2,1)}, u32[]{:S(2)}, u32[]{:S(2)}) collective-permute-start(bf16[14,128,1024]{2,1,0:T(8,128)(2,1)} %get-tuple-element.18), channel_id=1, source_target_pairs={{0,1},{1,0},{2,3},{3,2},{4,5},{5,4},{6,7},{7,6},{8,9},{9,8},{10,11... | collective-permute-start | bytes 11010056 | tf_op jit(solution)/shard_map/ppermute | solution.py:30
  9.3 4.7 %copy-start.1 = (bf16[2,128,1024]{2,1,0:T(8,128)(2,1)S(1)}, bf16[2,128,1024]{2,1,0:T(8,128)(2,1)}, u32[]{:S(2)}) copy-start(bf16[2,128,1024]{2,1,0:T(8,128)(2,1)} %get-tuple-element.21) | copy-start | bytes 1572868
  9.3 22.9 %all-to-all-start = ((bf16[8,3,192,128]{3,2,1,0:T(8,128)(2,1)}), bf16[8,3,192,128]{3,2,1,0:T(8,128)(2,1)S(1)}, u32[]{:S(2)}, u32[]{:S(2)}) async-start(bf16[8,3,192,128]{3,2,1,0:T(8,128)(2,1)} %shard_map.77), calls=%async_computation | async-start | bytes 2359296 | tf_op jit(solution)/shard_map/all_to_all | solution.py:352
  14.0 15.0 %collective-permute-start.1 = (bf16[2,128,1024]{2,1,0:T(8,128)(2,1)S(1)}, bf16[2,128,1024]{2,1,0:T(8,128)(2,1)S(1)}, u32[]{:S(2)}, u32[]{:S(2)}) collective-permute-start(bf16[2,128,1024]{2,1,0:T(8,128)(2,1)S(1)} %copy-done.1), channel_id=1, source_target_pairs={{8,0},{16,8},{24,16},{32,24},{40,32},{48,40},{56,48},{64,56},{72,6... | collective-permute-start | bytes 1572872 | tf_op jit(solution)/shard_map/ppermute | solution.py:36
  29.1 12.7 %copy-start = (bf16[2,128,1024]{2,1,0:T(8,128)(2,1)}, bf16[2,128,1024]{2,1,0:T(8,128)(2,1)S(1)}, u32[]{:S(2)}) copy-start(bf16[2,128,1024]{2,1,0:T(8,128)(2,1)S(1)} %collective-permute-done.1.lifts) | copy-start | bytes 1572868
  29.1 18.2 %collective-permute-start.2 = (bf16[2,128,1024]{2,1,0:T(8,128)(2,1)S(1)}, bf16[2,128,1024]{2,1,0:T(8,128)(2,1)S(1)}, u32[]{:S(2)}, u32[]{:S(2)}) collective-permute-start(bf16[2,128,1024]{2,1,0:T(8,128)(2,1)S(1)} %collective-permute-done.1.lifts), channel_id=1, source_target_pairs={{0,1},{1,0},{2,3},{3,2},{4,5},{5,4},{6,7},{7,6},{8,9},{9,8},{10,11... | collective-permute-start | bytes 1572872 | tf_op jit(solution)/shard_map/ppermute | solution.py:30
  33.0 19.1 %collective-permute-start.3 = (bf16[8,192,128]{2,1,0:T(8,128)(2,1)}, bf16[8,192,128]{2,1,0:T(8,128)(2,1)S(1)}, u32[]{:S(2)}, u32[]{:S(2)}) collective-permute-start(bf16[8,192,128]{2,1,0:T(8,128)(2,1)} %slice_bitcast_fusion), channel_id=1, source_target_pairs={{8,0},{16,8},{24,16},{32,24},{40,32},{48,40},{56,48},{64,56},{72,6... | collective-permute-start | bytes 1179656 | tf_op jit(solution)/shard_map/ppermute | solution.py:36
  43.0 10.7 %all-to-all-start.1 = ((bf16[4,2,192,128]{3,2,1,0:T(8,128)(2,1)}), bf16[4,2,192,128]{3,2,1,0:T(8,128)(2,1)S(1)}, u32[]{:S(2)}, u32[]{:S(2)}) async-start(bf16[4,2,192,128]{3,2,1,0:T(8,128)(2,1)} %shard_map.80), calls=%async_computation.1 | async-start | bytes 786432 | tf_op jit(solution)/shard_map/all_to_all | solution.py:25
  55.6 14.7 %all-to-all-start.2 = ((bf16[4,2,192,128]{3,2,1,0:T(8,128)(2,1)}), bf16[4,2,192,128]{3,2,1,0:T(8,128)(2,1)S(1)}, u32[]{:S(2)}, u32[]{:S(2)}) async-start(bf16[4,2,192,128]{3,2,1,0:T(8,128)(2,1)} %shard_map.82), calls=%async_computation.2 | async-start | bytes 786432 | tf_op jit(solution)/shard_map/all_to_all | solution.py:25
  61.6 8.7 %collective-permute-start.4 = (bf16[2,192,128]{2,1,0:T(8,128)(2,1)S(1)}, bf16[2,192,128]{2,1,0:T(8,128)(2,1)S(1)}, u32[]{:S(2)}, u32[]{:S(2)}) collective-permute-start(bf16[2,192,128]{2,1,0:T(8,128)(2,1)S(1)} %shard_map.84), channel_id=1, source_target_pairs={{0,8},{8,16},{16,24},{24,32},{32,40},{40,48},{48,56},{56,64},{64,7... | collective-permute-start | bytes 294920 | tf_op jit(solution)/shard_map/ppermute | solution.py:36

commit v6 on v5

--- a/solution.py
+++ b/solution.py
@@ -102,9 +102,9 @@
     return jnp.concatenate([blocks[peer, which] for peer in range(8)], axis=1)
 
 
-def from_four(blocks):
+def from_four(blocks, at=0):
     return jnp.concatenate(
-        [blocks[chip, side] for chip in range(4) for side in range(2)], axis=1
+        [blocks[chip, at + side] for chip in range(4) for side in range(2)], axis=1
     )
 
 
@@ -147,67 +147,65 @@
     )
 
 
-def from_following(following):
-    return jnp.concatenate([following[peer] for peer in range(8)], axis=1)
-
-
 def own_and_partner(total):
     return total[:, :WIDTH], total[:, WIDTH:]
 
 
-def spread(copies, results):
+def spread(copies, results, at=0):
     mine = core()
     for chip in range(4):
-        copies[chip, mine] = results[0]
-        copies[chip, 1 - mine] = results[1]
+        copies[chip, at + mine] = results[0]
+        copies[chip, at + 1 - mine] = results[1]
 
 
 def bundle_body(
-    one, two, solve_one, solve_two, sides, bundle, lifts, held, lifts_held, arrived, sent
+    one, two, solve_one, solve_two, sides, coarse, first, second, lifts,
+    first_held, held, lifts_held, arrived, sent,
 ):
     other = 1 - core()
     incoming, outgoing = Pieces(arrived), Pieces(sent)
+    pair, triple = pl.ds(0, 2), pl.ds(2, 3)
+    rows = []
+    for j in range(3 * STRIPS):
+        half = coarse.at[0, other] if j < STRIPS else sides.at[2 * (j // STRIPS - 1), other]
+        strip = half.at[pl.ds(STRIP * (j % STRIPS), STRIP)]
+        rows.append(incoming.load(strip, strip_of(first_held, j)))
     groups = (
+        (one.at[1], first_held.at[pair], first.at[pair]),
+        (one.at[0, 1], held.at[0], second.at[0]),
+        (two.at[0, 1], held.at[1], second.at[1]),
+        (solve_two.at[0], held.at[triple], second.at[triple]),
+        (solve_one.at[0], held.at[pl.ds(5, 3)], second.at[pl.ds(5, 3)]),
+        (solve_one.at[1], held.at[pl.ds(8, 3)], second.at[pl.ds(8, 3)]),
         (one.at[0, 0], lifts_held.at[0], lifts.at[0]),
         (two.at[0, 0], lifts_held.at[1], lifts.at[1]),
-        (one.at[1], held.at[pl.ds(0, 2)], bundle.at[pl.ds(0, 2)]),
-        (one.at[0, 1], held.at[2], bundle.at[2]),
-        (two.at[0, 1], held.at[3], bundle.at[3]),
-        (solve_two.at[0], held.at[pl.ds(4, 3)], bundle.at[pl.ds(4, 3)]),
-        (solve_one.at[0], held.at[pl.ds(7, 3)], bundle.at[pl.ds(7, 3)]),
-        (solve_one.at[1], held.at[pl.ds(10, 3)], bundle.at[pl.ds(10, 3)]),
     )
     loads = [incoming.load(source, place) for source, place, _ in groups]
-    rows = []
-    for j in range(2 * STRIPS):
-        strip = sides.at[2 * (j // STRIPS), other, pl.ds(STRIP * (j % STRIPS), STRIP)]
-        rows.append(incoming.load(strip, strip_of(held, j)))
+    for row in rows:
+        row.wait()
+    used = pl.ds(0, 2 * STRIP)
+    outgoing.load(first_held.at[2, used], first.at[2, used])
     for load, (_, place, target) in zip(loads, groups):
         load.wait()
         outgoing.load(place, target)
-    for row in rows:
-        row.wait()
-    outgoing.load(held.at[13, pl.ds(0, STRIP)], bundle.at[13, pl.ds(0, STRIP)])
     outgoing.wait()
 
 
 def strip_of(bundle, j):
-    return bundle.at[13, pl.ds(0, STRIP), pl.ds(WIDTH * j, WIDTH)]
+    row, column = (0, j) if j < 2 * STRIPS else (1, j - 2 * STRIPS)
+    return bundle.at[2, pl.ds(STRIP * row, STRIP), pl.ds(WIDTH * column, WIDTH)]
 
 
 def bundled(*arrays):
+    shapes = [(3, WIDTH, 1024), (11, WIDTH, 1024), (2, WIDTH, 1024)]
     return pl.pallas_call(
         bundle_body,
-        out_shape=[
-            pltpu.HBM((14, WIDTH, 1024), BF16),
-            pltpu.HBM((2, WIDTH, 1024), BF16),
-        ],
+        out_shape=[pltpu.HBM(shape, BF16) for shape in shapes],
         in_specs=[HBM] * len(arrays),
-        out_specs=[HBM] * 2,
-        scratch_shapes=[
-            pltpu.VMEM((14, WIDTH, 1024), BF16),
-            pltpu.VMEM((2, WIDTH, 1024), BF16),
-            pltpu.SemaphoreType.DMA((8 + 2 * STRIPS,)),
+        out_specs=[HBM] * 3,
+        scratch_shapes=[pltpu.VMEM(shape, BF16) for shape in shapes]
+        + [
+            pltpu.SemaphoreType.DMA((8 + 3 * STRIPS,)),
             pltpu.SemaphoreType.DMA((9,)),
         ],
         compiler_params=pltpu.CompilerParams(vmem_limit_bytes=12 << 20),
@@ -217,22 +215,23 @@
     )(*[pltpu.with_memory_space_constraint(x, pltpu.HBM) for x in arrays])
 
 
-def load_sides(pieces, which, sides, bundle, held):
-    pieces.load(sides.at[2 * which, core()], held.at[0])
+def load_half(pieces, own, bundle, which, held):
+    pieces.load(own, held.at[0])
     for j in range(STRIPS):
         place = held.at[1, pl.ds(STRIP * j, STRIP)]
         pieces.load(strip_of(bundle, STRIPS * which + j), place)
 
 
-def prepare_body(one, bundle, sides, matrices, begun, sems):
-    pieces = Pieces(sems)
+def prepare_body(one, bundle, sides, coarse, matrices, begun, coarse_pair, sems):
+    pieces, mine = Pieces(sems), core()
+    load_half(pieces, coarse.at[0, mine], bundle, 0, coarse_pair)
     for i in range(2):
         pieces.both(one.at[1, i], bundle.at[i], matrices.at[i])
-    load_sides(pieces, 1, sides, bundle, begun)
+    load_half(pieces, sides.at[2, mine], bundle, 2, begun)
     pieces.wait()
 
 
-def middle_body(odd, matrices, begun, copies, sems):
+def middle_body(odd, matrices, begun, following, copies, sems):
     total = apply(from_eight(odd, 0), matrices[0])
     total += apply(from_eight(odd, 1), matrices[1])
     spread(
@@ -242,28 +241,27 @@
             for i, part in enumerate(own_and_partner(total))
         ],
     )
+    spread(copies, [following[0], following[1]], 2)
 
 
 def early_body(
-    odd, one, solve, last, bundle, lifts, lifts_partner,
-    inverses, coarse, early, onward, held, sems,
+    odd, one, solve, last, bundle, inverses, coarse, early, onward, held, sems
 ):
     pieces = Pieces(sems)
     waits = [
         pieces.both(own, partner, held.at[i])
         for i, (own, partner) in enumerate(
             (
-                (last.at[0, 1], bundle.at[5]),
-                (solve.at[0, 0], bundle.at[7]),
-                (solve.at[0, 1], bundle.at[8]),
-                (solve.at[1, 0], bundle.at[10]),
-                (one.at[0, 1], bundle.at[2]),
-                (lifts.at[0], lifts_partner.at[0]),
+                (last.at[0, 1], bundle.at[3]),
+                (solve.at[0, 0], bundle.at[5]),
+                (solve.at[0, 1], bundle.at[6]),
+                (solve.at[1, 0], bundle.at[8]),
+                (one.at[0, 1], bundle.at[0]),
             )
         )
     ]
-    rest = pieces.both(last.at[0, 0], bundle.at[4], inverses.at[0])
-    rest += pieces.both(last.at[0, 2], bundle.at[6], inverses.at[1])
+    rest = pieces.both(last.at[0, 0], bundle.at[2], inverses.at[0])
+    rest += pieces.both(last.at[0, 2], bundle.at[4], inverses.at[1])
 
     def product(vector, i):
         for copy in waits[i]:
@@ -271,56 +269,53 @@
         return apply(vector, held[i])
 
     second, fourth, here = (from_eight(odd, i) for i in range(3))
+    onward[...] = fourth
     coarse[...] = product(here, 0)
     early[0] = product(second, 1) - product(here, 2)
     early[1] = product(fourth, 3)
     early[2] = product(second, 4)
-    onward[...] = product(fourth, 5)
     for copy in rest:
         copy.wait()
 
 
-def centre_body(middle, inverses, following, coarse, copies, held, sems):
+def centre_body(gathered, inverses, coarse, copies, sems):
+    total = apply(from_four(gathered), inverses[0])
+    total -= apply(from_four(gathered, 2), inverses[1]) + coarse[...]
+    spread(copies, [part.astype(BF16) for part in own_and_partner(total)])
+
+
+def onward_body(
+    gathered, fourth, lifts, lifts_partner, totals, held, fourth_held, sems
+):
     pieces = Pieces(sems)
-    pieces.load(coarse, held)
-    total = apply(from_four(middle), inverses[0])
-    total -= apply(from_following(following), inverses[1])
+    for i in range(2):
+        pieces.both(lifts.at[i], lifts_partner.at[i], held.at[i])
+    pieces.load(fourth, fourth_held)
+    full = from_four(gathered)
     pieces.wait()
-    total -= held[...]
-    spread(copies, [part.astype(BF16) for part in own_and_partner(total)])
-
-
-def onward_body(middle, begun, lifts, lifts_partner, totals, held, begun_held, sems):
-    pieces = Pieces(sems)
-    pieces.both(lifts.at[1], lifts_partner.at[1], held)
-    pieces.load(begun, begun_held)
-    full = from_four(middle)
-    pieces.wait()
-    total = begun_held[...] + apply(full, held[...])
+    total = apply(fourth_held[...], held[0]) + apply(full, held[1])
     for i, part in enumerate(own_and_partner(total)):
         totals[i] = part.astype(BF16)
 
 
 def reduced_body(
-    middle, early, two, solve, sides, coarse, bundle, following,
-    total, matrices, begun, kept, held, arrived, sides_held, early_held, sems,
+    gathered, early, two, solve, sides, coarse, first, second,
+    total, matrices, begun, kept, held, sides_held, early_held, sems,
 ):
     pieces = Pieces(sems)
-    pieces.both(two.at[0, 1], bundle.at[3], held.at[0])
-    pieces.both(solve.at[1, 2], bundle.at[12], held.at[1])
-    pieces.load(following, arrived)
+    pieces.both(two.at[0, 1], second.at[1], held.at[0])
+    pieces.both(solve.at[1, 2], second.at[10], held.at[1])
     pieces.load(early, early_held)
-    load_sides(pieces, 0, sides, bundle, sides_held)
-    pieces.both(solve.at[0, 2], bundle.at[9], matrices.at[0])
-    pieces.both(solve.at[1, 1], bundle.at[11], matrices.at[1])
+    load_half(pieces, sides.at[0, core()], first, 1, sides_held)
+    pieces.both(solve.at[0, 2], second.at[7], matrices.at[0])
+    pieces.both(solve.at[1, 1], second.at[9], matrices.at[1])
     pieces.load(coarse.at[0], kept)
-    full = from_four(middle)
     pieces.wait()
     begun[0] = early_held[0]
-    both = early_held[2] + apply(full, held[0])
+    both = early_held[2] + apply(from_four(gathered), held[0])
     for i, part in enumerate(own_and_partner(both)):
         total[i] = sides_held[i].astype(F32) - part
-    begun[1] = early_held[1] - apply(from_following(arrived), held[1])
+    begun[1] = early_held[1] - apply(from_four(gathered, 2), held[1])
 
 
 def final_body(centre, matrices, begun, total, before, kept, given, sems):
@@ -350,60 +345,62 @@
     coarse = coarse_solution.reshape(1, 2, HALF, WIDTH)
     packed = pack(sides, coarse)
     odd = lax.all_to_all(packed, "col", 0, 0)
-    bundle, lifts = bundled(lift_one, lift_two, solve_one, solve_two, sides)
+    first, second, lifts = bundled(
+        lift_one, lift_two, solve_one, solve_two, sides, coarse
+    )
+    first = from_partner(first)
+    second = from_partner(second)
+    lift_matrices, begun, coarse_pair = call(
+        prepare_body,
+        [
+            (IN_VMEM, (2, *MERGED), BF16),
+            (IN_VMEM, PAIR, BF16),
+            (IN_VMEM, PAIR, BF16),
+        ],
+        [],
+        [lift_one, first, sides, coarse],
+        copies=14,
+    )
+    following = passed_along(coarse_pair, -1)
     lifts_next = passed_along(lifts, -1)
-    bundle = from_partner(bundle)
-    following = passed_along(odd[:, 2], -1)
     lifts_partner = from_partner(lifts_next)
-
-    lift_matrices, begun = call(
-        prepare_body,
-        [(IN_VMEM, (2, *MERGED), BF16), (IN_VMEM, PAIR, BF16)],
-        [],
-        [lift_one, bundle, sides],
-        copies=9,
-    )
     (middle_copies,) = call(
         middle_body,
-        [(IN_HBM, COPIES, BF16)],
-        [odd, lift_matrices, begun],
+        [(IN_HBM, (4, 4, HALF, WIDTH), BF16)],
+        [odd, lift_matrices, begun, following],
         products=2,
     )
-    middle = over_chips(middle_copies)
+    gathered = over_chips(middle_copies)
     flat = (HALF, 2 * WIDTH)
-    inverses, coarse_begun, early, onward_begun = call(
+    inverses, coarse_begun, early, fourth = call(
         early_body,
         [
             (IN_VMEM, (2, *MERGED), BF16),
-            (IN_HBM, flat, F32),
+            (IN_VMEM, flat, F32),
             (IN_HBM, (3, *flat), F32),
-            (IN_HBM, flat, F32),
+            (IN_HBM, (HALF, 1024), BF16),
         ],
         [odd],
-        [lift_one, solve_one, solve_two, bundle, lifts_next],
-        [((6, *MERGED), BF16)],
-        copies=16,
-        products=6,
-        free=[lifts_partner],
+        [lift_one, solve_one, solve_two, second],
+        [((5, *MERGED), BF16)],
+        copies=14,
+        products=5,
     )
     (centre_copies,) = call(
         centre_body,
         [(IN_HBM, COPIES, BF16)],
-        [middle, inverses, following],
-        [coarse_begun],
-        [(flat, F32)],
-        copies=1,
+        [gathered, inverses, coarse_begun],
         products=2,
     )
     centre = over_chips(centre_copies)
     (onward,) = call(
         onward_body,
         [(IN_VMEM, PAIR, BF16)],
-        [middle],
-        [onward_begun, lifts_next],
-        [(MERGED, BF16), (flat, F32)],
+        [gathered],
+        [fourth, lifts_next],
+        [((2, *MERGED), BF16), ((HALF, 1024), BF16)],
         free=[lifts_partner],
-        copies=3,
+        copies=5,
     )
     before = passed_along(onward, 1)
     total, solve_matrices, ends_begun, coarse_kept = call(
@@ -414,17 +411,11 @@
             (IN_VMEM, (2, *flat), F32),
             (IN_VMEM, PAIR, BF16),
         ],
-        [middle],
-        [early, lift_two, solve_one, sides, coarse, bundle],
-        [
-            ((2, *MERGED), BF16),
-            ((8, HALF, WIDTH), BF16),
-            (PAIR, BF16),
-            ((3, *flat), F32),
-        ],
-        copies=16,
+        [gathered],
+        [early, lift_two, solve_one, sides, coarse, first, second],
+        [((2, *MERGED), BF16), (PAIR, BF16), ((3, *flat), F32)],
+        copies=15,
         products=3,
-        free=[following],
     )
     kept, given = call(
         final_body,

time: 76.7 us -> 74.2 us (0.967)
  waiting for transfers between devices: 16.7 us -> 13.5 us
  local copies, waits for them, and re-layouts: 0.8 us -> 2.47 us
  Pallas kernels: 20.5 us -> 19.7 us
    ppermute x3, waiting for transfers between devices: 15.1 us -> 11.8 us  [passed_along(): return lax.ppermute(array, 'rad', pairs)]
    ppermute x3, starting transfers between devices: 13.5 us -> 10.3 us  [passed_along(): return lax.ppermute(array, 'rad', pairs)]
    ppermute x2 -> x3, starting transfers between devices: 5.73 us -> 8.3 us  [from_partner(): return lax.ppermute(array, 'col', [(i, i ^ 1) for i in range(peers)])]
    unnamed x4 -> x10, local copies, waits for them, and re-layouts: 0.01 us -> 2.47 us
    squeeze x1 -> x0, local copies, waits for them, and re-layouts: 0.79 us -> none  [steps(): following = passed_along(odd[:, 2], -1)]
  transfers between devices with their start and end apart: 8 -> 9, of which waited for: 3 -> 3; matrix products, arithmetic and copies ran while one was open for 1% -> 0% of each run, Pallas kernels for 18% -> 20%
where the time goes in v6:
time: 74.2 us; the launch traced here: 73.6 us
  starting transfers between devices  32.2 us (43%)
  Pallas kernels  19.7 us (27%)
  waiting for transfers between devices  13.5 us (18%)
  blocking collectives  4.97 us (7%)
  local copies, waits for them, and re-layouts  2.47 us (3%)
  between operations  0.81 us (1%)
    pallas_call x8, Pallas kernels, call(): pl.pallas_call(body, out_shape=[space(shape, dtype) for space, shape, dty...  13.8 us
    ppermute x3, waiting for transfers between devices, passed_along(): return lax.ppermute(array, 'rad', pairs)  11.8 us
    ppermute x3, starting transfers between devices, passed_along(): return lax.ppermute(array, 'rad', pairs)  10.3 us
    all_to_all x2, starting transfers between devices, over_chips(): return lax.all_to_all(copies, 'col', 0, 0, axis_index_groups=groups)  8.87 us
    ppermute x3, starting transfers between devices, from_partner(): return lax.ppermute(array, 'col', [(i, i ^ 1) for i in range(peers)])  8.3 us
    all_gather x1, blocking collectives, steps(): taken = lax.all_gather(given, 'col', axis=0, axis_index_groups=cores)  4.97 us
    all_to_all x1, starting transfers between devices, steps(): odd = lax.all_to_all(packed, 'col', 0, 0)  4.69 us
    pallas_call x1, Pallas kernels, bundled(): pl.pallas_call(bundle_body, out_shape=[pltpu.HBM(shape, BF16) for shape i...  3.72 us
  transfers between devices with their start and end apart: 9, of which 3 were waited for; matrix products, arithmetic and copies ran while one was open for 0% of the time, Pallas kernels for 20%

profile of v6, /device:TPU:259, one launch (start us, length us, event | category | flops | bytes accessed | tf_op | source)
XLA Modules:
  0.0 73.6 jit_solution(558660329882949793)
XLA Ops:
  0.6 3.7 %shard_map.78 = (bf16[3,128,1024]{2,1,0:T(8,128)(2,1)}, bf16[11,128,1024]{2,1,0:T(8,128)(2,1)}, bf16[2,128,1024]{2,1,0:T(8,128)(2,1)}) custom-call(bf16[2,2,128,1024]{3,2,1,0:T(8,128)(2,1)} %one.5, bf16[1,2,128,1024]{3,2,1,0:T(8,128)(2,1)} %two.3, bf16[2,3,128,1024]{3,2,1,0:T(8,128)(2,1)} %solve.3, bf16[1,3,128,1024]{3,2,1,0:T(8,128)(2,1)} %last.1, ...), custom_call_target="tpu_custom_call" | custom-call | bytes 9000000 | tf_op jit(solution)/shard_map/pallas_call | solution.py:201
  4.4 2.6 %collective-permute-start.2 = (bf16[11,128,1024]{2,1,0:T(8,128)(2,1)}, bf16[11,128,1024]{2,1,0:T(8,128)(2,1)}, u32[]{:S(2)}, u32[]{:S(2)}) collective-permute-start(bf16[11,128,1024]{2,1,0:T(8,128)(2,1)} %get-tuple-element.24), channel_id=1, source_target_pairs={{0,1},{1,0},{2,3},{3,2},{4,5},{5,4},{6,7},{7,6},{8,9},{9,8},{10,11... | collective-permute-start | bytes 8650760 | tf_op jit(solution)/shard_map/ppermute | solution.py:30
  6.9 2.2 %shard_map.77 = bf16[8,3,192,128]{3,2,1,0:T(8,128)(2,1)} custom-call(bf16[4,2,192,128]{3,2,1,0:T(8,128)(2,1)} %bitcast.7, bf16[1,2,192,128]{3,2,1,0:T(8,128)(2,1)} %bitcast.11), custom_call_target="tpu_custom_call" | custom-call | tf_op jit(solution)/shard_map/pallas_call | solution.py:133
  9.1 0.0 copy-start.3
  9.2 0.0 copy-start.4
  9.2 4.7 %all-to-all-start = ((bf16[8,3,192,128]{3,2,1,0:T(8,128)(2,1)}), bf16[8,3,192,128]{3,2,1,0:T(8,128)(2,1)S(1)}, u32[]{:S(2)}, u32[]{:S(2)}) async-start(bf16[8,3,192,128]{3,2,1,0:T(8,128)(2,1)} %shard_map.77), calls=%async_computation | async-start | bytes 2359296 | tf_op jit(solution)/shard_map/all_to_all | solution.py:347
  13.9 0.0 copy-done.3
  13.9 2.3 %collective-permute-start = (bf16[3,128,1024]{2,1,0:T(8,128)(2,1)S(1)}, bf16[3,128,1024]{2,1,0:T(8,128)(2,1)S(1)}, u32[]{:S(2)}, u32[]{:S(2)}) collective-permute-start(bf16[3,128,1024]{2,1,0:T(8,128)(2,1)S(1)} %copy-done.3), channel_id=1, source_target_pairs={{0,1},{1,0},{2,3},{3,2},{4,5},{5,4},{6,7},{7,6},{8,9},{9,8},{10,11... | collective-permute-start | bytes 2359304 | tf_op jit(solution)/shard_map/ppermute | solution.py:30
  16.2 0.0 copy-done.4
  16.2 4.2 %collective-permute-start.3 = (bf16[2,128,1024]{2,1,0:T(8,128)(2,1)S(1)}, bf16[2,128,1024]{2,1,0:T(8,128)(2,1)}, u32[]{:S(2)}, u32[]{:S(2)}) collective-permute-start(bf16[2,128,1024]{2,1,0:T(8,128)(2,1)S(1)} %copy-done.4), channel_id=1, source_target_pairs={{8,0},{16,8},{24,16},{32,24},{40,32},{48,40},{56,48},{64,56},{72,6... | collective-permute-start | bytes 1572872 | tf_op jit(solution)/shard_map/ppermute | solution.py:36
  20.4 0.0 collective-permute-done.bundle.first
  20.4 0.0 copy-start.2
  20.4 0.9 %copy-done.2 = bf16[3,128,1024]{2,1,0:T(8,128)(2,1)} copy-done((bf16[3,128,1024]{2,1,0:T(8,128)(2,1)}, bf16[3,128,1024]{2,1,0:T(8,128)(2,1)S(1)}, u32[]{:S(2)}) %copy-start.2) | copy-done | bytes 786456
  21.3 1.4 %shard_map.79 = (bf16[2,256,1024]{2,1,0:T(8,128)(2,1)S(1)}, bf16[2,192,128]{2,1,0:T(8,128)(2,1)S(1)}, bf16[2,192,128]{2,1,0:T(8,128)(2,1)S(1)}) custom-call(bf16[2,2,128,1024]{3,2,1,0:T(8,128)(2,1)} %one.5, bf16[3,128,1024]{2,1,0:T(8,128)(2,1)} %copy-done.2, bf16[4,2,192,128]{3,2,1,0:T(8,128)(2,1)} %bitcast.8, bf16[1,2,192,128]{3,2,1,0:T(8,128)(2,1)} %bitcast.12), custom_call_target="tpu_custom_call" | custom-call | flops 100663296 | bytes 1000000 | tf_op jit(solution)/shard_map/pallas_call | solution.py:72
  22.7 3.0 %collective-permute-start.1 = (bf16[2,192,128]{2,1,0:T(8,128)(2,1)S(1)}, bf16[2,192,128]{2,1,0:T(8,128)(2,1)S(1)}, u32[]{:S(2)}, u32[]{:S(2)}) collective-permute-start(bf16[2,192,128]{2,1,0:T(8,128)(2,1)S(1)} %get-tuple-element.23), channel_id=1, source_target_pairs={{8,0},{16,8},{24,16},{32,24},{40,32},{48,40},{56,48},{64,56},{72,6... | collective-permute-start | bytes 294920 | tf_op jit(solution)/shard_map/ppermute | solution.py:36
  25.7 8.0 %collective-permute-done.1.following = bf16[2,192,128]{2,1,0:T(8,128)(2,1)S(1)} collective-permute-done((bf16[2,192,128]{2,1,0:T(8,128)(2,1)S(1)}, bf16[2,192,128]{2,1,0:T(8,128)(2,1)S(1)}, u32[]{:S(2)}, u32[]{:S(2)}) %collective-permute-start.1) | collective-permute-done | bytes 98336 | tf_op jit(solution)/shard_map/ppermute | solution.py:36
  33.6 0.0 all-to-all-done.odd
  33.6 1.4 %shard_map.80 = bf16[4,4,192,128]{3,2,1,0:T(8,128)(2,1)} custom-call(bf16[8,3,192,128]{3,2,1,0:T(8,128)(2,1)S(1)} %all-to-all-done.odd, bf16[2,256,1024]{2,1,0:T(8,128)(2,1)S(1)} %get-tuple-element.21.matrices, bf16[2,192,128]{2,1,0:T(8,128)(2,1)S(1)} %get-tuple-element.22.begun, bf16[2,192,128]{2,1,0:T(8,128)(2,1)S(1)} %collective-permute-done.1.following), custom_call_target="tpu_custom_call" | custom-call | flops 201326592 | bytes 2000000 | tf_op jit(solution)/shard_map/pallas_call | solution.py:72
  35.1 4.2 %all-to-all-start.1 = ((bf16[4,4,192,128]{3,2,1,0:T(8,128)(2,1)}), bf16[4,4,192,128]{3,2,1,0:T(8,128)(2,1)S(1)}, u32[]{:S(2)}, u32[]{:S(2)}) async-start(bf16[4,4,192,128]{3,2,1,0:T(8,128)(2,1)} %shard_map.80), calls=%async_computation.1 | async-start | bytes 1572864 | tf_op jit(solution)/shard_map/all_to_all | solution.py:25
  39.3 0.0 collective-permute-done.3.lifts
  39.3 3.4 %collective-permute-start.4 = (bf16[2,128,1024]{2,1,0:T(8,128)(2,1)}, bf16[2,128,1024]{2,1,0:T(8,128)(2,1)S(1)}, u32[]{:S(2)}, u32[]{:S(2)}) collective-permute-start(bf16[2,128,1024]{2,1,0:T(8,128)(2,1)} %collective-permute-done.3.lifts), channel_id=1, source_target_pairs={{0,1},{1,0},{2,3},{3,2},{4,5},{5,4},{6,7},{7,6},{8,9},{9,8},{10,11... | collective-permute-start | bytes 1572872 | tf_op jit(solution)/shard_map/ppermute | solution.py:30
  42.8 0.0 collective-permute-done.2.bundle.second
  42.8 4.2 %shard_map.81 = (bf16[2,256,1024]{2,1,0:T(8,128)(2,1)S(1)}, f32[192,256]{1,0:T(8,128)S(1)}, f32[3,192,256]{2,1,0:T(8,128)}, bf16[192,1024]{1,0:T(8,128)(2,1)}) custom-call(bf16[8,3,192,128]{3,2,1,0:T(8,128)(2,1)S(1)} %all-to-all-done.odd, bf16[2,2,128,1024]{3,2,1,0:T(8,128)(2,1)} %one.5, bf16[2,3,128,1024]{3,2,1,0:T(8,128)(2,1)} %solve.3, ...), custom_call_target="tpu_custom_call" | custom-call | flops 503316480 | bytes 5000000 | tf_op jit(solution)/shard_map/pallas_call | solution.py:72
  47.0 0.0 copy-start
  47.0 0.7 copy-done
  47.7 1.6 %all-to-all-done.1.gathered = bf16[4,4,192,128]{3,2,1,0:T(8,128)(2,1)S(1)} async-done(((bf16[4,4,192,128]{3,2,1,0:T(8,128)(2,1)}), bf16[4,4,192,128]{3,2,1,0:T(8,128)(2,1)S(1)}, u32[]{:S(2)}, u32[]{:S(2)}) %all-to-all-start.1) | async-done | bytes 786464 | tf_op jit(solution)/shard_map/all_to_all | solution.py:25
  49.3 0.0 copy-start.1
  49.3 0.9 %copy-done.1 = f32[192,256]{1,0:T(8,128)S(1)} copy-done((f32[192,256]{1,0:T(8,128)S(1)}, f32[192,256]{1,0:T(8,128)}, u32[]{:S(2)}) %copy-start.1) | copy-done | bytes 196632
  50.2 1.3 %shard_map.82 = bf16[4,2,192,128]{3,2,1,0:T(8,128)(2,1)} custom-call(bf16[4,4,192,128]{3,2,1,0:T(8,128)(2,1)S(1)} %all-to-all-done.1.gathered, bf16[2,256,1024]{2,1,0:T(8,128)(2,1)S(1)} %get-tuple-element.25.inverses, f32[192,256]{1,0:T(8,128)S(1)} %copy-done.1), custom_call_target="tpu_custom_call" | custom-call | flops 201326592 | bytes 2000000 | tf_op jit(solution)/shard_map/pallas_call | solution.py:72
  51.5 4.6 %all-to-all-start.2 = ((bf16[4,2,192,128]{3,2,1,0:T(8,128)(2,1)}), bf16[4,2,192,128]{3,2,1,0:T(8,128)(2,1)S(1)}, u32[]{:S(2)}, u32[]{:S(2)}) async-start(bf16[4,2,192,128]{3,2,1,0:T(8,128)(2,1)} %shard_map.82), calls=%async_computation.2 | async-start | bytes 786432 | tf_op jit(solution)/shard_map/all_to_all | solution.py:25
  56.1 0.0 collective-permute-done.4.lifts_partner
  56.1 1.7 %shard_map.84 = bf16[2,192,128]{2,1,0:T(8,128)(2,1)S(1)} custom-call(bf16[4,4,192,128]{3,2,1,0:T(8,128)(2,1)S(1)} %all-to-all-done.1.gathered, bf16[192,1024]{1,0:T(8,128)(2,1)} %get-tuple-element.31.fourth, bf16[2,128,1024]{2,1,0:T(8,128)(2,1)} %collective-permute-done.3.lifts, bf16[2,128,1024]{2,1,0:T(8,128)(2,1)S(1)} %collective-permute-done.4.lifts_partner), custom_call_target="tpu_custom_call" | custom-call | flops 100663296 | bytes 1000000 | tf_op jit(solution)/shard_map/pallas_call | solution.py:72
  57.8 3.1 %collective-permute-start.5 = (bf16[2,192,128]{2,1,0:T(8,128)(2,1)S(1)}, bf16[2,192,128]{2,1,0:T(8,128)(2,1)S(1)}, u32[]{:S(2)}, u32[]{:S(2)}) collective-permute-start(bf16[2,192,128]{2,1,0:T(8,128)(2,1)S(1)} %shard_map.84), channel_id=1, source_target_pairs={{0,8},{8,16},{16,24},{24,32},{32,40},{40,48},{48,56},{56,64},{64,7... | collective-permute-start | bytes 294920 | tf_op jit(solution)/shard_map/ppermute | solution.py:36
  61.0 2.4 %shard_map.83 = (f32[2,192,128]{2,1,0:T(8,128)S(1)}, bf16[2,256,1024]{2,1,0:T(8,128)(2,1)S(1)}, f32[2,192,256]{2,1,0:T(8,128)S(1)}, bf16[2,192,128]{2,1,0:T(8,128)(2,1)S(1)}) custom-call(bf16[4,4,192,128]{3,2,1,0:T(8,128)(2,1)S(1)} %all-to-all-done.1.gathered, f32[3,192,256]{2,1,0:T(8,128)} %get-tuple-element.27.early, bf16[1,2,128,1024]{3,2,1,0:T(8,128)(2,1)} %two.3, ...), custom_call_target="tpu_custom_call" | custom-call | flops 301989888 | bytes 3000000 | tf_op jit(solution)/shard_map/pallas_call | solution.py:72
  63.4 3.9 %collective-permute-done.5.before = bf16[2,192,128]{2,1,0:T(8,128)(2,1)S(1)} collective-permute-done((bf16[2,192,128]{2,1,0:T(8,128)(2,1)S(1)}, bf16[2,192,128]{2,1,0:T(8,128)(2,1)S(1)}, u32[]{:S(2)}, u32[]{:S(2)}) %collective-permute-start.5) | collective-permute-done | bytes 98336 | tf_op jit(solution)/shard_map/ppermute | solution.py:36
  67.3 0.0 all-to-all-done.2.centre
  67.3 0.5 shard_map.85
  67.8 5.0 %all-gather = bf16[8,192,128]{2,1,0:T(8,128)(2,1)S(1)} all-gather(bf16[4,192,128]{2,1,0:T(8,128)(2,1)S(1)} %get-tuple-element.33), channel_id=2, replica_groups={{0,1},{2,3},{4,5},{6,7},{8,9},{10,11},{12,13},{14,15},{16,17},{18,19},{..., dimensions={0}, use_global_device_ids=true | all-gather | bytes 589824 | tf_op jit(solution)/shard_map/all_gather | solution.py:427
  72.8 0.8 %shard_map.86 = (bf16[4,2,192,128]{3,2,1,0:T(8,128)(2,1)}, bf16[1,2,192,128]{3,2,1,0:T(8,128)(2,1)}) custom-call(bf16[2,4,192,128]{3,2,1,0:T(8,128)(2,1)S(1)} %bitcast.5, bf16[2,192,128]{2,1,0:T(8,128)(2,1)S(1)} %get-tuple-element.34.coarse, bf16[4,192,128]{2,1,0:T(8,128)(2,1)S(1)} %get-tuple-element.35.kept), custom_call_target="tpu_custom_call" | custom-call | flops 100663296 | bytes 1000000 | tf_op jit(solution)/shard_map/pallas_call | solution.py:72
Async XLA Ops:
  4.4 38.4 %collective-permute-start.2 = (bf16[11,128,1024]{2,1,0:T(8,128)(2,1)}, bf16[11,128,1024]{2,1,0:T(8,128)(2,1)}, u32[]{:S(2)}, u32[]{:S(2)}) collective-permute-start(bf16[11,128,1024]{2,1,0:T(8,128)(2,1)} %get-tuple-element.24), channel_id=1, source_target_pairs={{0,1},{1,0},{2,3},{3,2},{4,5},{5,4},{6,7},{7,6},{8,9},{9,8},{10,11... | collective-permute-start | bytes 8650760 | tf_op jit(solution)/shard_map/ppermute | solution.py:30
  9.1 4.7 %copy-start.3 = (bf16[3,128,1024]{2,1,0:T(8,128)(2,1)S(1)}, bf16[3,128,1024]{2,1,0:T(8,128)(2,1)}, u32[]{:S(2)}) copy-start(bf16[3,128,1024]{2,1,0:T(8,128)(2,1)} %get-tuple-element.20) | copy-start | bytes 2359300
  9.2 7.0 %copy-start.4 = (bf16[2,128,1024]{2,1,0:T(8,128)(2,1)S(1)}, bf16[2,128,1024]{2,1,0:T(8,128)(2,1)}, u32[]{:S(2)}) copy-start(bf16[2,128,1024]{2,1,0:T(8,128)(2,1)} %get-tuple-element.32) | copy-start | bytes 1572868
  9.2 24.5 %all-to-all-start = ((bf16[8,3,192,128]{3,2,1,0:T(8,128)(2,1)}), bf16[8,3,192,128]{3,2,1,0:T(8,128)(2,1)S(1)}, u32[]{:S(2)}, u32[]{:S(2)}) async-start(bf16[8,3,192,128]{3,2,1,0:T(8,128)(2,1)} %shard_map.77), calls=%async_computation | async-start | bytes 2359296 | tf_op jit(solution)/shard_map/all_to_all | solution.py:347
  13.9 6.5 %collective-permute-start = (bf16[3,128,1024]{2,1,0:T(8,128)(2,1)S(1)}, bf16[3,128,1024]{2,1,0:T(8,128)(2,1)S(1)}, u32[]{:S(2)}, u32[]{:S(2)}) collective-permute-start(bf16[3,128,1024]{2,1,0:T(8,128)(2,1)S(1)} %copy-done.3), channel_id=1, source_target_pairs={{0,1},{1,0},{2,3},{3,2},{4,5},{5,4},{6,7},{7,6},{8,9},{9,8},{10,11... | collective-permute-start | bytes 2359304 | tf_op jit(solution)/shard_map/ppermute | solution.py:30
  16.2 23.2 %collective-permute-start.3 = (bf16[2,128,1024]{2,1,0:T(8,128)(2,1)S(1)}, bf16[2,128,1024]{2,1,0:T(8,128)(2,1)}, u32[]{:S(2)}, u32[]{:S(2)}) collective-permute-start(bf16[2,128,1024]{2,1,0:T(8,128)(2,1)S(1)} %copy-done.4), channel_id=1, source_target_pairs={{8,0},{16,8},{24,16},{32,24},{40,32},{48,40},{56,48},{64,56},{72,6... | collective-permute-start | bytes 1572872 | tf_op jit(solution)/shard_map/ppermute | solution.py:36
  20.4 0.9 %copy-start.2 = (bf16[3,128,1024]{2,1,0:T(8,128)(2,1)}, bf16[3,128,1024]{2,1,0:T(8,128)(2,1)S(1)}, u32[]{:S(2)}) copy-start(bf16[3,128,1024]{2,1,0:T(8,128)(2,1)S(1)} %collective-permute-done.bundle.first) | copy-start | bytes 2359300
  22.7 10.9 %collective-permute-start.1 = (bf16[2,192,128]{2,1,0:T(8,128)(2,1)S(1)}, bf16[2,192,128]{2,1,0:T(8,128)(2,1)S(1)}, u32[]{:S(2)}, u32[]{:S(2)}) collective-permute-start(bf16[2,192,128]{2,1,0:T(8,128)(2,1)S(1)} %get-tuple-element.23), channel_id=1, source_target_pairs={{8,0},{16,8},{24,16},{32,24},{40,32},{48,40},{56,48},{64,56},{72,6... | collective-permute-start | bytes 294920 | tf_op jit(solution)/shard_map/ppermute | solution.py:36
  35.1 14.2 %all-to-all-start.1 = ((bf16[4,4,192,128]{3,2,1,0:T(8,128)(2,1)}), bf16[4,4,192,128]{3,2,1,0:T(8,128)(2,1)S(1)}, u32[]{:S(2)}, u32[]{:S(2)}) async-start(bf16[4,4,192,128]{3,2,1,0:T(8,128)(2,1)} %shard_map.80), calls=%async_computation.1 | async-start | bytes 1572864 | tf_op jit(solution)/shard_map/all_to_all | solution.py:25
  39.3 16.8 %collective-permute-start.4 = (bf16[2,128,1024]{2,1,0:T(8,128)(2,1)}, bf16[2,128,1024]{2,1,0:T(8,128)(2,1)S(1)}, u32[]{:S(2)}, u32[]{:S(2)}) collective-permute-start(bf16[2,128,1024]{2,1,0:T(8,128)(2,1)} %collective-permute-done.3.lifts), channel_id=1, source_target_pairs={{0,1},{1,0},{2,3},{3,2},{4,5},{5,4},{6,7},{7,6},{8,9},{9,8},{10,11... | collective-permute-start | bytes 1572872 | tf_op jit(solution)/shard_map/ppermute | solution.py:30
  47.0 0.7 copy-start
  49.3 0.9 %copy-start.1 = (f32[192,256]{1,0:T(8,128)S(1)}, f32[192,256]{1,0:T(8,128)}, u32[]{:S(2)}) copy-start(f32[192,256]{1,0:T(8,128)} %copy-done) | copy-start | bytes 589828
  51.5 15.8 %all-to-all-start.2 = ((bf16[4,2,192,128]{3,2,1,0:T(8,128)(2,1)}), bf16[4,2,192,128]{3,2,1,0:T(8,128)(2,1)S(1)}, u32[]{:S(2)}, u32[]{:S(2)}) async-start(bf16[4,2,192,128]{3,2,1,0:T(8,128)(2,1)} %shard_map.82), calls=%async_computation.2 | async-start | bytes 786432 | tf_op jit(solution)/shard_map/all_to_all | solution.py:25
  57.8 9.4 %collective-permute-start.5 = (bf16[2,192,128]{2,1,0:T(8,128)(2,1)S(1)}, bf16[2,192,128]{2,1,0:T(8,128)(2,1)S(1)}, u32[]{:S(2)}, u32[]{:S(2)}) collective-permute-start(bf16[2,192,128]{2,1,0:T(8,128)(2,1)S(1)} %shard_map.84), channel_id=1, source_target_pairs={{0,8},{8,16},{16,24},{24,32},{32,40},{40,48},{48,56},{56,64},{64,7... | collective-permute-start | bytes 294920 | tf_op jit(solution)/shard_map/ppermute | solution.py:36

commit v7 on v6

--- a/solution.py
+++ b/solution.py
@@ -222,12 +222,13 @@
         pieces.load(strip_of(bundle, STRIPS * which + j), place)
 
 
-def prepare_body(one, bundle, sides, coarse, matrices, begun, coarse_pair, sems):
+def prepare_body(one, sides, coarse, bundle, matrices, begun, coarse_pair, sems):
     pieces, mine = Pieces(sems), core()
     load_half(pieces, coarse.at[0, mine], bundle, 0, coarse_pair)
     for i in range(2):
         pieces.both(one.at[1, i], bundle.at[i], matrices.at[i])
-    load_half(pieces, sides.at[2, mine], bundle, 2, begun)
+    for i in range(2):
+        load_half(pieces, sides.at[2 * i, mine], bundle, 1 + i, begun.at[i])
     pieces.wait()
 
 
@@ -237,7 +238,7 @@
     spread(
         copies,
         [
-            (begun[i].astype(F32) - part).astype(BF16)
+            (begun[1, i].astype(F32) - part).astype(BF16)
             for i, part in enumerate(own_and_partner(total))
         ],
     )
@@ -299,14 +300,14 @@
 
 
 def reduced_body(
-    gathered, early, two, solve, sides, coarse, first, second,
+    gathered, early, two, solve, coarse, second, sides_begun,
     total, matrices, begun, kept, held, sides_held, early_held, sems,
 ):
     pieces = Pieces(sems)
     pieces.both(two.at[0, 1], second.at[1], held.at[0])
     pieces.both(solve.at[1, 2], second.at[10], held.at[1])
     pieces.load(early, early_held)
-    load_half(pieces, sides.at[0, core()], first, 1, sides_held)
+    pieces.load(sides_begun.at[0], sides_held)
     pieces.both(solve.at[0, 2], second.at[7], matrices.at[0])
     pieces.both(solve.at[1, 1], second.at[9], matrices.at[1])
     pieces.load(coarse.at[0], kept)
@@ -354,12 +355,13 @@
         prepare_body,
         [
             (IN_VMEM, (2, *MERGED), BF16),
+            (IN_VMEM, (2, *PAIR), BF16),
             (IN_VMEM, PAIR, BF16),
-            (IN_VMEM, PAIR, BF16),
         ],
         [],
-        [lift_one, first, sides, coarse],
-        copies=14,
+        [lift_one, sides, coarse],
+        free=[first],
+        copies=19,
     )
     following = passed_along(coarse_pair, -1)
     lifts_next = passed_along(lifts, -1)
@@ -412,9 +414,10 @@
             (IN_VMEM, PAIR, BF16),
         ],
         [gathered],
-        [early, lift_two, solve_one, sides, coarse, first, second],
+        [early, lift_two, solve_one, coarse, second],
         [((2, *MERGED), BF16), (PAIR, BF16), ((3, *flat), F32)],
-        copies=15,
+        free=[begun],
+        copies=11,
         products=3,
     )
     kept, given = call(

time: 74.2 us -> 73.4 us (0.989)
  local copies, waits for them, and re-layouts: 2.47 us -> 0.01 us
  waiting for transfers between devices: 13.5 us -> 15.2 us
    unnamed x10 -> x4, local copies, waits for them, and re-layouts: 2.47 us -> 0.01 us
    ppermute x3, waiting for transfers between devices: 11.8 us -> 12.9 us  [passed_along(): return lax.ppermute(array, 'rad', pairs)]
where the time goes in v7:
time: 73.4 us; the launch traced here: 72.8 us
  starting transfers between devices  32.1 us (44%)
  Pallas kernels  19.7 us (27%)
  waiting for transfers between devices  15.2 us (21%)
  blocking collectives  4.97 us (7%)
  between operations  0.79 us (1%)
    pallas_call x8, Pallas kernels, call(): pl.pallas_call(body, out_shape=[space(shape, dtype) for space, shape, dty...  13.7 us
    ppermute x3, waiting for transfers between devices, passed_along(): return lax.ppermute(array, 'rad', pairs)  12.9 us
    ppermute x3, starting transfers between devices, passed_along(): return lax.ppermute(array, 'rad', pairs)  10.3 us
    all_to_all x2, starting transfers between devices, over_chips(): return lax.all_to_all(copies, 'col', 0, 0, axis_index_groups=groups)  8.87 us
    ppermute x3, starting transfers between devices, from_partner(): return lax.ppermute(array, 'col', [(i, i ^ 1) for i in range(peers)])  8.3 us
    all_gather x1, blocking collectives, steps(): taken = lax.all_gather(given, 'col', axis=0, axis_index_groups=cores)  4.97 us
    all_to_all x1, starting transfers between devices, steps(): odd = lax.all_to_all(packed, 'col', 0, 0)  4.69 us
    pallas_call x1, Pallas kernels, bundled(): pl.pallas_call(bundle_body, out_shape=[pltpu.HBM(shape, BF16) for shape i...  3.74 us
  transfers between devices with their start and end apart: 9, of which 3 were waited for; matrix products, arithmetic and copies ran while one was open for 0% of the time, Pallas kernels for 20%

profile of v7, /device:TPU:259, one launch (start us, length us, event | category | flops | bytes accessed | tf_op | source)
XLA Modules:
  0.0 72.8 jit_solution(3048841981501283365)
XLA Ops:
  0.6 3.7 %shard_map.78 = (bf16[3,128,1024]{2,1,0:T(8,128)(2,1)}, bf16[11,128,1024]{2,1,0:T(8,128)(2,1)}, bf16[2,128,1024]{2,1,0:T(8,128)(2,1)}) custom-call(bf16[2,2,128,1024]{3,2,1,0:T(8,128)(2,1)} %one.5, bf16[1,2,128,1024]{3,2,1,0:T(8,128)(2,1)} %two.3, bf16[2,3,128,1024]{3,2,1,0:T(8,128)(2,1)} %solve.3, bf16[1,3,128,1024]{3,2,1,0:T(8,128)(2,1)} %last.1, ...), custom_call_target="tpu_custom_call" | custom-call | bytes 9000000 | tf_op jit(solution)/shard_map/pallas_call | solution.py:201
  4.4 2.6 %collective-permute-start.2 = (bf16[11,128,1024]{2,1,0:T(8,128)(2,1)}, bf16[11,128,1024]{2,1,0:T(8,128)(2,1)}, u32[]{:S(2)}, u32[]{:S(2)}) collective-permute-start(bf16[11,128,1024]{2,1,0:T(8,128)(2,1)} %get-tuple-element.24), channel_id=1, source_target_pairs={{0,1},{1,0},{2,3},{3,2},{4,5},{5,4},{6,7},{7,6},{8,9},{9,8},{10,11... | collective-permute-start | bytes 8650760 | tf_op jit(solution)/shard_map/ppermute | solution.py:30
  7.0 2.2 %shard_map.77 = bf16[8,3,192,128]{3,2,1,0:T(8,128)(2,1)} custom-call(bf16[4,2,192,128]{3,2,1,0:T(8,128)(2,1)} %bitcast.7, bf16[1,2,192,128]{3,2,1,0:T(8,128)(2,1)} %bitcast.10), custom_call_target="tpu_custom_call" | custom-call | tf_op jit(solution)/shard_map/pallas_call | solution.py:133
  9.2 0.0 copy-start
  9.2 0.0 copy-start.1
  9.2 4.7 %all-to-all-start = ((bf16[8,3,192,128]{3,2,1,0:T(8,128)(2,1)}), bf16[8,3,192,128]{3,2,1,0:T(8,128)(2,1)S(1)}, u32[]{:S(2)}, u32[]{:S(2)}) async-start(bf16[8,3,192,128]{3,2,1,0:T(8,128)(2,1)} %shard_map.77), calls=%async_computation | async-start | bytes 2359296 | tf_op jit(solution)/shard_map/all_to_all | solution.py:348
  13.9 0.0 copy-done
  13.9 2.3 %collective-permute-start = (bf16[3,128,1024]{2,1,0:T(8,128)(2,1)S(1)}, bf16[3,128,1024]{2,1,0:T(8,128)(2,1)S(1)}, u32[]{:S(2)}, u32[]{:S(2)}) collective-permute-start(bf16[3,128,1024]{2,1,0:T(8,128)(2,1)S(1)} %copy-done), channel_id=1, source_target_pairs={{0,1},{1,0},{2,3},{3,2},{4,5},{5,4},{6,7},{7,6},{8,9},{9,8},{10,11... | collective-permute-start | bytes 2359304 | tf_op jit(solution)/shard_map/ppermute | solution.py:30
  16.2 0.0 copy-done.1
  16.2 4.2 %collective-permute-start.3 = (bf16[2,128,1024]{2,1,0:T(8,128)(2,1)S(1)}, bf16[2,128,1024]{2,1,0:T(8,128)(2,1)}, u32[]{:S(2)}, u32[]{:S(2)}) collective-permute-start(bf16[2,128,1024]{2,1,0:T(8,128)(2,1)S(1)} %copy-done.1), channel_id=1, source_target_pairs={{8,0},{16,8},{24,16},{32,24},{40,32},{48,40},{56,48},{64,56},{72,6... | collective-permute-start | bytes 1572872 | tf_op jit(solution)/shard_map/ppermute | solution.py:36
  20.4 0.0 collective-permute-done.bundle
  20.4 1.3 %shard_map.79 = (bf16[2,256,1024]{2,1,0:T(8,128)(2,1)S(1)}, bf16[2,2,192,128]{3,2,1,0:T(8,128)(2,1)S(1)}, bf16[2,192,128]{2,1,0:T(8,128)(2,1)S(1)}) custom-call(bf16[2,2,128,1024]{3,2,1,0:T(8,128)(2,1)} %one.5, bf16[4,2,192,128]{3,2,1,0:T(8,128)(2,1)} %bitcast.8, bf16[1,2,192,128]{3,2,1,0:T(8,128)(2,1)} %bitcast.11, ...), custom_call_target="tpu_custom_call" | custom-call | flops 100663296 | bytes 1000000 | tf_op jit(solution)/shard_map/pallas_call | solution.py:72
  21.7 3.0 %collective-permute-start.1 = (bf16[2,192,128]{2,1,0:T(8,128)(2,1)S(1)}, bf16[2,192,128]{2,1,0:T(8,128)(2,1)S(1)}, u32[]{:S(2)}, u32[]{:S(2)}) collective-permute-start(bf16[2,192,128]{2,1,0:T(8,128)(2,1)S(1)} %get-tuple-element.23), channel_id=1, source_target_pairs={{8,0},{16,8},{24,16},{32,24},{40,32},{48,40},{56,48},{64,56},{72,6... | collective-permute-start | bytes 294920 | tf_op jit(solution)/shard_map/ppermute | solution.py:36
  24.7 9.0 %collective-permute-done.1.following = bf16[2,192,128]{2,1,0:T(8,128)(2,1)S(1)} collective-permute-done((bf16[2,192,128]{2,1,0:T(8,128)(2,1)S(1)}, bf16[2,192,128]{2,1,0:T(8,128)(2,1)S(1)}, u32[]{:S(2)}, u32[]{:S(2)}) %collective-permute-start.1) | collective-permute-done | bytes 98336 | tf_op jit(solution)/shard_map/ppermute | solution.py:36
  33.7 0.0 all-to-all-done.odd
  33.7 1.4 %shard_map.80 = bf16[4,4,192,128]{3,2,1,0:T(8,128)(2,1)} custom-call(bf16[8,3,192,128]{3,2,1,0:T(8,128)(2,1)S(1)} %all-to-all-done.odd, bf16[2,256,1024]{2,1,0:T(8,128)(2,1)S(1)} %get-tuple-element.21.matrices, bf16[2,2,192,128]{3,2,1,0:T(8,128)(2,1)S(1)} %get-tuple-element.22.begun.sides_begun, bf16[2,192,128]{2,1,0:T(8,128)(2,1)S(1)} %collective-permute-done.1.following), custom_call_target="tpu_custom_call" | custom-call | flops 201326592 | bytes 2000000 | tf_op jit(solution)/shard_map/pallas_call | solution.py:72
  35.1 4.2 %all-to-all-start.1 = ((bf16[4,4,192,128]{3,2,1,0:T(8,128)(2,1)}), bf16[4,4,192,128]{3,2,1,0:T(8,128)(2,1)S(1)}, u32[]{:S(2)}, u32[]{:S(2)}) async-start(bf16[4,4,192,128]{3,2,1,0:T(8,128)(2,1)} %shard_map.80), calls=%async_computation.1 | async-start | bytes 1572864 | tf_op jit(solution)/shard_map/all_to_all | solution.py:25
  39.4 0.0 collective-permute-done.3.lifts
  39.4 3.4 %collective-permute-start.4 = (bf16[2,128,1024]{2,1,0:T(8,128)(2,1)}, bf16[2,128,1024]{2,1,0:T(8,128)(2,1)}, u32[]{:S(2)}, u32[]{:S(2)}) collective-permute-start(bf16[2,128,1024]{2,1,0:T(8,128)(2,1)} %collective-permute-done.3.lifts), channel_id=1, source_target_pairs={{0,1},{1,0},{2,3},{3,2},{4,5},{5,4},{6,7},{7,6},{8,9},{9,8},{10,11... | collective-permute-start | bytes 1572872 | tf_op jit(solution)/shard_map/ppermute | solution.py:30
  42.8 0.0 collective-permute-done.2.bundle.second
  42.8 4.2 %shard_map.81 = (bf16[2,256,1024]{2,1,0:T(8,128)(2,1)S(1)}, f32[192,256]{1,0:T(8,128)S(1)}, f32[3,192,256]{2,1,0:T(8,128)}, bf16[192,1024]{1,0:T(8,128)(2,1)}) custom-call(bf16[8,3,192,128]{3,2,1,0:T(8,128)(2,1)S(1)} %all-to-all-done.odd, bf16[2,2,128,1024]{3,2,1,0:T(8,128)(2,1)} %one.5, bf16[2,3,128,1024]{3,2,1,0:T(8,128)(2,1)} %solve.3, ...), custom_call_target="tpu_custom_call" | custom-call | flops 503316480 | bytes 5000000 | tf_op jit(solution)/shard_map/pallas_call | solution.py:72
  47.0 2.3 %all-to-all-done.1.gathered = bf16[4,4,192,128]{3,2,1,0:T(8,128)(2,1)S(1)} async-done(((bf16[4,4,192,128]{3,2,1,0:T(8,128)(2,1)}), bf16[4,4,192,128]{3,2,1,0:T(8,128)(2,1)S(1)}, u32[]{:S(2)}, u32[]{:S(2)}) %all-to-all-start.1) | async-done | bytes 786464 | tf_op jit(solution)/shard_map/all_to_all | solution.py:25
  49.3 1.3 %shard_map.82 = bf16[4,2,192,128]{3,2,1,0:T(8,128)(2,1)} custom-call(bf16[4,4,192,128]{3,2,1,0:T(8,128)(2,1)S(1)} %all-to-all-done.1.gathered, bf16[2,256,1024]{2,1,0:T(8,128)(2,1)S(1)} %get-tuple-element.25.inverses, f32[192,256]{1,0:T(8,128)S(1)} %get-tuple-element.26.coarse), custom_call_target="tpu_custom_call" | custom-call | flops 201326592 | bytes 2000000 | tf_op jit(solution)/shard_map/pallas_call | solution.py:72
  50.6 4.6 %all-to-all-start.2 = ((bf16[4,2,192,128]{3,2,1,0:T(8,128)(2,1)}), bf16[4,2,192,128]{3,2,1,0:T(8,128)(2,1)S(1)}, u32[]{:S(2)}, u32[]{:S(2)}) async-start(bf16[4,2,192,128]{3,2,1,0:T(8,128)(2,1)} %shard_map.82), calls=%async_computation.2 | async-start | bytes 786432 | tf_op jit(solution)/shard_map/all_to_all | solution.py:25
  55.2 0.0 collective-permute-done.4.lifts_partner
  55.2 1.9 %shard_map.84 = bf16[2,192,128]{2,1,0:T(8,128)(2,1)S(1)} custom-call(bf16[4,4,192,128]{3,2,1,0:T(8,128)(2,1)S(1)} %all-to-all-done.1.gathered, bf16[192,1024]{1,0:T(8,128)(2,1)} %get-tuple-element.31.fourth, bf16[2,128,1024]{2,1,0:T(8,128)(2,1)} %collective-permute-done.3.lifts, bf16[2,128,1024]{2,1,0:T(8,128)(2,1)} %collective-permute-done.4.lifts_partner), custom_call_target="tpu_custom_call" | custom-call | flops 100663296 | bytes 1000000 | tf_op jit(solution)/shard_map/pallas_call | solution.py:72
  57.1 3.1 %collective-permute-start.5 = (bf16[2,192,128]{2,1,0:T(8,128)(2,1)S(1)}, bf16[2,192,128]{2,1,0:T(8,128)(2,1)S(1)}, u32[]{:S(2)}, u32[]{:S(2)}) collective-permute-start(bf16[2,192,128]{2,1,0:T(8,128)(2,1)S(1)} %shard_map.84), channel_id=1, source_target_pairs={{0,8},{8,16},{16,24},{24,32},{32,40},{40,48},{48,56},{56,64},{64,7... | collective-permute-start | bytes 294920 | tf_op jit(solution)/shard_map/ppermute | solution.py:36
  60.2 2.4 %shard_map.83 = (f32[2,192,128]{2,1,0:T(8,128)S(1)}, bf16[2,256,1024]{2,1,0:T(8,128)(2,1)S(1)}, f32[2,192,256]{2,1,0:T(8,128)S(1)}, bf16[2,192,128]{2,1,0:T(8,128)(2,1)S(1)}) custom-call(bf16[4,4,192,128]{3,2,1,0:T(8,128)(2,1)S(1)} %all-to-all-done.1.gathered, f32[3,192,256]{2,1,0:T(8,128)} %get-tuple-element.27.early, bf16[1,2,128,1024]{3,2,1,0:T(8,128)(2,1)} %two.3, ...), custom_call_target="tpu_custom_call" | custom-call | flops 301989888 | bytes 3000000 | tf_op jit(solution)/shard_map/pallas_call | solution.py:72
  62.6 3.9 %collective-permute-done.5.before = bf16[2,192,128]{2,1,0:T(8,128)(2,1)S(1)} collective-permute-done((bf16[2,192,128]{2,1,0:T(8,128)(2,1)S(1)}, bf16[2,192,128]{2,1,0:T(8,128)(2,1)S(1)}, u32[]{:S(2)}, u32[]{:S(2)}) %collective-permute-start.5) | collective-permute-done | bytes 98336 | tf_op jit(solution)/shard_map/ppermute | solution.py:36
  66.5 0.0 all-to-all-done.2.centre
  66.5 0.5 shard_map.85
  67.0 5.0 %all-gather = bf16[8,192,128]{2,1,0:T(8,128)(2,1)S(1)} all-gather(bf16[4,192,128]{2,1,0:T(8,128)(2,1)S(1)} %get-tuple-element.33), channel_id=2, replica_groups={{0,1},{2,3},{4,5},{6,7},{8,9},{10,11},{12,13},{14,15},{16,17},{18,19},{..., dimensions={0}, use_global_device_ids=true | all-gather | bytes 589824 | tf_op jit(solution)/shard_map/all_gather | solution.py:430
  72.0 0.8 %shard_map.86 = (bf16[4,2,192,128]{3,2,1,0:T(8,128)(2,1)}, bf16[1,2,192,128]{3,2,1,0:T(8,128)(2,1)}) custom-call(bf16[2,4,192,128]{3,2,1,0:T(8,128)(2,1)S(1)} %bitcast.5, bf16[2,192,128]{2,1,0:T(8,128)(2,1)S(1)} %get-tuple-element.34.coarse, bf16[4,192,128]{2,1,0:T(8,128)(2,1)S(1)} %get-tuple-element.35.kept), custom_call_target="tpu_custom_call" | custom-call | flops 100663296 | bytes 1000000 | tf_op jit(solution)/shard_map/pallas_call | solution.py:72
Async XLA Ops:
  4.4 38.4 %collective-permute-start.2 = (bf16[11,128,1024]{2,1,0:T(8,128)(2,1)}, bf16[11,128,1024]{2,1,0:T(8,128)(2,1)}, u32[]{:S(2)}, u32[]{:S(2)}) collective-permute-start(bf16[11,128,1024]{2,1,0:T(8,128)(2,1)} %get-tuple-element.24), channel_id=1, source_target_pairs={{0,1},{1,0},{2,3},{3,2},{4,5},{5,4},{6,7},{7,6},{8,9},{9,8},{10,11... | collective-permute-start | bytes 8650760 | tf_op jit(solution)/shard_map/ppermute | solution.py:30
  9.2 4.7 %copy-start = (bf16[3,128,1024]{2,1,0:T(8,128)(2,1)S(1)}, bf16[3,128,1024]{2,1,0:T(8,128)(2,1)}, u32[]{:S(2)}) copy-start(bf16[3,128,1024]{2,1,0:T(8,128)(2,1)} %get-tuple-element.20) | copy-start | bytes 2359300
  9.2 7.0 %copy-start.1 = (bf16[2,128,1024]{2,1,0:T(8,128)(2,1)S(1)}, bf16[2,128,1024]{2,1,0:T(8,128)(2,1)}, u32[]{:S(2)}) copy-start(bf16[2,128,1024]{2,1,0:T(8,128)(2,1)} %get-tuple-element.32) | copy-start | bytes 1572868
  9.2 24.5 %all-to-all-start = ((bf16[8,3,192,128]{3,2,1,0:T(8,128)(2,1)}), bf16[8,3,192,128]{3,2,1,0:T(8,128)(2,1)S(1)}, u32[]{:S(2)}, u32[]{:S(2)}) async-start(bf16[8,3,192,128]{3,2,1,0:T(8,128)(2,1)} %shard_map.77), calls=%async_computation | async-start | bytes 2359296 | tf_op jit(solution)/shard_map/all_to_all | solution.py:348
  13.9 6.5 %collective-permute-start = (bf16[3,128,1024]{2,1,0:T(8,128)(2,1)S(1)}, bf16[3,128,1024]{2,1,0:T(8,128)(2,1)S(1)}, u32[]{:S(2)}, u32[]{:S(2)}) collective-permute-start(bf16[3,128,1024]{2,1,0:T(8,128)(2,1)S(1)} %copy-done), channel_id=1, source_target_pairs={{0,1},{1,0},{2,3},{3,2},{4,5},{5,4},{6,7},{7,6},{8,9},{9,8},{10,11... | collective-permute-start | bytes 2359304 | tf_op jit(solution)/shard_map/ppermute | solution.py:30
  16.2 23.2 %collective-permute-start.3 = (bf16[2,128,1024]{2,1,0:T(8,128)(2,1)S(1)}, bf16[2,128,1024]{2,1,0:T(8,128)(2,1)}, u32[]{:S(2)}, u32[]{:S(2)}) collective-permute-start(bf16[2,128,1024]{2,1,0:T(8,128)(2,1)S(1)} %copy-done.1), channel_id=1, source_target_pairs={{8,0},{16,8},{24,16},{32,24},{40,32},{48,40},{56,48},{64,56},{72,6... | collective-permute-start | bytes 1572872 | tf_op jit(solution)/shard_map/ppermute | solution.py:36
  21.7 12.0 %collective-permute-start.1 = (bf16[2,192,128]{2,1,0:T(8,128)(2,1)S(1)}, bf16[2,192,128]{2,1,0:T(8,128)(2,1)S(1)}, u32[]{:S(2)}, u32[]{:S(2)}) collective-permute-start(bf16[2,192,128]{2,1,0:T(8,128)(2,1)S(1)} %get-tuple-element.23), channel_id=1, source_target_pairs={{8,0},{16,8},{24,16},{32,24},{40,32},{48,40},{56,48},{64,56},{72,6... | collective-permute-start | bytes 294920 | tf_op jit(solution)/shard_map/ppermute | solution.py:36
  35.1 14.2 %all-to-all-start.1 = ((bf16[4,4,192,128]{3,2,1,0:T(8,128)(2,1)}), bf16[4,4,192,128]{3,2,1,0:T(8,128)(2,1)S(1)}, u32[]{:S(2)}, u32[]{:S(2)}) async-start(bf16[4,4,192,128]{3,2,1,0:T(8,128)(2,1)} %shard_map.80), calls=%async_computation.1 | async-start | bytes 1572864 | tf_op jit(solution)/shard_map/all_to_all | solution.py:25
  39.4 15.9 %collective-permute-start.4 = (bf16[2,128,1024]{2,1,0:T(8,128)(2,1)}, bf16[2,128,1024]{2,1,0:T(8,128)(2,1)}, u32[]{:S(2)}, u32[]{:S(2)}) collective-permute-start(bf16[2,128,1024]{2,1,0:T(8,128)(2,1)} %collective-permute-done.3.lifts), channel_id=1, source_target_pairs={{0,1},{1,0},{2,3},{3,2},{4,5},{5,4},{6,7},{7,6},{8,9},{9,8},{10,11... | collective-permute-start | bytes 1572872 | tf_op jit(solution)/shard_map/ppermute | solution.py:30
  50.6 15.9 %all-to-all-start.2 = ((bf16[4,2,192,128]{3,2,1,0:T(8,128)(2,1)}), bf16[4,2,192,128]{3,2,1,0:T(8,128)(2,1)S(1)}, u32[]{:S(2)}, u32[]{:S(2)}) async-start(bf16[4,2,192,128]{3,2,1,0:T(8,128)(2,1)} %shard_map.82), calls=%async_computation.2 | async-start | bytes 786432 | tf_op jit(solution)/shard_map/all_to_all | solution.py:25
  57.1 9.4 %collective-permute-start.5 = (bf16[2,192,128]{2,1,0:T(8,128)(2,1)S(1)}, bf16[2,192,128]{2,1,0:T(8,128)(2,1)S(1)}, u32[]{:S(2)}, u32[]{:S(2)}) collective-permute-start(bf16[2,192,128]{2,1,0:T(8,128)(2,1)S(1)} %shard_map.84), channel_id=1, source_target_pairs={{0,8},{8,16},{16,24},{24,32},{32,40},{40,48},{48,56},{56,64},{64,7... | collective-permute-start | bytes 294920 | tf_op jit(solution)/shard_map/ppermute | solution.py:36

commit v8 on v7

--- a/solution.py
+++ b/solution.py
@@ -111,18 +111,20 @@
 def pack_body(sides, coarse, packed, held, arrived, sent):
     arrays = [sides.at[1], sides.at[3], coarse.at[0]]
     loads = [
-        pltpu.make_async_copy(array, held.at[i], arrived.at[i])
-        for i, array in enumerate(arrays)
+        [
+            pltpu.make_async_copy(array.at[half], held.at[half, i], arrived.at[half, i])
+            for i, array in enumerate(arrays)
+        ]
+        for half in range(2)
     ]
-    for load in loads:
+    for load in loads[0] + loads[1]:
         load.start()
     stores = []
-    for i, load in enumerate(loads):
-        load.wait()
-        for peer in range(8):
-            store = pltpu.make_async_copy(
-                held.at[i, peer % 2], packed.at[peer, i], sent.at[i, peer]
-            )
+    for half in range(2):
+        for load in loads[half]:
+            load.wait()
+        for peer in range(half, 8, 2):
+            store = pltpu.make_async_copy(held.at[half], packed.at[peer], sent.at[peer])
             store.start()
             stores.append(store)
     for store in stores:
@@ -136,9 +138,9 @@
         in_specs=[HBM, HBM],
         out_specs=HBM,
         scratch_shapes=[
-            pltpu.VMEM((3, 2, HALF, WIDTH), BF16),
-            pltpu.SemaphoreType.DMA((3,)),
-            pltpu.SemaphoreType.DMA((3, 8)),
+            pltpu.VMEM((2, 3, HALF, WIDTH), BF16),
+            pltpu.SemaphoreType.DMA((2, 3)),
+            pltpu.SemaphoreType.DMA((8,)),
         ],
         compiler_params=pltpu.CompilerParams(vmem_limit_bytes=4 << 20),
     )(

time: 73.4 us -> 73.3 us (level)
  no operation moved by 1% of the time
where the time goes in v8:
time: 73.3 us; the launch traced here: 72.7 us
  starting transfers between devices  32.2 us (44%)
  Pallas kernels  19.5 us (27%)
  waiting for transfers between devices  15.2 us (21%)
  blocking collectives  4.97 us (7%)
  between operations  0.79 us (1%)
    pallas_call x8, Pallas kernels, call(): pl.pallas_call(body, out_shape=[space(shape, dtype) for space, shape, dty...  13.7 us
    ppermute x3, waiting for transfers between devices, passed_along(): return lax.ppermute(array, 'rad', pairs)  12.9 us
    ppermute x3, starting transfers between devices, passed_along(): return lax.ppermute(array, 'rad', pairs)  10.3 us
    all_to_all x2, starting transfers between devices, over_chips(): return lax.all_to_all(copies, 'col', 0, 0, axis_index_groups=groups)  8.86 us
    ppermute x3, starting transfers between devices, from_partner(): return lax.ppermute(array, 'col', [(i, i ^ 1) for i in range(peers)])  8.3 us
    all_gather x1, blocking collectives, steps(): taken = lax.all_gather(given, 'col', axis=0, axis_index_groups=cores)  4.97 us
    all_to_all x1, starting transfers between devices, steps(): odd = lax.all_to_all(packed, 'col', 0, 0)  4.69 us
    pallas_call x1, Pallas kernels, bundled(): pl.pallas_call(bundle_body, out_shape=[pltpu.HBM(shape, BF16) for shape i...  3.74 us
  transfers between devices with their start and end apart: 9, of which 3 were waited for; matrix products, arithmetic and copies ran while one was open for 0% of the time, Pallas kernels for 20%

profile of v8, /device:TPU:259, one launch (start us, length us, event | category | flops | bytes accessed | tf_op | source)
XLA Modules:
  0.0 72.7 jit_solution(6206995572158268982)
XLA Ops:
  0.6 3.7 %shard_map.78 = (bf16[3,128,1024]{2,1,0:T(8,128)(2,1)}, bf16[11,128,1024]{2,1,0:T(8,128)(2,1)}, bf16[2,128,1024]{2,1,0:T(8,128)(2,1)}) custom-call(bf16[2,2,128,1024]{3,2,1,0:T(8,128)(2,1)} %one.5, bf16[1,2,128,1024]{3,2,1,0:T(8,128)(2,1)} %two.3, bf16[2,3,128,1024]{3,2,1,0:T(8,128)(2,1)} %solve.3, bf16[1,3,128,1024]{3,2,1,0:T(8,128)(2,1)} %last.1, ...), custom_call_target="tpu_custom_call" | custom-call | bytes 9000000 | tf_op jit(solution)/shard_map/pallas_call | solution.py:203
  4.4 2.6 %collective-permute-start.2 = (bf16[11,128,1024]{2,1,0:T(8,128)(2,1)}, bf16[11,128,1024]{2,1,0:T(8,128)(2,1)}, u32[]{:S(2)}, u32[]{:S(2)}) collective-permute-start(bf16[11,128,1024]{2,1,0:T(8,128)(2,1)} %get-tuple-element.24), channel_id=1, source_target_pairs={{0,1},{1,0},{2,3},{3,2},{4,5},{5,4},{6,7},{7,6},{8,9},{9,8},{10,11... | collective-permute-start | bytes 8650760 | tf_op jit(solution)/shard_map/ppermute | solution.py:30
  7.0 2.0 %shard_map.77 = bf16[8,3,192,128]{3,2,1,0:T(8,128)(2,1)} custom-call(bf16[4,2,192,128]{3,2,1,0:T(8,128)(2,1)} %bitcast.7, bf16[1,2,192,128]{3,2,1,0:T(8,128)(2,1)} %bitcast.10), custom_call_target="tpu_custom_call" | custom-call | tf_op jit(solution)/shard_map/pallas_call | solution.py:135
  9.0 0.0 copy-start
  9.0 0.0 copy-start.1
  9.0 4.7 %all-to-all-start = ((bf16[8,3,192,128]{3,2,1,0:T(8,128)(2,1)}), bf16[8,3,192,128]{3,2,1,0:T(8,128)(2,1)S(1)}, u32[]{:S(2)}, u32[]{:S(2)}) async-start(bf16[8,3,192,128]{3,2,1,0:T(8,128)(2,1)} %shard_map.77), calls=%async_computation | async-start | bytes 2359296 | tf_op jit(solution)/shard_map/all_to_all | solution.py:350
  13.7 0.0 copy-done
  13.7 2.3 %collective-permute-start = (bf16[3,128,1024]{2,1,0:T(8,128)(2,1)S(1)}, bf16[3,128,1024]{2,1,0:T(8,128)(2,1)S(1)}, u32[]{:S(2)}, u32[]{:S(2)}) collective-permute-start(bf16[3,128,1024]{2,1,0:T(8,128)(2,1)S(1)} %copy-done), channel_id=1, source_target_pairs={{0,1},{1,0},{2,3},{3,2},{4,5},{5,4},{6,7},{7,6},{8,9},{9,8},{10,11... | collective-permute-start | bytes 2359304 | tf_op jit(solution)/shard_map/ppermute | solution.py:30
  16.0 0.0 copy-done.1
  16.0 4.2 %collective-permute-start.3 = (bf16[2,128,1024]{2,1,0:T(8,128)(2,1)S(1)}, bf16[2,128,1024]{2,1,0:T(8,128)(2,1)}, u32[]{:S(2)}, u32[]{:S(2)}) collective-permute-start(bf16[2,128,1024]{2,1,0:T(8,128)(2,1)S(1)} %copy-done.1), channel_id=1, source_target_pairs={{8,0},{16,8},{24,16},{32,24},{40,32},{48,40},{56,48},{64,56},{72,6... | collective-permute-start | bytes 1572872 | tf_op jit(solution)/shard_map/ppermute | solution.py:36
  20.2 0.0 collective-permute-done.bundle
  20.2 1.3 %shard_map.79 = (bf16[2,256,1024]{2,1,0:T(8,128)(2,1)S(1)}, bf16[2,2,192,128]{3,2,1,0:T(8,128)(2,1)S(1)}, bf16[2,192,128]{2,1,0:T(8,128)(2,1)S(1)}) custom-call(bf16[2,2,128,1024]{3,2,1,0:T(8,128)(2,1)} %one.5, bf16[4,2,192,128]{3,2,1,0:T(8,128)(2,1)} %bitcast.8, bf16[1,2,192,128]{3,2,1,0:T(8,128)(2,1)} %bitcast.11, ...), custom_call_target="tpu_custom_call" | custom-call | flops 100663296 | bytes 1000000 | tf_op jit(solution)/shard_map/pallas_call | solution.py:72
  21.5 3.0 %collective-permute-start.1 = (bf16[2,192,128]{2,1,0:T(8,128)(2,1)S(1)}, bf16[2,192,128]{2,1,0:T(8,128)(2,1)S(1)}, u32[]{:S(2)}, u32[]{:S(2)}) collective-permute-start(bf16[2,192,128]{2,1,0:T(8,128)(2,1)S(1)} %get-tuple-element.23), channel_id=1, source_target_pairs={{8,0},{16,8},{24,16},{32,24},{40,32},{48,40},{56,48},{64,56},{72,6... | collective-permute-start | bytes 294920 | tf_op jit(solution)/shard_map/ppermute | solution.py:36
  24.5 9.0 %collective-permute-done.1.following = bf16[2,192,128]{2,1,0:T(8,128)(2,1)S(1)} collective-permute-done((bf16[2,192,128]{2,1,0:T(8,128)(2,1)S(1)}, bf16[2,192,128]{2,1,0:T(8,128)(2,1)S(1)}, u32[]{:S(2)}, u32[]{:S(2)}) %collective-permute-start.1) | collective-permute-done | bytes 98336 | tf_op jit(solution)/shard_map/ppermute | solution.py:36
  33.5 0.0 all-to-all-done.odd
  33.5 1.4 %shard_map.80 = bf16[4,4,192,128]{3,2,1,0:T(8,128)(2,1)} custom-call(bf16[8,3,192,128]{3,2,1,0:T(8,128)(2,1)S(1)} %all-to-all-done.odd, bf16[2,256,1024]{2,1,0:T(8,128)(2,1)S(1)} %get-tuple-element.21.matrices, bf16[2,2,192,128]{3,2,1,0:T(8,128)(2,1)S(1)} %get-tuple-element.22.begun.sides_begun, bf16[2,192,128]{2,1,0:T(8,128)(2,1)S(1)} %collective-permute-done.1.following), custom_call_target="tpu_custom_call" | custom-call | flops 201326592 | bytes 2000000 | tf_op jit(solution)/shard_map/pallas_call | solution.py:72
  34.9 4.2 %all-to-all-start.1 = ((bf16[4,4,192,128]{3,2,1,0:T(8,128)(2,1)}), bf16[4,4,192,128]{3,2,1,0:T(8,128)(2,1)S(1)}, u32[]{:S(2)}, u32[]{:S(2)}) async-start(bf16[4,4,192,128]{3,2,1,0:T(8,128)(2,1)} %shard_map.80), calls=%async_computation.1 | async-start | bytes 1572864 | tf_op jit(solution)/shard_map/all_to_all | solution.py:25
  39.2 0.0 collective-permute-done.3.lifts
  39.2 3.4 %collective-permute-start.4 = (bf16[2,128,1024]{2,1,0:T(8,128)(2,1)}, bf16[2,128,1024]{2,1,0:T(8,128)(2,1)}, u32[]{:S(2)}, u32[]{:S(2)}) collective-permute-start(bf16[2,128,1024]{2,1,0:T(8,128)(2,1)} %collective-permute-done.3.lifts), channel_id=1, source_target_pairs={{0,1},{1,0},{2,3},{3,2},{4,5},{5,4},{6,7},{7,6},{8,9},{9,8},{10,11... | collective-permute-start | bytes 1572872 | tf_op jit(solution)/shard_map/ppermute | solution.py:30
  42.6 0.0 collective-permute-done.2.bundle.second
  42.6 4.2 %shard_map.81 = (bf16[2,256,1024]{2,1,0:T(8,128)(2,1)S(1)}, f32[192,256]{1,0:T(8,128)S(1)}, f32[3,192,256]{2,1,0:T(8,128)}, bf16[192,1024]{1,0:T(8,128)(2,1)}) custom-call(bf16[8,3,192,128]{3,2,1,0:T(8,128)(2,1)S(1)} %all-to-all-done.odd, bf16[2,2,128,1024]{3,2,1,0:T(8,128)(2,1)} %one.5, bf16[2,3,128,1024]{3,2,1,0:T(8,128)(2,1)} %solve.3, ...), custom_call_target="tpu_custom_call" | custom-call | flops 503316480 | bytes 5000000 | tf_op jit(solution)/shard_map/pallas_call | solution.py:72
  46.9 2.3 %all-to-all-done.1.gathered = bf16[4,4,192,128]{3,2,1,0:T(8,128)(2,1)S(1)} async-done(((bf16[4,4,192,128]{3,2,1,0:T(8,128)(2,1)}), bf16[4,4,192,128]{3,2,1,0:T(8,128)(2,1)S(1)}, u32[]{:S(2)}, u32[]{:S(2)}) %all-to-all-start.1) | async-done | bytes 786464 | tf_op jit(solution)/shard_map/all_to_all | solution.py:25
  49.1 1.3 %shard_map.82 = bf16[4,2,192,128]{3,2,1,0:T(8,128)(2,1)} custom-call(bf16[4,4,192,128]{3,2,1,0:T(8,128)(2,1)S(1)} %all-to-all-done.1.gathered, bf16[2,256,1024]{2,1,0:T(8,128)(2,1)S(1)} %get-tuple-element.25.inverses, f32[192,256]{1,0:T(8,128)S(1)} %get-tuple-element.26.coarse), custom_call_target="tpu_custom_call" | custom-call | flops 201326592 | bytes 2000000 | tf_op jit(solution)/shard_map/pallas_call | solution.py:72
  50.4 4.6 %all-to-all-start.2 = ((bf16[4,2,192,128]{3,2,1,0:T(8,128)(2,1)}), bf16[4,2,192,128]{3,2,1,0:T(8,128)(2,1)S(1)}, u32[]{:S(2)}, u32[]{:S(2)}) async-start(bf16[4,2,192,128]{3,2,1,0:T(8,128)(2,1)} %shard_map.82), calls=%async_computation.2 | async-start | bytes 786432 | tf_op jit(solution)/shard_map/all_to_all | solution.py:25
  55.0 0.0 collective-permute-done.4.lifts_partner
  55.1 1.9 %shard_map.84 = bf16[2,192,128]{2,1,0:T(8,128)(2,1)S(1)} custom-call(bf16[4,4,192,128]{3,2,1,0:T(8,128)(2,1)S(1)} %all-to-all-done.1.gathered, bf16[192,1024]{1,0:T(8,128)(2,1)} %get-tuple-element.31.fourth, bf16[2,128,1024]{2,1,0:T(8,128)(2,1)} %collective-permute-done.3.lifts, bf16[2,128,1024]{2,1,0:T(8,128)(2,1)} %collective-permute-done.4.lifts_partner), custom_call_target="tpu_custom_call" | custom-call | flops 100663296 | bytes 1000000 | tf_op jit(solution)/shard_map/pallas_call | solution.py:72
  56.9 3.1 %collective-permute-start.5 = (bf16[2,192,128]{2,1,0:T(8,128)(2,1)S(1)}, bf16[2,192,128]{2,1,0:T(8,128)(2,1)S(1)}, u32[]{:S(2)}, u32[]{:S(2)}) collective-permute-start(bf16[2,192,128]{2,1,0:T(8,128)(2,1)S(1)} %shard_map.84), channel_id=1, source_target_pairs={{0,8},{8,16},{16,24},{24,32},{32,40},{40,48},{48,56},{56,64},{64,7... | collective-permute-start | bytes 294920 | tf_op jit(solution)/shard_map/ppermute | solution.py:36
  60.1 2.3 %shard_map.83 = (f32[2,192,128]{2,1,0:T(8,128)S(1)}, bf16[2,256,1024]{2,1,0:T(8,128)(2,1)S(1)}, f32[2,192,256]{2,1,0:T(8,128)S(1)}, bf16[2,192,128]{2,1,0:T(8,128)(2,1)S(1)}) custom-call(bf16[4,4,192,128]{3,2,1,0:T(8,128)(2,1)S(1)} %all-to-all-done.1.gathered, f32[3,192,256]{2,1,0:T(8,128)} %get-tuple-element.27.early, bf16[1,2,128,1024]{3,2,1,0:T(8,128)(2,1)} %two.3, ...), custom_call_target="tpu_custom_call" | custom-call | flops 301989888 | bytes 3000000 | tf_op jit(solution)/shard_map/pallas_call | solution.py:72
  62.4 3.9 %collective-permute-done.5.before = bf16[2,192,128]{2,1,0:T(8,128)(2,1)S(1)} collective-permute-done((bf16[2,192,128]{2,1,0:T(8,128)(2,1)S(1)}, bf16[2,192,128]{2,1,0:T(8,128)(2,1)S(1)}, u32[]{:S(2)}, u32[]{:S(2)}) %collective-permute-start.5) | collective-permute-done | bytes 98336 | tf_op jit(solution)/shard_map/ppermute | solution.py:36
  66.4 0.0 all-to-all-done.2.centre
  66.4 0.5 shard_map.85
  66.9 5.0 %all-gather = bf16[8,192,128]{2,1,0:T(8,128)(2,1)S(1)} all-gather(bf16[4,192,128]{2,1,0:T(8,128)(2,1)S(1)} %get-tuple-element.33), channel_id=2, replica_groups={{0,1},{2,3},{4,5},{6,7},{8,9},{10,11},{12,13},{14,15},{16,17},{18,19},{..., dimensions={0}, use_global_device_ids=true | all-gather | bytes 589824 | tf_op jit(solution)/shard_map/all_gather | solution.py:432
  71.9 0.8 %shard_map.86 = (bf16[4,2,192,128]{3,2,1,0:T(8,128)(2,1)}, bf16[1,2,192,128]{3,2,1,0:T(8,128)(2,1)}) custom-call(bf16[2,4,192,128]{3,2,1,0:T(8,128)(2,1)S(1)} %bitcast.5, bf16[2,192,128]{2,1,0:T(8,128)(2,1)S(1)} %get-tuple-element.34.coarse, bf16[4,192,128]{2,1,0:T(8,128)(2,1)S(1)} %get-tuple-element.35.kept), custom_call_target="tpu_custom_call" | custom-call | flops 100663296 | bytes 1000000 | tf_op jit(solution)/shard_map/pallas_call | solution.py:72
Async XLA Ops:
  4.4 38.3 %collective-permute-start.2 = (bf16[11,128,1024]{2,1,0:T(8,128)(2,1)}, bf16[11,128,1024]{2,1,0:T(8,128)(2,1)}, u32[]{:S(2)}, u32[]{:S(2)}) collective-permute-start(bf16[11,128,1024]{2,1,0:T(8,128)(2,1)} %get-tuple-element.24), channel_id=1, source_target_pairs={{0,1},{1,0},{2,3},{3,2},{4,5},{5,4},{6,7},{7,6},{8,9},{9,8},{10,11... | collective-permute-start | bytes 8650760 | tf_op jit(solution)/shard_map/ppermute | solution.py:30
  9.0 4.7 %copy-start = (bf16[3,128,1024]{2,1,0:T(8,128)(2,1)S(1)}, bf16[3,128,1024]{2,1,0:T(8,128)(2,1)}, u32[]{:S(2)}) copy-start(bf16[3,128,1024]{2,1,0:T(8,128)(2,1)} %get-tuple-element.20) | copy-start | bytes 2359300
  9.0 7.0 %copy-start.1 = (bf16[2,128,1024]{2,1,0:T(8,128)(2,1)S(1)}, bf16[2,128,1024]{2,1,0:T(8,128)(2,1)}, u32[]{:S(2)}) copy-start(bf16[2,128,1024]{2,1,0:T(8,128)(2,1)} %get-tuple-element.32) | copy-start | bytes 1572868
  9.0 24.5 %all-to-all-start = ((bf16[8,3,192,128]{3,2,1,0:T(8,128)(2,1)}), bf16[8,3,192,128]{3,2,1,0:T(8,128)(2,1)S(1)}, u32[]{:S(2)}, u32[]{:S(2)}) async-start(bf16[8,3,192,128]{3,2,1,0:T(8,128)(2,1)} %shard_map.77), calls=%async_computation | async-start | bytes 2359296 | tf_op jit(solution)/shard_map/all_to_all | solution.py:350
  13.7 6.5 %collective-permute-start = (bf16[3,128,1024]{2,1,0:T(8,128)(2,1)S(1)}, bf16[3,128,1024]{2,1,0:T(8,128)(2,1)S(1)}, u32[]{:S(2)}, u32[]{:S(2)}) collective-permute-start(bf16[3,128,1024]{2,1,0:T(8,128)(2,1)S(1)} %copy-done), channel_id=1, source_target_pairs={{0,1},{1,0},{2,3},{3,2},{4,5},{5,4},{6,7},{7,6},{8,9},{9,8},{10,11... | collective-permute-start | bytes 2359304 | tf_op jit(solution)/shard_map/ppermute | solution.py:30
  16.0 23.2 %collective-permute-start.3 = (bf16[2,128,1024]{2,1,0:T(8,128)(2,1)S(1)}, bf16[2,128,1024]{2,1,0:T(8,128)(2,1)}, u32[]{:S(2)}, u32[]{:S(2)}) collective-permute-start(bf16[2,128,1024]{2,1,0:T(8,128)(2,1)S(1)} %copy-done.1), channel_id=1, source_target_pairs={{8,0},{16,8},{24,16},{32,24},{40,32},{48,40},{56,48},{64,56},{72,6... | collective-permute-start | bytes 1572872 | tf_op jit(solution)/shard_map/ppermute | solution.py:36
  21.5 12.0 %collective-permute-start.1 = (bf16[2,192,128]{2,1,0:T(8,128)(2,1)S(1)}, bf16[2,192,128]{2,1,0:T(8,128)(2,1)S(1)}, u32[]{:S(2)}, u32[]{:S(2)}) collective-permute-start(bf16[2,192,128]{2,1,0:T(8,128)(2,1)S(1)} %get-tuple-element.23), channel_id=1, source_target_pairs={{8,0},{16,8},{24,16},{32,24},{40,32},{48,40},{56,48},{64,56},{72,6... | collective-permute-start | bytes 294920 | tf_op jit(solution)/shard_map/ppermute | solution.py:36
  34.9 14.2 %all-to-all-start.1 = ((bf16[4,4,192,128]{3,2,1,0:T(8,128)(2,1)}), bf16[4,4,192,128]{3,2,1,0:T(8,128)(2,1)S(1)}, u32[]{:S(2)}, u32[]{:S(2)}) async-start(bf16[4,4,192,128]{3,2,1,0:T(8,128)(2,1)} %shard_map.80), calls=%async_computation.1 | async-start | bytes 1572864 | tf_op jit(solution)/shard_map/all_to_all | solution.py:25
  39.2 15.9 %collective-permute-start.4 = (bf16[2,128,1024]{2,1,0:T(8,128)(2,1)}, bf16[2,128,1024]{2,1,0:T(8,128)(2,1)}, u32[]{:S(2)}, u32[]{:S(2)}) collective-permute-start(bf16[2,128,1024]{2,1,0:T(8,128)(2,1)} %collective-permute-done.3.lifts), channel_id=1, source_target_pairs={{0,1},{1,0},{2,3},{3,2},{4,5},{5,4},{6,7},{7,6},{8,9},{9,8},{10,11... | collective-permute-start | bytes 1572872 | tf_op jit(solution)/shard_map/ppermute | solution.py:30
  50.4 15.9 %all-to-all-start.2 = ((bf16[4,2,192,128]{3,2,1,0:T(8,128)(2,1)}), bf16[4,2,192,128]{3,2,1,0:T(8,128)(2,1)S(1)}, u32[]{:S(2)}, u32[]{:S(2)}) async-start(bf16[4,2,192,128]{3,2,1,0:T(8,128)(2,1)} %shard_map.82), calls=%async_computation.2 | async-start | bytes 786432 | tf_op jit(solution)/shard_map/all_to_all | solution.py:25
  56.9 9.4 %collective-permute-start.5 = (bf16[2,192,128]{2,1,0:T(8,128)(2,1)S(1)}, bf16[2,192,128]{2,1,0:T(8,128)(2,1)S(1)}, u32[]{:S(2)}, u32[]{:S(2)}) collective-permute-start(bf16[2,192,128]{2,1,0:T(8,128)(2,1)S(1)} %shard_map.84), channel_id=1, source_target_pairs={{0,8},{8,16},{16,24},{24,32},{32,40},{40,48},{48,56},{56,64},{64,7... | collective-permute-start | bytes 294920 | tf_op jit(solution)/shard_map/ppermute | solution.py:36
